TPU v7x, 32 devices: a whole 2x2x4 slice. The times are simulated.
32 devices in a mesh: dp: 4 (over y, x), expert: 8 (over z, core).
Axes of the slice: x: 2, y: 2, z: 4, core: 2. Of those that a mesh axis runs over, the one named last changes fastest.
Arguments:
- tokens: bfloat16 [1024, 3584], P('expert', 'dp'), may hold values from -6 to 6
- expert_ids: int32 [1024, 8], P('expert'), may hold values from 0 to 7, as said below
- replica_choice: int32 [1024, 8], P('expert'), may hold values from 0 to 1, as said below
- gate_weights: float32 [1024, 8], P('expert'), may hold values from 0.1 to 1
- placement: int32 [4, 2], replicated, may hold values from 0 to 7, as said below
- capacity: int32 [12], replicated, may hold values from 16 to 32, as said below
- w_gate: bfloat16 [8, 2, 3584, 1024], P('expert', None, 'dp'), as said below
- w_up: bfloat16 [8, 2, 3584, 1024], P('expert', None, 'dp'), as said below
- w_down: bfloat16 [8, 2, 1024, 3584], P('expert', None, None, 'dp'), as said below
Outputs:
- combined: bfloat16 [1024, 3584], P('expert', 'dp')
Inputs may be any that keep to these rules, and one draw needn't show every extreme that they name: `expert_ids`: each row names 8 different experts; in every aligned block of 128 rows some hot expert is named by at least 64 rows. `replica_choice`: 1 only where the slot's expert is hot; in every aligned block of 128 rows both replicas of some hot expert whose replicas have capacity 32 receive 32 or more slots. `placement`: column 0 holds 4 different expert numbers; column 1 holds 4 different expert-axis indices, none of them the own index of a hot expert. Entry e below 8 belongs to expert e's own replica, entry 8 + j to the copy of expert placement[j, 0]; both replicas of some hot expert have capacity 32. w_gate[placement[j, 1], 1] equals w_gate[placement[j, 0], 0]; entry [h, 1] is zero where index h hosts no copy. `w_up`: laid out as w_gate. `w_down`: laid out as w_gate.
All inputs are finite; a program needn't handle non-finite values.
Results may differ from a plain program's by a relative error of at most 0.0057.
Values may be sent and summed in bfloat16 or wider, within the bound.
No kernel may reach another device: no remote copies, remote signals or barrier semaphores. Data moves between devices by JAX's collectives and lax.ppermute only.
A program may use at most 128 MiB of HBM per device.

v0:
```python
import functools

import jax
import jax.numpy as jnp
from jax import lax
from jax.experimental import pallas as pl
from jax.experimental.pallas import tpu as pltpu
from jax.sharding import PartitionSpec as P


BF16 = jnp.bfloat16
F32 = jnp.float32
I32 = jnp.int32
DIRECT_LIMIT = 8


def round_up(n, m):
    return -(-n // m) * m


def slot_room(token_count, top_count, expert_count):
    return max(2, min(token_count // 4, 3 * token_count * top_count // (4 * expert_count)))


def dot(a, b):
    return jnp.dot(a, b, preferred_element_type=F32)


def vmem_specs(n):
    return [pl.BlockSpec(memory_space=pltpu.VMEM)] * n


PARAMS = pltpu.CompilerParams(vmem_limit_bytes=24 * 2**20)


def in_hbm(x):
    return pltpu.with_memory_space_constraint(x, pltpu.HBM)


def cost(flops, size):
    return pl.CostEstimate(flops=flops, bytes_accessed=size, transcendentals=0)


SMEM_SPEC = pl.BlockSpec(memory_space=pltpu.SMEM)


def route_kernel(
    sizes, chunks, place_in, cap_in, ids_in, choice_in, gate_in, tok_in, second, *refs
):
    experts, hot, _, half, room_a, room_b, direct = sizes
    n = len(chunks)
    mats, pieces = refs[: 2 * n], refs[2 * n : 2 * n + experts]
    place, cap, ids_ref, choice_ref, gate_ref, tok_ref, sems = refs[2 * n + experts :]
    copies = [
        pltpu.make_async_copy(src, dst, sems.at[i])
        for i, (src, dst) in enumerate(
            (
                (ids_in, ids_ref),
                (choice_in, choice_ref),
                (gate_in, gate_ref),
                (place_in, place),
                (cap_in, cap),
                (tok_in, tok_ref),
            )
        )
    ]
    for copy in copies:
        copy.start()
    top, count = ids_ref.shape
    per = room_a + room_b
    me = lax.axis_index("expert")
    earlier = lax.broadcasted_iota(I32, (count, count), 1) < lax.broadcasted_iota(
        I32, (count, count), 0
    )
    lane = lax.broadcasted_iota(I32, (count, 2 * experts), 1).astype(F32)
    lane_row = lax.broadcasted_iota(I32, (1, 2 * experts), 1)
    for copy in copies[:5]:
        copy.wait()
    hosting = jnp.int32(0)
    for j in range(hot):
        hosting = jnp.where(place[1, j] == me, 1, hosting)
    second[0] = lax.axis_index("dp")
    second[1] = hosting
    key = (ids_ref[...] + experts * choice_ref[...]).astype(F32).T
    gate = gate_ref[...].T
    member = jnp.zeros((count, 2 * experts), F32)
    weight = jnp.zeros((count, 2 * experts), F32)
    for k in range(top):
        hit = key[:, k : k + 1] == lane
        member = jnp.where(hit, 1.0, member)
        weight = jnp.where(hit, gate[:, k : k + 1], weight)
    rank = dot(jnp.where(earlier, 1.0, 0.0).astype(BF16), member.astype(BF16))
    limit = jnp.zeros((1, 2 * experts), I32)
    for e in range(experts):
        limit = jnp.where(lane_row == e, cap[e], limit)
    for j in range(hot):
        limit = jnp.where(lane_row == place[0, j] + experts, cap[experts + j], limit)
    kept = (member > 0.5) & (rank < limit.astype(F32))
    rank = jnp.where(kept, rank, -1.0).astype(BF16)
    weight_high = weight.astype(BF16)
    weight_low = (weight - weight_high.astype(F32)).astype(BF16)

    done = 0
    for c, chunk in enumerate(chunks):
        columns = len(chunk) * per
        column = lax.broadcasted_iota(I32, (1, columns), 1)
        block = jnp.floor((column.astype(F32) + 0.5) * (1.0 / per)).astype(I32)
        slot = column - block * per
        if direct:
            flip = jnp.zeros((1, columns), I32)
            for i, j in enumerate(chunk):
                flip = jnp.where(block == i, j, flip)
            dest = flip ^ me
        else:
            dest = block + chunk[0]
        pair_key = jnp.full((1, columns), -1, I32)
        start = jnp.zeros((1, columns), I32)
        for j in range(hot):
            owner, host = dest == place[0, j], dest == place[1, j]
            pair_key = jnp.where(owner | host, place[0, j] + experts, pair_key)
            start = jnp.where(host, half, start)
        first = slot < room_a
        in_pair = slot - room_a
        wanted = jnp.where(first, dest, jnp.where(in_pair < half, pair_key, -1))
        place_rank = jnp.where(first, slot, in_pair + start).astype(F32)
        spread = jnp.where(
            lax.broadcasted_iota(I32, (2 * experts, columns), 0) == wanted, 1.0, 0.0
        ).astype(BF16)
        chosen = (dot(rank, spread) == place_rank) & (wanted >= 0)
        mats[2 * c][...] = jnp.where(chosen, dot(weight_high, spread), 0.0).astype(BF16)
        mats[2 * c + 1][...] = jnp.where(chosen, dot(weight_low, spread), 0.0).astype(BF16)
        picks = jnp.where(chosen, 1.0, 0.0).T.astype(BF16)
        if not c:
            copies[5].wait()
        rows = dot(picks, tok_ref[...]).astype(BF16)
        for i in range(len(chunk)):
            pieces[done + i][...] = rows[i * per : (i + 1) * per]
        done += len(chunk)


def stage_kernel(at, w_gate, w_up, *refs):
    outs, sems = refs[:-1], refs[-1]
    block = outs[0].shape[2] // 2
    copies = []
    for k, out in enumerate(outs):
        columns = pl.ds(pl.multiple_of((at[0] ^ k) * block, block), block)
        for i, which in enumerate((0, at[1])):
            for g, w in enumerate((w_gate, w_up)):
                copies.append(
                    pltpu.make_async_copy(
                        w.at[0, which, :, columns],
                        out.at[i, :, pl.ds(g * block, block)],
                        sems.at[len(copies)],
                    )
                )
    for copy in copies:
        copy.start()
    for copy in copies:
        copy.wait()


def up_sums(xa, xb, weights, out):
    rows_a = xa.shape[0]
    out[:rows_a] = dot(xa, weights[0]).astype(out.dtype)
    out[rows_a:] = dot(xb, weights[1]).astype(out.dtype)


def up_first_kernel(sizes, *refs):
    blocks, room_a, room_b = sizes
    x_refs, weights = refs[:blocks], refs[blocks]
    out, xa, xb = refs[blocks + 1 :]
    for i, ref in enumerate(x_refs):
        xa[i * room_a : (i + 1) * room_a] = ref[:room_a]
        xb[i * room_b : (i + 1) * room_b] = ref[room_a:]
    up_sums(xa[...], xb[...], weights, out)


def up_next_kernel(xa, xb, weights, out):
    up_sums(xa[...], xb[...], weights, out)


def hidden_kernel(own, *refs):
    out = refs[-1]
    block = own.shape[1] // 2
    total = own[...]
    for ref in refs[:-1]:
        total += ref[...].astype(F32)
    out[...] = (jax.nn.silu(total[:, :block]) * total[:, block:]).astype(BF16)


def down_kernel(sizes, at, w, *refs):
    parts, blocks, room_a, room_b = sizes
    hids, outs = refs[:parts], refs[parts:]
    rows_a, depth = blocks * room_a, hids[0].shape[1]
    ra = rb = 0.0
    for k, h in enumerate(hids):
        units = pl.ds(pl.multiple_of((at[0] ^ k) * depth, depth), depth)
        ra += dot(h[:rows_a], w[0, 0, units])
        rb += dot(h[rows_a:], w[0, at[1], units])
    ra, rb = ra.astype(BF16), rb.astype(BF16)
    for i, out in enumerate(outs):
        out[:room_a] = ra[i * room_a : (i + 1) * room_a]
        out[room_a:] = rb[i * room_b : (i + 1) * room_b]


def combine_kernel(has_base, *refs):
    base, (high, low) = refs[:has_base], refs[has_base : has_base + 2]
    pieces, out, res = refs[has_base + 2 : -2], refs[-2], refs[-1]
    per = pieces[0].shape[0]
    for i, ref in enumerate(pieces):
        res[i * per : (i + 1) * per] = ref[...]
    rows = res[...]
    total = dot(high[...], rows) + dot(low[...], rows)
    for ref in base:
        total += ref[...]
    out[...] = total.astype(out.dtype)


def flips(n, j):
    return [(i, i ^ j) for i in range(n)]


def exchange(pieces, chunks, axis):
    n = len(pieces)
    if n > DIRECT_LIMIT:
        moved = lax.all_to_all(jnp.stack(pieces), axis, split_axis=0, concat_axis=0, tiled=True)
        return [moved[i] for i in range(n)]
    moved = []
    for j, piece in zip([j for chunk in chunks for j in chunk], pieces):
        moved.append(lax.ppermute(piece, axis, flips(n, j)) if j else piece)
    return moved


def chunks_of(experts):
    if experts == 8:
        return ((4, 5, 1, 0), (2, 3, 6, 7))
    return (tuple(range(experts)),)


def on_device(
    tokens, expert_ids, replica_choice, gate_weights, placement, capacity, w_gate, w_up, w_down
):
    experts = lax.axis_size("expert")
    parts = lax.axis_size("dp")
    count, cols = tokens.shape
    ff = w_gate.shape[3]
    hot = placement.shape[0]
    room = slot_room(count, expert_ids.shape[1], experts)
    half = -(-room // 2)
    room_a, room_b = round_up(room, 16), round_up(half, 16)
    per = room_a + room_b
    chunks = chunks_of(experts)
    sds = jax.ShapeDtypeStruct
    hbm = pl.BlockSpec(memory_space=pltpu.HBM)
    top = expert_ids.shape[1]
    mat_shapes = [sds((count, len(c) * per), BF16) for c in chunks for _ in range(2)]
    scalars, *made = pl.pallas_call(
        functools.partial(
            route_kernel,
            (experts, hot, room, half, room_a, room_b, experts <= DIRECT_LIMIT),
            chunks,
        ),
        out_shape=[sds((2,), I32)] + mat_shapes + [sds((per, cols), BF16)] * experts,
        in_specs=[hbm] * 6,
        out_specs=[SMEM_SPEC] + vmem_specs(len(mat_shapes) + experts),
        scratch_shapes=[
            pltpu.SMEM((2, hot), I32),
            pltpu.SMEM(capacity.shape, I32),
            pltpu.VMEM((top, count), I32),
            pltpu.VMEM((top, count), I32),
            pltpu.VMEM((top, count), F32),
            pltpu.VMEM((count, cols), BF16),
            pltpu.SemaphoreType.DMA((6,)),
        ],
        compiler_params=PARAMS,
        name="route",
    )(
        *map(
            in_hbm,
            (placement.T, capacity, expert_ids.T, replica_choice.T, gate_weights.T, tokens),
        )
    )
    mats, pieces = made[: len(mat_shapes)], made[len(mat_shapes) :]
    arrived = exchange(pieces, chunks, "expert")

    block = ff // parts
    order = list(range(parts - 1, 0, -1)) + [0]
    staged = pl.pallas_call(
        stage_kernel,
        out_shape=[sds((2, cols, 2 * block), BF16)] * parts,
        in_specs=[SMEM_SPEC] + [hbm] * 2,
        out_specs=vmem_specs(parts),
        scratch_shapes=[pltpu.SemaphoreType.DMA((4 * parts,))],
        compiler_params=PARAMS,
        cost_estimate=cost(0, 16 * cols * ff),
        name="stage",
    )(scalars, in_hbm(w_gate), in_hbm(w_up))

    results, done = [], 0
    for chunk in chunks:
        blocks = len(chunk)
        rows_a, rows = blocks * room_a, blocks * per
        step = 2 * rows * cols * block
        sums = {}
        for i, k in enumerate(order):
            piece = sds((rows, 2 * block), BF16 if k else F32)
            halves = [sds((rows_a, cols), BF16), sds((rows - rows_a, cols), BF16)]
            made = pl.pallas_call(
                up_next_kernel
                if i
                else functools.partial(up_first_kernel, (blocks, room_a, room_b)),
                out_shape=[piece] + ([] if i else halves),
                in_specs=vmem_specs(3 if i else blocks + 1),
                out_specs=vmem_specs(1 if i else 3),
                compiler_params=PARAMS,
                cost_estimate=cost(2 * step, rows * (cols + 2 * block) * 2),
                name="up",
            )(*([xa, xb] if i else arrived[done : done + blocks]), staged[k])
            sums[k] = made[0]
            if not i:
                xa, xb = made[1:]
            if k:
                sums[k] = lax.ppermute(sums[k], "dp", flips(parts, k))
        hidden = pl.pallas_call(
            hidden_kernel,
            out_shape=sds((rows, block), BF16),
            in_specs=vmem_specs(parts),
            out_specs=vmem_specs(1)[0],
            compiler_params=PARAMS,
            name="hidden",
        )(*[sums[k] for k in range(parts)])
        spread = {0: hidden}
        for k in order[:-1]:
            spread[k] = lax.ppermute(hidden, "dp", flips(parts, k))
        results += pl.pallas_call(
            functools.partial(down_kernel, (parts, blocks, room_a, room_b)),
            out_shape=[sds((per, cols), BF16)] * blocks,
            in_specs=[SMEM_SPEC] + vmem_specs(1 + parts),
            out_specs=vmem_specs(blocks),
            compiler_params=PARAMS,
            cost_estimate=cost(parts * step, 4 * cols * ff),
            name="down",
        )(scalars, w_down, *[spread[k] for k in range(parts)])
        done += blocks
    returned = exchange(results, chunks, "expert")
    total, done = [], 0
    for c, chunk in enumerate(chunks):
        last = c + 1 == len(chunks)
        total = [
            pl.pallas_call(
                functools.partial(combine_kernel, len(total)),
                out_shape=sds((count, cols), BF16 if last else F32),
                in_specs=vmem_specs(len(total) + 2 + len(chunk)),
                out_specs=vmem_specs(1)[0],
                scratch_shapes=[pltpu.VMEM((len(chunk) * per, cols), BF16)],
                compiler_params=PARAMS,
                name="combine",
            )(*total, *mats[2 * c : 2 * c + 2], *returned[done : done + len(chunk)])
        ]
        done += len(chunk)
    return total[0]


def solution(mesh):
    return jax.shard_map(
        on_device,
        mesh=mesh,
        in_specs=(
            P("expert", "dp"),
            P("expert", None),
            P("expert", None),
            P("expert", None),
            P(),
            P(),
            P("expert", None, "dp", None),
            P("expert", None, "dp", None),
            P("expert", None, None, "dp"),
        ),
        out_specs=P("expert", "dp"),
        check_vma=False,
    )
```

profile of v0, /device:TPU:0, one launch (start us, length us, event | category | flops | bytes accessed | tf_op | source)
XLA Modules:
  0.0 65.9 jit_solution(16637538805748131084)
XLA Ops:
  0.0 2.5 %route.1 = (s32[2]{0:T(128)S(1)}, bf16[128,192]{1,0:T(8,128)(2,1)S(1)}, bf16[128,192]{1,0:T(8,128)(2,1)S(1)}, bf16[128,192]{1,0:T(8,128)(2,1)S(1)}, bf16[128,192...) custom-call(s32[2,4]{1,0:T(2,128)} %bitcast.7, ...), custom_call_target="tpu_custom_call" | custom-call | tf_op jit(solution)/shard_map/route/pallas_call | solution.py:257
  2.5 4.1 %collective-permute-start = (bf16[48,896]{1,0:T(8,128)(2,1)S(1)}, bf16[48,896]{1,0:T(8,128)(2,1)S(1)}, u32[]{:S(2)}, u32[]{:S(2)}) collective-permute-start(bf16[48,896]{1,0:T(8,128)(2,1)S(1)} %get-tuple-element.39), channel_id=1, source_target_pairs={{0,4},{1,5},{2,6},{3,7},{4,0},{5,1},{6,2},{7,3},{8,12},{9,13},{10,... | collective-permute-start | bytes 258056 | tf_op jit(solution)/shard_map/ppermute | solution.py:230
  6.9 1.8 %collective-permute-start.12 = (bf16[48,896]{1,0:T(8,128)(2,1)S(1)}, bf16[48,896]{1,0:T(8,128)(2,1)S(1)}, u32[]{:S(2)}, u32[]{:S(2)}) collective-permute-start(bf16[48,896]{1,0:T(8,128)(2,1)S(1)} %get-tuple-element.56), channel_id=1, source_target_pairs={{0,2},{1,3},{2,0},{3,1},{4,6},{5,7},{6,4},{7,5},{8,10},{9,11},{10,... | collective-permute-start | bytes 258056 | tf_op jit(solution)/shard_map/ppermute | solution.py:230
  8.7 3.9 %stage.1 = (bf16[2,896,512]{2,1,0:T(8,128)(2,1)S(1)}, bf16[2,896,512]{2,1,0:T(8,128)(2,1)S(1)}, bf16[2,896,512]{2,1,0:T(8,128)(2,1)S(1)}, bf16[2,896,512]{2,1,0:T(8,128)(2,1)S(1)}) custom-call(s32[2]{0:T(128)S(1)} %get-tuple-element.38.at, bf16[1,2,896,1024]{3,2,1,0:T(8,128)(2,1)} %w_gate.1, bf16[1,2,896,1024]{3,2,1,0:T(8,128)(2,1)} %w_up.1), custom_call_target="tpu_custom_call" | custom-call | bytes 14680064 | tf_op jit(solution)/shard_map/stage/pallas_call | solution.py:288
  12.6 0.7 %collective-permute-done.refs_0_ = bf16[48,896]{1,0:T(8,128)(2,1)S(1)} collective-permute-done((bf16[48,896]{1,0:T(8,128)(2,1)S(1)}, bf16[48,896]{1,0:T(8,128)(2,1)S(1)}, u32[]{:S(2)}, u32[]{:S(2)}) %collective-permute-start) | collective-permute-done | bytes 86048 | tf_op jit(solution)/shard_map/ppermute | solution.py:230
  13.3 3.3 %collective-permute-start.14 = (bf16[48,896]{1,0:T(8,128)(2,1)S(1)}, bf16[48,896]{1,0:T(8,128)(2,1)S(1)}, u32[]{:S(2)}, u32[]{:S(2)}) collective-permute-start(bf16[48,896]{1,0:T(8,128)(2,1)S(1)} %get-tuple-element.58), channel_id=1, source_target_pairs={{0,6},{1,7},{2,4},{3,5},{4,2},{5,3},{6,0},{7,1},{8,14},{9,15},{10,... | collective-permute-start | bytes 258056 | tf_op jit(solution)/shard_map/ppermute | solution.py:230
  16.6 1.3 %collective-permute-start.15 = (bf16[48,896]{1,0:T(8,128)(2,1)S(1)}, bf16[48,896]{1,0:T(8,128)(2,1)S(1)}, u32[]{:S(2)}, u32[]{:S(2)}) collective-permute-start(bf16[48,896]{1,0:T(8,128)(2,1)S(1)} %get-tuple-element.59), channel_id=1, source_target_pairs={{0,7},{1,6},{2,5},{3,4},{4,3},{5,2},{6,1},{7,0},{8,15},{9,14},{10,... | collective-permute-start | bytes 258056 | tf_op jit(solution)/shard_map/ppermute | solution.py:230
  18.8 1.6 %collective-permute-start.3 = (bf16[192,512]{1,0:T(8,128)(2,1)S(1)}, bf16[192,512]{1,0:T(8,128)(2,1)S(1)}, u32[]{:S(2)}, u32[]{:S(2)}) collective-permute-start(bf16[192,512]{1,0:T(8,128)(2,1)S(1)} %up.10), channel_id=1, source_target_pairs={{0,8},{8,0},{16,24},{24,16},{1,9},{9,1},{17,25},{25,17},{2,10},{10... | collective-permute-start | bytes 589832 | tf_op jit(solution)/shard_map/ppermute | solution.py:323
  20.8 1.6 %collective-permute-start.4 = (bf16[192,512]{1,0:T(8,128)(2,1)S(1)}, bf16[192,512]{1,0:T(8,128)(2,1)S(1)}, u32[]{:S(2)}, u32[]{:S(2)}) collective-permute-start(bf16[192,512]{1,0:T(8,128)(2,1)S(1)} %up.11), channel_id=1, source_target_pairs={{0,16},{8,24},{16,0},{24,8},{1,17},{9,25},{17,1},{25,9},{2,18},{10... | collective-permute-start | bytes 589832 | tf_op jit(solution)/shard_map/ppermute | solution.py:323
  22.4 0.5 collective-permute-start.5
  24.1 1.6 %collective-permute-start.16 = (bf16[192,512]{1,0:T(8,128)(2,1)S(1)}, bf16[192,512]{1,0:T(8,128)(2,1)S(1)}, u32[]{:S(2)}, u32[]{:S(2)}) collective-permute-start(bf16[192,512]{1,0:T(8,128)(2,1)S(1)} %up.14), channel_id=1, source_target_pairs={{0,8},{8,0},{16,24},{24,16},{1,9},{9,1},{17,25},{25,17},{2,10},{10... | collective-permute-start | bytes 589832 | tf_op jit(solution)/shard_map/ppermute | solution.py:323
  26.1 1.6 %collective-permute-start.17 = (bf16[192,512]{1,0:T(8,128)(2,1)S(1)}, bf16[192,512]{1,0:T(8,128)(2,1)S(1)}, u32[]{:S(2)}, u32[]{:S(2)}) collective-permute-start(bf16[192,512]{1,0:T(8,128)(2,1)S(1)} %up.15), channel_id=1, source_target_pairs={{0,16},{8,24},{16,0},{24,8},{1,17},{9,25},{17,1},{25,9},{2,18},{10... | collective-permute-start | bytes 589832 | tf_op jit(solution)/shard_map/ppermute | solution.py:323
  27.7 1.4 %collective-permute-start.18 = (bf16[192,512]{1,0:T(8,128)(2,1)S(1)}, bf16[192,512]{1,0:T(8,128)(2,1)S(1)}, u32[]{:S(2)}, u32[]{:S(2)}) collective-permute-start(bf16[192,512]{1,0:T(8,128)(2,1)S(1)} %get-tuple-element.62), channel_id=1, source_target_pairs={{0,24},{8,16},{16,8},{24,0},{1,25},{9,17},{17,9},{25,1},{2,26},{10... | collective-permute-start | bytes 589832 | tf_op jit(solution)/shard_map/ppermute | solution.py:323
  29.5 3.2 %collective-permute-done.4.refs_1_ = bf16[192,512]{1,0:T(8,128)(2,1)S(1)} collective-permute-done((bf16[192,512]{1,0:T(8,128)(2,1)S(1)}, bf16[192,512]{1,0:T(8,128)(2,1)S(1)}, u32[]{:S(2)}, u32[]{:S(2)}) %collective-permute-start.4) | collective-permute-done | bytes 196640 | tf_op jit(solution)/shard_map/ppermute | solution.py:323
  32.9 1.6 %collective-permute-start.8 = (bf16[192,256]{1,0:T(8,128)(2,1)S(1)}, bf16[192,256]{1,0:T(8,128)(2,1)S(1)}, u32[]{:S(2)}, u32[]{:S(2)}) collective-permute-start(bf16[192,256]{1,0:T(8,128)(2,1)S(1)} %hidden.2.refs_0_), channel_id=1, source_target_pairs={{0,24},{8,16},{16,8},{24,0},{1,25},{9,17},{17,9},{25,1},{2,26},{10... | collective-permute-start | bytes 294920 | tf_op jit(solution)/shard_map/ppermute | solution.py:334
  34.5 0.5 collective-permute-start.7
  35.1 1.5 %collective-permute-start.6 = (bf16[192,256]{1,0:T(8,128)(2,1)S(1)}, bf16[192,256]{1,0:T(8,128)(2,1)S(1)}, u32[]{:S(2)}, u32[]{:S(2)}) collective-permute-start(bf16[192,256]{1,0:T(8,128)(2,1)S(1)} %hidden.2.refs_0_), channel_id=1, source_target_pairs={{0,8},{8,0},{16,24},{24,16},{1,9},{9,1},{17,25},{25,17},{2,10},{10... | collective-permute-start | bytes 294920 | tf_op jit(solution)/shard_map/ppermute | solution.py:334
  37.1 6.2 %collective-permute-done.17.refs_1_ = bf16[192,512]{1,0:T(8,128)(2,1)S(1)} collective-permute-done((bf16[192,512]{1,0:T(8,128)(2,1)S(1)}, bf16[192,512]{1,0:T(8,128)(2,1)S(1)}, u32[]{:S(2)}, u32[]{:S(2)}) %collective-permute-start.17) | collective-permute-done | bytes 196640 | tf_op jit(solution)/shard_map/ppermute | solution.py:323
  43.4 1.6 %collective-permute-start.21 = (bf16[192,256]{1,0:T(8,128)(2,1)S(1)}, bf16[192,256]{1,0:T(8,128)(2,1)S(1)}, u32[]{:S(2)}, u32[]{:S(2)}) collective-permute-start(bf16[192,256]{1,0:T(8,128)(2,1)S(1)} %hidden.3.refs_0_), channel_id=1, source_target_pairs={{0,24},{8,16},{16,8},{24,0},{1,25},{9,17},{17,9},{25,1},{2,26},{10... | collective-permute-start | bytes 294920 | tf_op jit(solution)/shard_map/ppermute | solution.py:334
  45.2 1.8 %collective-permute-start.19 = (bf16[192,256]{1,0:T(8,128)(2,1)S(1)}, bf16[192,256]{1,0:T(8,128)(2,1)S(1)}, u32[]{:S(2)}, u32[]{:S(2)}) collective-permute-start(bf16[192,256]{1,0:T(8,128)(2,1)S(1)} %hidden.3.refs_0_), channel_id=1, source_target_pairs={{0,8},{8,0},{16,24},{24,16},{1,9},{9,1},{17,25},{25,17},{2,10},{10... | collective-permute-start | bytes 294920 | tf_op jit(solution)/shard_map/ppermute | solution.py:334
  47.0 1.3 %down.2 = (bf16[48,896]{1,0:T(8,128)(2,1)S(1)}, bf16[48,896]{1,0:T(8,128)(2,1)S(1)}, bf16[48,896]{1,0:T(8,128)(2,1)S(1)}, bf16[48,896]{1,0:T(8,128)(2,1)S(1)}) custom-call(s32[2]{0:T(128)S(1)} %get-tuple-element.38.at, bf16[1,2,1024,896]{3,2,1,0:T(8,128)(2,1)S(1)} %copy-done, bf16[192,256]{1,0:T(8,128)(2,1)S(1)} %hidden.2.refs_0_, ...), custom_call_target="tpu_custom_call" | custom-call | flops 352321536 | bytes 3670016 | tf_op jit(solution)/shard_map/down/pallas_call | solution.py:335
  48.4 0.6 collective-permute-done.21.refs_3_
  49.0 1.0 %collective-permute-done.20.refs_2_ = bf16[192,256]{1,0:T(8,128)(2,1)S(1)} collective-permute-done((bf16[192,256]{1,0:T(8,128)(2,1)S(1)}, bf16[192,256]{1,0:T(8,128)(2,1)S(1)}, u32[]{:S(2)}, u32[]{:S(2)}) %collective-permute-start.20) | collective-permute-done | bytes 98336 | tf_op jit(solution)/shard_map/ppermute | solution.py:334
  50.3 1.3 %down.3 = (bf16[48,896]{1,0:T(8,128)(2,1)S(1)}, bf16[48,896]{1,0:T(8,128)(2,1)S(1)}, bf16[48,896]{1,0:T(8,128)(2,1)S(1)}, bf16[48,896]{1,0:T(8,128)(2,1)S(1)}) custom-call(s32[2]{0:T(128)S(1)} %get-tuple-element.38.at, bf16[1,2,1024,896]{3,2,1,0:T(8,128)(2,1)S(1)} %copy-done, bf16[192,256]{1,0:T(8,128)(2,1)S(1)} %hidden.3.refs_0_, ...), custom_call_target="tpu_custom_call" | custom-call | flops 352321536 | bytes 3670016 | tf_op jit(solution)/shard_map/down/pallas_call | solution.py:335
  51.5 0.9 %collective-permute-start.22 = (bf16[48,896]{1,0:T(8,128)(2,1)S(1)}, bf16[48,896]{1,0:T(8,128)(2,1)S(1)}, u32[]{:S(2)}, u32[]{:S(2)}) collective-permute-start(bf16[48,896]{1,0:T(8,128)(2,1)S(1)} %get-tuple-element.63), channel_id=1, source_target_pairs={{0,2},{1,3},{2,0},{3,1},{4,6},{5,7},{6,4},{7,5},{8,10},{9,11},{10,... | collective-permute-start | bytes 258056 | tf_op jit(solution)/shard_map/ppermute | solution.py:230
  52.8 1.3 %collective-permute-start.23 = (bf16[48,896]{1,0:T(8,128)(2,1)S(1)}, bf16[48,896]{1,0:T(8,128)(2,1)S(1)}, u32[]{:S(2)}, u32[]{:S(2)}) collective-permute-start(bf16[48,896]{1,0:T(8,128)(2,1)S(1)} %get-tuple-element.64), channel_id=1, source_target_pairs={{0,3},{1,2},{2,1},{3,0},{4,7},{5,6},{6,5},{7,4},{8,11},{9,10},{10,... | collective-permute-start | bytes 258056 | tf_op jit(solution)/shard_map/ppermute | solution.py:230
  54.1 2.7 %collective-permute-done.9.refs_2_ = bf16[48,896]{1,0:T(8,128)(2,1)S(1)} collective-permute-done((bf16[48,896]{1,0:T(8,128)(2,1)S(1)}, bf16[48,896]{1,0:T(8,128)(2,1)S(1)}, u32[]{:S(2)}, u32[]{:S(2)}) %collective-permute-start.9) | collective-permute-done | bytes 86048 | tf_op jit(solution)/shard_map/ppermute | solution.py:230
  56.7 1.6 %collective-permute-start.24 = (bf16[48,896]{1,0:T(8,128)(2,1)S(1)}, bf16[48,896]{1,0:T(8,128)(2,1)S(1)}, u32[]{:S(2)}, u32[]{:S(2)}) collective-permute-start(bf16[48,896]{1,0:T(8,128)(2,1)S(1)} %get-tuple-element.65), channel_id=1, source_target_pairs={{0,6},{1,7},{2,4},{3,5},{4,2},{5,3},{6,0},{7,1},{8,14},{9,15},{10,... | collective-permute-start | bytes 258056 | tf_op jit(solution)/shard_map/ppermute | solution.py:230
  59.1 2.9 %collective-permute-done.23.refs_4_ = bf16[48,896]{1,0:T(8,128)(2,1)S(1)} collective-permute-done((bf16[48,896]{1,0:T(8,128)(2,1)S(1)}, bf16[48,896]{1,0:T(8,128)(2,1)S(1)}, u32[]{:S(2)}, u32[]{:S(2)}) %collective-permute-start.23) | collective-permute-done | bytes 86048 | tf_op jit(solution)/shard_map/ppermute | solution.py:230
  62.0 1.1 %collective-permute-done.24.refs_5_ = bf16[48,896]{1,0:T(8,128)(2,1)S(1)} collective-permute-done((bf16[48,896]{1,0:T(8,128)(2,1)S(1)}, bf16[48,896]{1,0:T(8,128)(2,1)S(1)}, u32[]{:S(2)}, u32[]{:S(2)}) %collective-permute-start.24) | collective-permute-done | bytes 86048 | tf_op jit(solution)/shard_map/ppermute | solution.py:230
  63.1 1.8 %collective-permute-done.25.refs_6_ = bf16[48,896]{1,0:T(8,128)(2,1)S(1)} collective-permute-done((bf16[48,896]{1,0:T(8,128)(2,1)S(1)}, bf16[48,896]{1,0:T(8,128)(2,1)S(1)}, u32[]{:S(2)}, u32[]{:S(2)}) %collective-permute-start.25) | collective-permute-done | bytes 86048 | tf_op jit(solution)/shard_map/ppermute | solution.py:230
  65.0 1.0 %combine.3 = bf16[128,896]{1,0:T(8,128)(2,1)} custom-call(f32[128,896]{1,0:T(8,128)S(1)} %combine.2.refs_0_, bf16[128,192]{1,0:T(8,128)(2,1)S(1)} %get-tuple-element.54.refs_1_, bf16[128,192]{1,0:T(8,128)(2,1)S(1)} %get-tuple-element.55.refs_2_, bf16[48,896]{1,0:T(8,128)(2,1)S(1)} %collective-permute-done.22.refs_3_, ...), custom_call_target="tpu_custom_call" | custom-call | tf_op jit(solution)/shard_map/combine/pallas_call | solution.py:350
  (38 shorter events, 6.0 us)
Async XLA Ops:
  2.5 10.7 %collective-permute-start = (bf16[48,896]{1,0:T(8,128)(2,1)S(1)}, bf16[48,896]{1,0:T(8,128)(2,1)S(1)}, u32[]{:S(2)}, u32[]{:S(2)}) collective-permute-start(bf16[48,896]{1,0:T(8,128)(2,1)S(1)} %get-tuple-element.39), channel_id=1, source_target_pairs={{0,4},{1,5},{2,6},{3,7},{4,0},{5,1},{6,2},{7,3},{8,12},{9,13},{10,... | collective-permute-start | bytes 258056 | tf_op jit(solution)/shard_map/ppermute | solution.py:230
  6.7 10.0 %collective-permute-start.1 = (bf16[48,896]{1,0:T(8,128)(2,1)S(1)}, bf16[48,896]{1,0:T(8,128)(2,1)S(1)}, u32[]{:S(2)}, u32[]{:S(2)}) collective-permute-start(bf16[48,896]{1,0:T(8,128)(2,1)S(1)} %get-tuple-element.40), channel_id=1, source_target_pairs={{0,5},{1,4},{2,7},{3,6},{4,1},{5,0},{6,3},{7,2},{8,13},{9,12},{10,... | collective-permute-start | bytes 258056 | tf_op jit(solution)/shard_map/ppermute | solution.py:230
  6.7 11.3 %collective-permute-start.2 = (bf16[48,896]{1,0:T(8,128)(2,1)S(1)}, bf16[48,896]{1,0:T(8,128)(2,1)S(1)}, u32[]{:S(2)}, u32[]{:S(2)}) collective-permute-start(bf16[48,896]{1,0:T(8,128)(2,1)S(1)} %get-tuple-element.41), channel_id=1, source_target_pairs={{0,1},{1,0},{2,3},{3,2},{4,5},{5,4},{6,7},{7,6},{8,9},{9,8},{10,11... | collective-permute-start | bytes 258056 | tf_op jit(solution)/shard_map/ppermute | solution.py:230
  6.9 14.0 %collective-permute-start.12 = (bf16[48,896]{1,0:T(8,128)(2,1)S(1)}, bf16[48,896]{1,0:T(8,128)(2,1)S(1)}, u32[]{:S(2)}, u32[]{:S(2)}) collective-permute-start(bf16[48,896]{1,0:T(8,128)(2,1)S(1)} %get-tuple-element.56), channel_id=1, source_target_pairs={{0,2},{1,3},{2,0},{3,1},{4,6},{5,7},{6,4},{7,5},{8,10},{9,11},{10,... | collective-permute-start | bytes 258056 | tf_op jit(solution)/shard_map/ppermute | solution.py:230
  8.7 13.7 %collective-permute-start.13 = (bf16[48,896]{1,0:T(8,128)(2,1)S(1)}, bf16[48,896]{1,0:T(8,128)(2,1)S(1)}, u32[]{:S(2)}, u32[]{:S(2)}) collective-permute-start(bf16[48,896]{1,0:T(8,128)(2,1)S(1)} %get-tuple-element.57), channel_id=1, source_target_pairs={{0,3},{1,2},{2,1},{3,0},{4,7},{5,6},{6,5},{7,4},{8,11},{9,10},{10,... | collective-permute-start | bytes 258056 | tf_op jit(solution)/shard_map/ppermute | solution.py:230
  13.3 9.6 %collective-permute-start.14 = (bf16[48,896]{1,0:T(8,128)(2,1)S(1)}, bf16[48,896]{1,0:T(8,128)(2,1)S(1)}, u32[]{:S(2)}, u32[]{:S(2)}) collective-permute-start(bf16[48,896]{1,0:T(8,128)(2,1)S(1)} %get-tuple-element.58), channel_id=1, source_target_pairs={{0,6},{1,7},{2,4},{3,5},{4,2},{5,3},{6,0},{7,1},{8,14},{9,15},{10,... | collective-permute-start | bytes 258056 | tf_op jit(solution)/shard_map/ppermute | solution.py:230
  16.6 6.6 %collective-permute-start.15 = (bf16[48,896]{1,0:T(8,128)(2,1)S(1)}, bf16[48,896]{1,0:T(8,128)(2,1)S(1)}, u32[]{:S(2)}, u32[]{:S(2)}) collective-permute-start(bf16[48,896]{1,0:T(8,128)(2,1)S(1)} %get-tuple-element.59), channel_id=1, source_target_pairs={{0,7},{1,6},{2,5},{3,4},{4,3},{5,2},{6,1},{7,0},{8,15},{9,14},{10,... | collective-permute-start | bytes 258056 | tf_op jit(solution)/shard_map/ppermute | solution.py:230
  18.8 8.9 %collective-permute-start.3 = (bf16[192,512]{1,0:T(8,128)(2,1)S(1)}, bf16[192,512]{1,0:T(8,128)(2,1)S(1)}, u32[]{:S(2)}, u32[]{:S(2)}) collective-permute-start(bf16[192,512]{1,0:T(8,128)(2,1)S(1)} %up.10), channel_id=1, source_target_pairs={{0,8},{8,0},{16,24},{24,16},{1,9},{9,1},{17,25},{25,17},{2,10},{10... | collective-permute-start | bytes 589832 | tf_op jit(solution)/shard_map/ppermute | solution.py:323
  20.8 11.9 %collective-permute-start.4 = (bf16[192,512]{1,0:T(8,128)(2,1)S(1)}, bf16[192,512]{1,0:T(8,128)(2,1)S(1)}, u32[]{:S(2)}, u32[]{:S(2)}) collective-permute-start(bf16[192,512]{1,0:T(8,128)(2,1)S(1)} %up.11), channel_id=1, source_target_pairs={{0,16},{8,24},{16,0},{24,8},{1,17},{9,25},{17,1},{25,9},{2,18},{10... | collective-permute-start | bytes 589832 | tf_op jit(solution)/shard_map/ppermute | solution.py:323
  22.4 10.3 %collective-permute-start.5 = (bf16[192,512]{1,0:T(8,128)(2,1)S(1)}, bf16[192,512]{1,0:T(8,128)(2,1)S(1)}, u32[]{:S(2)}, u32[]{:S(2)}) collective-permute-start(bf16[192,512]{1,0:T(8,128)(2,1)S(1)} %get-tuple-element.49), channel_id=1, source_target_pairs={{0,24},{8,16},{16,8},{24,0},{1,25},{9,17},{17,9},{25,1},{2,26},{10... | collective-permute-start | bytes 589832 | tf_op jit(solution)/shard_map/ppermute | solution.py:323
  24.1 11.0 %collective-permute-start.16 = (bf16[192,512]{1,0:T(8,128)(2,1)S(1)}, bf16[192,512]{1,0:T(8,128)(2,1)S(1)}, u32[]{:S(2)}, u32[]{:S(2)}) collective-permute-start(bf16[192,512]{1,0:T(8,128)(2,1)S(1)} %up.14), channel_id=1, source_target_pairs={{0,8},{8,0},{16,24},{24,16},{1,9},{9,1},{17,25},{25,17},{2,10},{10... | collective-permute-start | bytes 589832 | tf_op jit(solution)/shard_map/ppermute | solution.py:323
  26.1 17.2 %collective-permute-start.17 = (bf16[192,512]{1,0:T(8,128)(2,1)S(1)}, bf16[192,512]{1,0:T(8,128)(2,1)S(1)}, u32[]{:S(2)}, u32[]{:S(2)}) collective-permute-start(bf16[192,512]{1,0:T(8,128)(2,1)S(1)} %up.15), channel_id=1, source_target_pairs={{0,16},{8,24},{16,0},{24,8},{1,17},{9,25},{17,1},{25,9},{2,18},{10... | collective-permute-start | bytes 589832 | tf_op jit(solution)/shard_map/ppermute | solution.py:323
  27.7 15.6 %collective-permute-start.18 = (bf16[192,512]{1,0:T(8,128)(2,1)S(1)}, bf16[192,512]{1,0:T(8,128)(2,1)S(1)}, u32[]{:S(2)}, u32[]{:S(2)}) collective-permute-start(bf16[192,512]{1,0:T(8,128)(2,1)S(1)} %get-tuple-element.62), channel_id=1, source_target_pairs={{0,24},{8,16},{16,8},{24,0},{1,25},{9,17},{17,9},{25,1},{2,26},{10... | collective-permute-start | bytes 589832 | tf_op jit(solution)/shard_map/ppermute | solution.py:323
  32.8 14.2 %copy-start = (bf16[1,2,1024,896]{3,2,1,0:T(8,128)(2,1)S(1)}, bf16[1,2,1024,896]{3,2,1,0:T(8,128)(2,1)}, u32[]{:S(2)}) copy-start(bf16[1,2,1024,896]{3,2,1,0:T(8,128)(2,1)} %w.3) | copy-start | bytes 11010052
  32.9 12.3 %collective-permute-start.8 = (bf16[192,256]{1,0:T(8,128)(2,1)S(1)}, bf16[192,256]{1,0:T(8,128)(2,1)S(1)}, u32[]{:S(2)}, u32[]{:S(2)}) collective-permute-start(bf16[192,256]{1,0:T(8,128)(2,1)S(1)} %hidden.2.refs_0_), channel_id=1, source_target_pairs={{0,24},{8,16},{16,8},{24,0},{1,25},{9,17},{17,9},{25,1},{2,26},{10... | collective-permute-start | bytes 294920 | tf_op jit(solution)/shard_map/ppermute | solution.py:334
  34.5 12.5 %collective-permute-start.7 = (bf16[192,256]{1,0:T(8,128)(2,1)S(1)}, bf16[192,256]{1,0:T(8,128)(2,1)S(1)}, u32[]{:S(2)}, u32[]{:S(2)}) collective-permute-start(bf16[192,256]{1,0:T(8,128)(2,1)S(1)} %hidden.2.refs_0_), channel_id=1, source_target_pairs={{0,16},{8,24},{16,0},{24,8},{1,17},{9,25},{17,1},{25,9},{2,18},{10... | collective-permute-start | bytes 294920 | tf_op jit(solution)/shard_map/ppermute | solution.py:334
  35.1 11.8 %collective-permute-start.6 = (bf16[192,256]{1,0:T(8,128)(2,1)S(1)}, bf16[192,256]{1,0:T(8,128)(2,1)S(1)}, u32[]{:S(2)}, u32[]{:S(2)}) collective-permute-start(bf16[192,256]{1,0:T(8,128)(2,1)S(1)} %hidden.2.refs_0_), channel_id=1, source_target_pairs={{0,8},{8,0},{16,24},{24,16},{1,9},{9,1},{17,25},{25,17},{2,10},{10... | collective-permute-start | bytes 294920 | tf_op jit(solution)/shard_map/ppermute | solution.py:334
  43.4 5.6 %collective-permute-start.21 = (bf16[192,256]{1,0:T(8,128)(2,1)S(1)}, bf16[192,256]{1,0:T(8,128)(2,1)S(1)}, u32[]{:S(2)}, u32[]{:S(2)}) collective-permute-start(bf16[192,256]{1,0:T(8,128)(2,1)S(1)} %hidden.3.refs_0_), channel_id=1, source_target_pairs={{0,24},{8,16},{16,8},{24,0},{1,25},{9,17},{17,9},{25,1},{2,26},{10... | collective-permute-start | bytes 294920 | tf_op jit(solution)/shard_map/ppermute | solution.py:334
  45.0 5.0 %collective-permute-start.20 = (bf16[192,256]{1,0:T(8,128)(2,1)S(1)}, bf16[192,256]{1,0:T(8,128)(2,1)S(1)}, u32[]{:S(2)}, u32[]{:S(2)}) collective-permute-start(bf16[192,256]{1,0:T(8,128)(2,1)S(1)} %hidden.3.refs_0_), channel_id=1, source_target_pairs={{0,16},{8,24},{16,0},{24,8},{1,17},{9,25},{17,1},{25,9},{2,18},{10... | collective-permute-start | bytes 294920 | tf_op jit(solution)/shard_map/ppermute | solution.py:334
  45.2 5.1 %collective-permute-start.19 = (bf16[192,256]{1,0:T(8,128)(2,1)S(1)}, bf16[192,256]{1,0:T(8,128)(2,1)S(1)}, u32[]{:S(2)}, u32[]{:S(2)}) collective-permute-start(bf16[192,256]{1,0:T(8,128)(2,1)S(1)} %hidden.3.refs_0_), channel_id=1, source_target_pairs={{0,8},{8,0},{16,24},{24,16},{1,9},{9,1},{17,25},{25,17},{2,10},{10... | collective-permute-start | bytes 294920 | tf_op jit(solution)/shard_map/ppermute | solution.py:334
  48.2 8.5 %collective-permute-start.9 = (bf16[48,896]{1,0:T(8,128)(2,1)S(1)}, bf16[48,896]{1,0:T(8,128)(2,1)S(1)}, u32[]{:S(2)}, u32[]{:S(2)}) collective-permute-start(bf16[48,896]{1,0:T(8,128)(2,1)S(1)} %get-tuple-element.50), channel_id=1, source_target_pairs={{0,4},{1,5},{2,6},{3,7},{4,0},{5,1},{6,2},{7,3},{8,12},{9,13},{10,... | collective-permute-start | bytes 258056 | tf_op jit(solution)/shard_map/ppermute | solution.py:230
  48.3 10.1 %collective-permute-start.10 = (bf16[48,896]{1,0:T(8,128)(2,1)S(1)}, bf16[48,896]{1,0:T(8,128)(2,1)S(1)}, u32[]{:S(2)}, u32[]{:S(2)}) collective-permute-start(bf16[48,896]{1,0:T(8,128)(2,1)S(1)} %get-tuple-element.51), channel_id=1, source_target_pairs={{0,5},{1,4},{2,7},{3,6},{4,1},{5,0},{6,3},{7,2},{8,13},{9,12},{10,... | collective-permute-start | bytes 258056 | tf_op jit(solution)/shard_map/ppermute | solution.py:230
  51.5 7.6 %collective-permute-start.22 = (bf16[48,896]{1,0:T(8,128)(2,1)S(1)}, bf16[48,896]{1,0:T(8,128)(2,1)S(1)}, u32[]{:S(2)}, u32[]{:S(2)}) collective-permute-start(bf16[48,896]{1,0:T(8,128)(2,1)S(1)} %get-tuple-element.63), channel_id=1, source_target_pairs={{0,2},{1,3},{2,0},{3,1},{4,6},{5,7},{6,4},{7,5},{8,10},{9,11},{10,... | collective-permute-start | bytes 258056 | tf_op jit(solution)/shard_map/ppermute | solution.py:230
  52.4 6.4 %collective-permute-start.11 = (bf16[48,896]{1,0:T(8,128)(2,1)S(1)}, bf16[48,896]{1,0:T(8,128)(2,1)S(1)}, u32[]{:S(2)}, u32[]{:S(2)}) collective-permute-start(bf16[48,896]{1,0:T(8,128)(2,1)S(1)} %get-tuple-element.52), channel_id=1, source_target_pairs={{0,1},{1,0},{2,3},{3,2},{4,5},{5,4},{6,7},{7,6},{8,9},{9,8},{10,11... | collective-permute-start | bytes 258056 | tf_op jit(solution)/shard_map/ppermute | solution.py:230
  52.8 9.3 %collective-permute-start.23 = (bf16[48,896]{1,0:T(8,128)(2,1)S(1)}, bf16[48,896]{1,0:T(8,128)(2,1)S(1)}, u32[]{:S(2)}, u32[]{:S(2)}) collective-permute-start(bf16[48,896]{1,0:T(8,128)(2,1)S(1)} %get-tuple-element.64), channel_id=1, source_target_pairs={{0,3},{1,2},{2,1},{3,0},{4,7},{5,6},{6,5},{7,4},{8,11},{9,10},{10,... | collective-permute-start | bytes 258056 | tf_op jit(solution)/shard_map/ppermute | solution.py:230
  56.7 6.4 %collective-permute-start.24 = (bf16[48,896]{1,0:T(8,128)(2,1)S(1)}, bf16[48,896]{1,0:T(8,128)(2,1)S(1)}, u32[]{:S(2)}, u32[]{:S(2)}) collective-permute-start(bf16[48,896]{1,0:T(8,128)(2,1)S(1)} %get-tuple-element.65), channel_id=1, source_target_pairs={{0,6},{1,7},{2,4},{3,5},{4,2},{5,3},{6,0},{7,1},{8,14},{9,15},{10,... | collective-permute-start | bytes 258056 | tf_op jit(solution)/shard_map/ppermute | solution.py:230
  58.4 6.6 %collective-permute-start.25 = (bf16[48,896]{1,0:T(8,128)(2,1)S(1)}, bf16[48,896]{1,0:T(8,128)(2,1)S(1)}, u32[]{:S(2)}, u32[]{:S(2)}) collective-permute-start(bf16[48,896]{1,0:T(8,128)(2,1)S(1)} %get-tuple-element.66), channel_id=1, source_target_pairs={{0,7},{1,6},{2,5},{3,4},{4,3},{5,2},{6,1},{7,0},{8,15},{9,14},{10,... | collective-permute-start | bytes 258056 | tf_op jit(solution)/shard_map/ppermute | solution.py:230
where the time goes:
time: 66.1 us; the launch traced here: 65.9 us
  starting transfers between devices  30.9 us (47%)
  waiting for transfers between devices  21 us (32%)
  Pallas kernels  13.9 us (21%)
    ppermute x14, starting transfers between devices, exchange(): moved.append(lax.ppermute(piece, axis, flips(n, j)) if j else piece)  15.5 us
    ppermute x14, waiting for transfers between devices, exchange(): moved.append(lax.ppermute(piece, axis, flips(n, j)) if j else piece)  9.6 us
    ppermute x6, waiting for transfers between devices, on_device(): sums[k] = lax.ppermute(sums[k], 'dp', flips(parts, k))  9.55 us
    ppermute x6, starting transfers between devices, on_device(): sums[k] = lax.ppermute(sums[k], 'dp', flips(parts, k))  8.18 us
    ppermute x6, starting transfers between devices, on_device(): spread[k] = lax.ppermute(hidden, 'dp', flips(parts, k))  7.19 us
    pallas_call x1, Pallas kernels, on_device(): pl.pallas_call(stage_kernel, out_shape=[sds((2, cols, 2 * block), BF16)]...  3.87 us
    pallas_call x8, Pallas kernels, on_device(): pl.pallas_call(up_next_kernel if i else functools.partial(up_first_kernel...  3.46 us
    pallas_call x1, Pallas kernels, on_device(): pl.pallas_call(functools.partial(route_kernel, (experts, hot, room, half,...  2.53 us
  transfers between devices with their start and end apart: 26, of which 13 were waited for; matrix products, arithmetic and copies ran while one was open for 0% of the time, Pallas kernels for 16%

commit v1 on v0

v1 whole, which is shorter than its diff:
```python
import functools

import jax
import jax.numpy as jnp
from jax import lax
from jax.experimental import pallas as pl
from jax.experimental.pallas import tpu as pltpu
from jax.sharding import PartitionSpec as P


BF16 = jnp.bfloat16
F32 = jnp.float32
I32 = jnp.int32
DIRECT_LIMIT = 8


def round_up(n, m):
    return -(-n // m) * m


def slot_room(token_count, top_count, expert_count):
    return max(2, min(token_count // 4, 3 * token_count * top_count // (4 * expert_count)))


def dot(a, b):
    return jnp.dot(a, b, preferred_element_type=F32)


def vmem_specs(n):
    return [pl.BlockSpec(memory_space=pltpu.VMEM)] * n


PARAMS = pltpu.CompilerParams(vmem_limit_bytes=24 * 2**20)


def in_hbm(x):
    return pltpu.with_memory_space_constraint(x, pltpu.HBM)


def cost(flops, size):
    return pl.CostEstimate(flops=flops, bytes_accessed=size, transcendentals=0)


def slots_of(sizes, place, cap, ids_ref, choice_ref):
    experts, hot = sizes[:2]
    top, count = ids_ref.shape
    key = (ids_ref[...] + experts * choice_ref[...]).astype(F32).T
    lane = lax.broadcasted_iota(I32, (count, 2 * experts), 1).astype(F32)
    hits = [key[:, k : k + 1] == lane for k in range(top)]
    member = jnp.zeros((count, 2 * experts), F32)
    for hit in hits:
        member = jnp.where(hit, 1.0, member)
    earlier = lax.broadcasted_iota(I32, (count, count), 1) < lax.broadcasted_iota(
        I32, (count, count), 0
    )
    rank = dot(jnp.where(earlier, 1.0, 0.0).astype(BF16), member.astype(BF16))
    lane_row = lax.broadcasted_iota(I32, (1, 2 * experts), 1)
    limit = jnp.zeros((1, 2 * experts), I32)
    for e in range(experts):
        limit = jnp.where(lane_row == e, cap[e], limit)
    for j in range(hot):
        limit = jnp.where(lane_row == place[0, j] + experts, cap[experts + j], limit)
    kept = (member > 0.5) & (rank < limit.astype(F32))
    return jnp.where(kept, rank, -1.0).astype(BF16), hits


def columns_of(sizes, place, chunk):
    experts, hot, _, half, room_a, room_b, direct = sizes
    per = room_a + room_b
    columns = len(chunk) * per
    column = lax.broadcasted_iota(I32, (1, columns), 1)
    block = jnp.floor((column.astype(F32) + 0.5) * (1.0 / per)).astype(I32)
    slot = column - block * per
    if direct:
        flip = jnp.zeros((1, columns), I32)
        for i, j in enumerate(chunk):
            flip = jnp.where(block == i, j, flip)
        dest = flip ^ lax.axis_index("expert")
    else:
        dest = block + chunk[0]
    pair_key = jnp.full((1, columns), -1, I32)
    start = jnp.zeros((1, columns), I32)
    for j in range(hot):
        owner, host = dest == place[0, j], dest == place[1, j]
        pair_key = jnp.where(owner | host, place[0, j] + experts, pair_key)
        start = jnp.where(host, half, start)
    first = slot < room_a
    in_pair = slot - room_a
    wanted = jnp.where(first, dest, jnp.where(in_pair < half, pair_key, -1))
    place_rank = jnp.where(first, slot, in_pair + start).astype(F32)
    place_rank = jnp.where(wanted >= 0, place_rank, -2.0)
    spread = jnp.where(
        lax.broadcasted_iota(I32, (2 * experts, columns), 0) == wanted, 1.0, 0.0
    ).astype(BF16)
    return spread, place_rank


def fetch(pairs, sems):
    copies = [
        pltpu.make_async_copy(src, dst, sems.at[i]) for i, (src, dst) in enumerate(pairs)
    ]
    for copy in copies:
        copy.start()
    return copies


def route_kernel(sizes, chunks, place_in, cap_in, ids_in, choice_in, tok_in, *refs):
    pieces = refs[:-6]
    place, cap, ids_ref, choice_ref, tok_ref, sems = refs[-6:]
    copies = fetch(
        (
            (ids_in, ids_ref),
            (choice_in, choice_ref),
            (place_in, place),
            (cap_in, cap),
            (tok_in, tok_ref),
        ),
        sems,
    )
    for copy in copies[:4]:
        copy.wait()
    rank, _ = slots_of(sizes, place, cap, ids_ref, choice_ref)
    per = pieces[0].shape[0]
    done = 0
    for chunk in chunks:
        spread, place_rank = columns_of(sizes, place, chunk)
        picks = jnp.where(dot(rank, spread) == place_rank, 1.0, 0.0).T.astype(BF16)
        if not done:
            copies[4].wait()
        rows = dot(picks, tok_ref[...]).astype(BF16)
        for i in range(len(chunk)):
            pieces[done + i][...] = rows[i * per : (i + 1) * per]
        done += len(chunk)


def weigh_kernel(sizes, chunks, place_in, cap_in, ids_in, choice_in, gate_in, *refs):
    mats = refs[:-6]
    place, cap, ids_ref, choice_ref, gate_ref, sems = refs[-6:]
    copies = fetch(
        (
            (ids_in, ids_ref),
            (choice_in, choice_ref),
            (place_in, place),
            (cap_in, cap),
            (gate_in, gate_ref),
        ),
        sems,
    )
    for copy in copies:
        copy.wait()
    rank, hits = slots_of(sizes, place, cap, ids_ref, choice_ref)
    gate = gate_ref[...].T
    weight = jnp.zeros(rank.shape, F32)
    for k, hit in enumerate(hits):
        weight = jnp.where(hit, gate[:, k : k + 1], weight)
    weight_high = weight.astype(BF16)
    weight_low = (weight - weight_high.astype(F32)).astype(BF16)
    for c, chunk in enumerate(chunks):
        spread, place_rank = columns_of(sizes, place, chunk)
        chosen = dot(rank, spread) == place_rank
        for part, out in zip((weight_high, weight_low), mats[2 * c : 2 * c + 2]):
            out[...] = jnp.where(chosen, dot(part, spread), 0.0).astype(BF16)


def hosting(place):
    found = jnp.int32(0)
    for j in range(place.shape[1]):
        found = jnp.where(place[1, j] == lax.axis_index("expert"), 1, found)
    return found


def stage_weights(place_in, place, sems, moves):
    looked = pltpu.make_async_copy(place_in, place, sems.at[0])
    looked.start()
    copies = []

    def begin(which, i):
        for src, dst in moves(which, i):
            copies.append(pltpu.make_async_copy(src, dst, sems.at[len(copies) + 1]))
            copies[-1].start()

    begin(0, 0)
    looked.wait()
    begin(hosting(place), 1)
    for copy in copies:
        copy.wait()


def stage_kernel(place_in, w_gate, w_up, *refs):
    outs, place, sems = refs[:-2], refs[-2], refs[-1]
    block = outs[0].shape[2] // 2

    def moves(which, i):
        for k, out in enumerate(outs):
            q = lax.axis_index("dp") ^ k
            columns = pl.ds(pl.multiple_of(q * block, block), block)
            for g, w in enumerate((w_gate, w_up)):
                yield w.at[0, which, :, columns], out.at[i, :, pl.ds(g * block, block)]

    stage_weights(place_in, place, sems, moves)


def stage_down_kernel(parts, place_in, w_down, out, place, sems):
    block = out.shape[1] // parts

    def moves(which, i):
        for k in range(parts):
            q = lax.axis_index("dp") ^ k
            units = pl.ds(pl.multiple_of(q * block, block), block)
            yield w_down.at[0, which, units], out.at[i, pl.ds(k * block, block)]

    stage_weights(place_in, place, sems, moves)


def up_sums(xa, xb, weights, out):
    rows_a = xa.shape[0]
    out[:rows_a] = dot(xa, weights[0]).astype(out.dtype)
    out[rows_a:] = dot(xb, weights[1]).astype(out.dtype)


def up_first_kernel(sizes, *refs):
    blocks, room_a, room_b = sizes
    x_refs, weights = refs[:blocks], refs[blocks]
    out, xa, xb = refs[blocks + 1 :]
    for i, ref in enumerate(x_refs):
        xa[i * room_a : (i + 1) * room_a] = ref[:room_a]
        xb[i * room_b : (i + 1) * room_b] = ref[room_a:]
    up_sums(xa[...], xb[...], weights, out)


def up_next_kernel(xa, xb, weights, out):
    up_sums(xa[...], xb[...], weights, out)


def hidden_kernel(own, *refs):
    out = refs[-1]
    block = own.shape[1] // 2
    total = own[...]
    for ref in refs[:-1]:
        total += ref[...].astype(F32)
    out[...] = (jax.nn.silu(total[:, :block]) * total[:, block:]).astype(BF16)


def down_kernel(sizes, w, *refs):
    parts, blocks, room_a, room_b = sizes
    hids, outs, full = refs[:parts], refs[parts:-1], refs[-1]
    rows_a, depth = blocks * room_a, hids[0].shape[1]
    for k, h in enumerate(hids):
        full[:, k * depth : (k + 1) * depth] = h[...]
    ra = dot(full[:rows_a], w[0]).astype(BF16)
    rb = dot(full[rows_a:], w[1]).astype(BF16)
    for i, out in enumerate(outs):
        out[:room_a] = ra[i * room_a : (i + 1) * room_a]
        out[room_a:] = rb[i * room_b : (i + 1) * room_b]


def combine_kernel(has_base, *refs):
    base, (high, low) = refs[:has_base], refs[has_base : has_base + 2]
    pieces, out, res = refs[has_base + 2 : -2], refs[-2], refs[-1]
    per = pieces[0].shape[0]
    for i, ref in enumerate(pieces):
        res[i * per : (i + 1) * per] = ref[...]
    rows = res[...]
    total = dot(high[...], rows) + dot(low[...], rows)
    for ref in base:
        total += ref[...]
    out[...] = total.astype(out.dtype)


def flips(n, j):
    return [(i, i ^ j) for i in range(n)]


def exchange(pieces, chunks, axis):
    n = len(pieces)
    if n > DIRECT_LIMIT:
        moved = lax.all_to_all(jnp.stack(pieces), axis, split_axis=0, concat_axis=0, tiled=True)
        return [moved[i] for i in range(n)]
    moved = []
    for j, piece in zip([j for chunk in chunks for j in chunk], pieces):
        moved.append(lax.ppermute(piece, axis, flips(n, j)) if j else piece)
    return moved


def chunks_of(experts):
    if experts == 8:
        return ((4, 5, 1, 0), (2, 3, 6, 7))
    return (tuple(range(experts)),)


def on_device(
    tokens, expert_ids, replica_choice, gate_weights, placement, capacity, w_gate, w_up, w_down
):
    experts = lax.axis_size("expert")
    parts = lax.axis_size("dp")
    count, cols = tokens.shape
    ff = w_gate.shape[3]
    hot = placement.shape[0]
    room = slot_room(count, expert_ids.shape[1], experts)
    half = -(-room // 2)
    room_a, room_b = round_up(room, 16), round_up(half, 16)
    per = room_a + room_b
    chunks = chunks_of(experts)
    sds = jax.ShapeDtypeStruct
    hbm = pl.BlockSpec(memory_space=pltpu.HBM)
    top = expert_ids.shape[1]
    sizes = (experts, hot, room, half, room_a, room_b, experts <= DIRECT_LIMIT)
    small = [placement.T, capacity, expert_ids.T, replica_choice.T]
    small_scratch = [
        pltpu.SMEM((2, hot), I32),
        pltpu.SMEM(capacity.shape, I32),
        pltpu.VMEM((top, count), I32),
        pltpu.VMEM((top, count), I32),
    ]
    pieces = pl.pallas_call(
        functools.partial(route_kernel, sizes, chunks),
        out_shape=[sds((per, cols), BF16)] * experts,
        in_specs=[hbm] * 5,
        out_specs=vmem_specs(experts),
        scratch_shapes=small_scratch
        + [pltpu.VMEM((count, cols), BF16), pltpu.SemaphoreType.DMA((5,))],
        compiler_params=PARAMS,
        name="route",
    )(*map(in_hbm, [*small, tokens]))
    mat_shapes = [sds((count, len(c) * per), BF16) for c in chunks for _ in range(2)]
    mats = pl.pallas_call(
        functools.partial(weigh_kernel, sizes, chunks),
        out_shape=mat_shapes,
        in_specs=[hbm] * 5,
        out_specs=vmem_specs(len(mat_shapes)),
        scratch_shapes=small_scratch
        + [pltpu.VMEM((top, count), F32), pltpu.SemaphoreType.DMA((5,))],
        compiler_params=PARAMS,
        name="weigh",
    )(*map(in_hbm, [*small, gate_weights.T]))
    arrived = exchange(pieces, chunks, "expert")

    block = ff // parts
    order = list(range(parts - 1, 0, -1)) + [0]
    staged = pl.pallas_call(
        stage_kernel,
        out_shape=[sds((2, cols, 2 * block), BF16)] * parts,
        in_specs=[hbm] * 3,
        out_specs=vmem_specs(parts),
        scratch_shapes=[pltpu.SMEM((2, hot), I32), pltpu.SemaphoreType.DMA((4 * parts + 1,))],
        compiler_params=PARAMS,
        cost_estimate=cost(0, 16 * cols * ff),
        name="stage",
    )(*map(in_hbm, [placement.T, w_gate, w_up]))
    staged_down = pl.pallas_call(
        functools.partial(stage_down_kernel, parts),
        out_shape=sds((2, ff, cols), BF16),
        in_specs=[hbm] * 2,
        out_specs=vmem_specs(1)[0],
        scratch_shapes=[pltpu.SMEM((2, hot), I32), pltpu.SemaphoreType.DMA((2 * parts + 1,))],
        compiler_params=PARAMS,
        cost_estimate=cost(0, 8 * cols * ff),
        name="stage_down",
    )(*map(in_hbm, [placement.T, w_down]))

    results, done = [], 0
    for chunk in chunks:
        blocks = len(chunk)
        rows_a, rows = blocks * room_a, blocks * per
        step = 2 * rows * cols * block
        sums = {}
        for i, k in enumerate(order):
            piece = sds((rows, 2 * block), BF16 if k else F32)
            halves = [sds((rows_a, cols), BF16), sds((rows - rows_a, cols), BF16)]
            made = pl.pallas_call(
                up_next_kernel
                if i
                else functools.partial(up_first_kernel, (blocks, room_a, room_b)),
                out_shape=[piece] + ([] if i else halves),
                in_specs=vmem_specs(3 if i else blocks + 1),
                out_specs=vmem_specs(1 if i else 3),
                compiler_params=PARAMS,
                cost_estimate=cost(2 * step, rows * (cols + 2 * block) * 2),
                name="up",
            )(*([xa, xb] if i else arrived[done : done + blocks]), staged[k])
            sums[k] = made[0]
            if not i:
                xa, xb = made[1:]
            if k:
                sums[k] = lax.ppermute(sums[k], "dp", flips(parts, k))
        hidden = pl.pallas_call(
            hidden_kernel,
            out_shape=sds((rows, block), BF16),
            in_specs=vmem_specs(parts),
            out_specs=vmem_specs(1)[0],
            compiler_params=PARAMS,
            name="hidden",
        )(*[sums[k] for k in range(parts)])
        spread = {0: hidden}
        for k in order[:-1]:
            spread[k] = lax.ppermute(hidden, "dp", flips(parts, k))
        results += pl.pallas_call(
            functools.partial(down_kernel, (parts, blocks, room_a, room_b)),
            out_shape=[sds((per, cols), BF16)] * blocks,
            in_specs=vmem_specs(1 + parts),
            out_specs=vmem_specs(blocks),
            scratch_shapes=[pltpu.VMEM((rows, ff), BF16)],
            compiler_params=PARAMS,
            cost_estimate=cost(parts * step, 4 * cols * ff),
            name="down",
        )(staged_down, *[spread[k] for k in range(parts)])
        done += blocks
    returned = exchange(results, chunks, "expert")
    total, done = [], 0
    for c, chunk in enumerate(chunks):
        last = c + 1 == len(chunks)
        total = [
            pl.pallas_call(
                functools.partial(combine_kernel, len(total)),
                out_shape=sds((count, cols), BF16 if last else F32),
                in_specs=vmem_specs(len(total) + 2 + len(chunk)),
                out_specs=vmem_specs(1)[0],
                scratch_shapes=[pltpu.VMEM((len(chunk) * per, cols), BF16)],
                compiler_params=PARAMS,
                name="combine",
            )(*total, *mats[2 * c : 2 * c + 2], *returned[done : done + len(chunk)])
        ]
        done += len(chunk)
    return total[0]


def solution(mesh):
    return jax.shard_map(
        on_device,
        mesh=mesh,
        in_specs=(
            P("expert", "dp"),
            P("expert", None),
            P("expert", None),
            P("expert", None),
            P(),
            P(),
            P("expert", None, "dp", None),
            P("expert", None, "dp", None),
            P("expert", None, None, "dp"),
        ),
        out_specs=P("expert", "dp"),
        check_vma=False,
    )
```

time: 66.1 us -> 64 us (0.968)
  waiting for transfers between devices: 21 us -> 14 us
  Pallas kernels: 13.9 us -> 16 us
  starting transfers between devices: 30.9 us -> 32.9 us
    ppermute x14, waiting for transfers between devices: 9.6 us -> 5.12 us  [exchange(): moved.append(lax.ppermute(piece, axis, flips(n, j)) if j else piece)]
    pallas_call x1 -> x3, Pallas kernels: 2.53 us -> 6.17 us  [the longest x1 2.34 us: on_device(): pl.pallas_call(functools.partial(stage_down_kernel, parts), out_shape=sds...]
    ppermute x6, waiting for transfers between devices: 9.55 us -> 7.13 us  [on_device(): sums[k] = lax.ppermute(sums[k], 'dp', flips(parts, k))]
    ppermute x14, starting transfers between devices: 15.5 us -> 16.9 us  [exchange(): moved.append(lax.ppermute(piece, axis, flips(n, j)) if j else piece)]
    pallas_call x2, Pallas kernels: 2.52 us -> 1.43 us  [on_device(): pl.pallas_call(functools.partial(down_kernel, (parts, blocks, room_a, roo...]
    ppermute x6, starting transfers between devices: 7.19 us -> 8.2 us  [on_device(): spread[k] = lax.ppermute(hidden, 'dp', flips(parts, k))]
  transfers between devices with their start and end apart: 26 -> 26, of which waited for: 13 -> 9; matrix products, arithmetic and copies ran while one was open for 0% -> 0% of each run, Pallas kernels for 16% -> 20%
where the time goes in v1:
time: 64 us; the launch traced here: 63.2 us
  starting transfers between devices  32.9 us (51%)
  Pallas kernels  16 us (25%)
  waiting for transfers between devices  14 us (22%)
    ppermute x14, starting transfers between devices, exchange(): moved.append(lax.ppermute(piece, axis, flips(n, j)) if j else piece)  16.9 us
    ppermute x6, starting transfers between devices, on_device(): spread[k] = lax.ppermute(hidden, 'dp', flips(parts, k))  8.2 us
    ppermute x6, starting transfers between devices, on_device(): sums[k] = lax.ppermute(sums[k], 'dp', flips(parts, k))  7.82 us
    ppermute x6, waiting for transfers between devices, on_device(): sums[k] = lax.ppermute(sums[k], 'dp', flips(parts, k))  7.13 us
    ppermute x14, waiting for transfers between devices, exchange(): moved.append(lax.ppermute(piece, axis, flips(n, j)) if j else piece)  5.12 us
    pallas_call x1, Pallas kernels, on_device(): pl.pallas_call(stage_kernel, out_shape=[sds((2, cols, 2 * block), BF16)]...  3.49 us
    pallas_call x8, Pallas kernels, on_device(): pl.pallas_call(up_next_kernel if i else functools.partial(up_first_kernel...  3.43 us
    pallas_call x1, Pallas kernels, on_device(): pl.pallas_call(functools.partial(stage_down_kernel, parts), out_shape=sds...  2.34 us
  transfers between devices with their start and end apart: 26, of which 9 were waited for; matrix products, arithmetic and copies ran while one was open for 0% of the time, Pallas kernels for 20%

profile of v1, /device:TPU:0, one launch (start us, length us, event | category | flops | bytes accessed | tf_op | source)
XLA Modules:
  0.0 63.2 jit_solution(6238229332018466678)
XLA Ops:
  0.0 2.1 %route.1 = (bf16[48,896]{1,0:T(8,128)(2,1)S(1)}, bf16[48,896]{1,0:T(8,128)(2,1)S(1)}, bf16[48,896]{1,0:T(8,128)(2,1)S(1)}, bf16[48,896]{1,0:T(8,128)(2,1)S(1)}, ...) custom-call(s32[2,4]{1,0:T(2,128)} %bitcast.8, ...), custom_call_target="tpu_custom_call" | custom-call | tf_op jit(solution)/shard_map/route/pallas_call | solution.py:315
  2.1 4.1 %collective-permute-start = (bf16[48,896]{1,0:T(8,128)(2,1)S(1)}, bf16[48,896]{1,0:T(8,128)(2,1)S(1)}, u32[]{:S(2)}, u32[]{:S(2)}) collective-permute-start(bf16[48,896]{1,0:T(8,128)(2,1)S(1)} %get-tuple-element.37), channel_id=1, source_target_pairs={{0,4},{1,5},{2,6},{3,7},{4,0},{5,1},{6,2},{7,3},{8,12},{9,13},{10,... | collective-permute-start | bytes 258056 | tf_op jit(solution)/shard_map/ppermute | solution.py:281
  6.4 1.8 %collective-permute-start.12 = (bf16[48,896]{1,0:T(8,128)(2,1)S(1)}, bf16[48,896]{1,0:T(8,128)(2,1)S(1)}, u32[]{:S(2)}, u32[]{:S(2)}) collective-permute-start(bf16[48,896]{1,0:T(8,128)(2,1)S(1)} %get-tuple-element.54), channel_id=1, source_target_pairs={{0,2},{1,3},{2,0},{3,1},{4,6},{5,7},{6,4},{7,5},{8,10},{9,11},{10,... | collective-permute-start | bytes 258056 | tf_op jit(solution)/shard_map/ppermute | solution.py:281
  8.3 3.5 %stage.1 = (bf16[2,896,512]{2,1,0:T(8,128)(2,1)S(1)}, bf16[2,896,512]{2,1,0:T(8,128)(2,1)S(1)}, bf16[2,896,512]{2,1,0:T(8,128)(2,1)S(1)}, bf16[2,896,512]{2,1,0:T(8,128)(2,1)S(1)}) custom-call(s32[2,4]{1,0:T(2,128)} %bitcast.9, bf16[1,2,896,1024]{3,2,1,0:T(8,128)(2,1)} %w_gate.1, bf16[1,2,896,1024]{3,2,1,0:T(8,128)(2,1)} %w_up.1), custom_call_target="tpu_custom_call" | custom-call | bytes 14680064 | tf_op jit(solution)/shard_map/stage/pallas_call | solution.py:340
  11.8 1.1 %collective-permute-done.refs_0_ = bf16[48,896]{1,0:T(8,128)(2,1)S(1)} collective-permute-done((bf16[48,896]{1,0:T(8,128)(2,1)S(1)}, bf16[48,896]{1,0:T(8,128)(2,1)S(1)}, u32[]{:S(2)}, u32[]{:S(2)}) %collective-permute-start) | collective-permute-done | bytes 86048 | tf_op jit(solution)/shard_map/ppermute | solution.py:281
  12.8 3.3 %collective-permute-start.14 = (bf16[48,896]{1,0:T(8,128)(2,1)S(1)}, bf16[48,896]{1,0:T(8,128)(2,1)S(1)}, u32[]{:S(2)}, u32[]{:S(2)}) collective-permute-start(bf16[48,896]{1,0:T(8,128)(2,1)S(1)} %get-tuple-element.56), channel_id=1, source_target_pairs={{0,6},{1,7},{2,4},{3,5},{4,2},{5,3},{6,0},{7,1},{8,14},{9,15},{10,... | collective-permute-start | bytes 258056 | tf_op jit(solution)/shard_map/ppermute | solution.py:281
  16.2 1.3 %collective-permute-start.15 = (bf16[48,896]{1,0:T(8,128)(2,1)S(1)}, bf16[48,896]{1,0:T(8,128)(2,1)S(1)}, u32[]{:S(2)}, u32[]{:S(2)}) collective-permute-start(bf16[48,896]{1,0:T(8,128)(2,1)S(1)} %get-tuple-element.57), channel_id=1, source_target_pairs={{0,7},{1,6},{2,5},{3,4},{4,3},{5,2},{6,1},{7,0},{8,15},{9,14},{10,... | collective-permute-start | bytes 258056 | tf_op jit(solution)/shard_map/ppermute | solution.py:281
  18.4 1.6 %collective-permute-start.4 = (bf16[192,512]{1,0:T(8,128)(2,1)S(1)}, bf16[192,512]{1,0:T(8,128)(2,1)S(1)}, u32[]{:S(2)}, u32[]{:S(2)}) collective-permute-start(bf16[192,512]{1,0:T(8,128)(2,1)S(1)} %up.11), channel_id=1, source_target_pairs={{0,16},{8,24},{16,0},{24,8},{1,17},{9,25},{17,1},{25,9},{2,18},{10... | collective-permute-start | bytes 589832 | tf_op jit(solution)/shard_map/ppermute | solution.py:385
  20.4 1.6 %collective-permute-start.3 = (bf16[192,512]{1,0:T(8,128)(2,1)S(1)}, bf16[192,512]{1,0:T(8,128)(2,1)S(1)}, u32[]{:S(2)}, u32[]{:S(2)}) collective-permute-start(bf16[192,512]{1,0:T(8,128)(2,1)S(1)} %up.10), channel_id=1, source_target_pairs={{0,8},{8,0},{16,24},{24,16},{1,9},{9,1},{17,25},{25,17},{2,10},{10... | collective-permute-start | bytes 589832 | tf_op jit(solution)/shard_map/ppermute | solution.py:385
  23.5 1.6 %collective-permute-start.17 = (bf16[192,512]{1,0:T(8,128)(2,1)S(1)}, bf16[192,512]{1,0:T(8,128)(2,1)S(1)}, u32[]{:S(2)}, u32[]{:S(2)}) collective-permute-start(bf16[192,512]{1,0:T(8,128)(2,1)S(1)} %up.15), channel_id=1, source_target_pairs={{0,16},{8,24},{16,0},{24,8},{1,17},{9,25},{17,1},{25,9},{2,18},{10... | collective-permute-start | bytes 589832 | tf_op jit(solution)/shard_map/ppermute | solution.py:385
  25.5 1.6 %collective-permute-start.16 = (bf16[192,512]{1,0:T(8,128)(2,1)S(1)}, bf16[192,512]{1,0:T(8,128)(2,1)S(1)}, u32[]{:S(2)}, u32[]{:S(2)}) collective-permute-start(bf16[192,512]{1,0:T(8,128)(2,1)S(1)} %up.14), channel_id=1, source_target_pairs={{0,8},{8,0},{16,24},{24,16},{1,9},{9,1},{17,25},{25,17},{2,10},{10... | collective-permute-start | bytes 589832 | tf_op jit(solution)/shard_map/ppermute | solution.py:385
  27.1 1.1 %collective-permute-start.18 = (bf16[192,512]{1,0:T(8,128)(2,1)S(1)}, bf16[192,512]{1,0:T(8,128)(2,1)S(1)}, u32[]{:S(2)}, u32[]{:S(2)}) collective-permute-start(bf16[192,512]{1,0:T(8,128)(2,1)S(1)} %get-tuple-element.60), channel_id=1, source_target_pairs={{0,24},{8,16},{16,8},{24,0},{1,25},{9,17},{17,9},{25,1},{2,26},{10... | collective-permute-start | bytes 589832 | tf_op jit(solution)/shard_map/ppermute | solution.py:385
  28.6 3.9 %collective-permute-done.5.refs_2_ = bf16[192,512]{1,0:T(8,128)(2,1)S(1)} collective-permute-done((bf16[192,512]{1,0:T(8,128)(2,1)S(1)}, bf16[192,512]{1,0:T(8,128)(2,1)S(1)}, u32[]{:S(2)}, u32[]{:S(2)}) %collective-permute-start.5) | collective-permute-done | bytes 196640 | tf_op jit(solution)/shard_map/ppermute | solution.py:385
  32.6 1.6 %collective-permute-start.6 = (bf16[192,256]{1,0:T(8,128)(2,1)S(1)}, bf16[192,256]{1,0:T(8,128)(2,1)S(1)}, u32[]{:S(2)}, u32[]{:S(2)}) collective-permute-start(bf16[192,256]{1,0:T(8,128)(2,1)S(1)} %hidden.2.refs_0_), channel_id=1, source_target_pairs={{0,8},{8,0},{16,24},{24,16},{1,9},{9,1},{17,25},{25,17},{2,10},{10... | collective-permute-start | bytes 294920 | tf_op jit(solution)/shard_map/ppermute | solution.py:396
  34.1 1.5 %collective-permute-start.7 = (bf16[192,256]{1,0:T(8,128)(2,1)S(1)}, bf16[192,256]{1,0:T(8,128)(2,1)S(1)}, u32[]{:S(2)}, u32[]{:S(2)}) collective-permute-start(bf16[192,256]{1,0:T(8,128)(2,1)S(1)} %hidden.2.refs_0_), channel_id=1, source_target_pairs={{0,16},{8,24},{16,0},{24,8},{1,17},{9,25},{17,1},{25,9},{2,18},{10... | collective-permute-start | bytes 294920 | tf_op jit(solution)/shard_map/ppermute | solution.py:396
  35.7 1.6 %collective-permute-start.8 = (bf16[192,256]{1,0:T(8,128)(2,1)S(1)}, bf16[192,256]{1,0:T(8,128)(2,1)S(1)}, u32[]{:S(2)}, u32[]{:S(2)}) collective-permute-start(bf16[192,256]{1,0:T(8,128)(2,1)S(1)} %hidden.2.refs_0_), channel_id=1, source_target_pairs={{0,24},{8,16},{16,8},{24,0},{1,25},{9,17},{17,9},{25,1},{2,26},{10... | collective-permute-start | bytes 294920 | tf_op jit(solution)/shard_map/ppermute | solution.py:396
  37.7 3.3 %collective-permute-done.18.refs_2_ = bf16[192,512]{1,0:T(8,128)(2,1)S(1)} collective-permute-done((bf16[192,512]{1,0:T(8,128)(2,1)S(1)}, bf16[192,512]{1,0:T(8,128)(2,1)S(1)}, u32[]{:S(2)}, u32[]{:S(2)}) %collective-permute-start.18) | collective-permute-done | bytes 196640 | tf_op jit(solution)/shard_map/ppermute | solution.py:385
  41.0 1.6 %collective-permute-start.19 = (bf16[192,256]{1,0:T(8,128)(2,1)S(1)}, bf16[192,256]{1,0:T(8,128)(2,1)S(1)}, u32[]{:S(2)}, u32[]{:S(2)}) collective-permute-start(bf16[192,256]{1,0:T(8,128)(2,1)S(1)} %hidden.3.refs_0_), channel_id=1, source_target_pairs={{0,8},{8,0},{16,24},{24,16},{1,9},{9,1},{17,25},{25,17},{2,10},{10... | collective-permute-start | bytes 294920 | tf_op jit(solution)/shard_map/ppermute | solution.py:396
  42.6 1.5 %collective-permute-start.20 = (bf16[192,256]{1,0:T(8,128)(2,1)S(1)}, bf16[192,256]{1,0:T(8,128)(2,1)S(1)}, u32[]{:S(2)}, u32[]{:S(2)}) collective-permute-start(bf16[192,256]{1,0:T(8,128)(2,1)S(1)} %hidden.3.refs_0_), channel_id=1, source_target_pairs={{0,16},{8,24},{16,0},{24,8},{1,17},{9,25},{17,1},{25,9},{2,18},{10... | collective-permute-start | bytes 294920 | tf_op jit(solution)/shard_map/ppermute | solution.py:396
  44.6 2.3 %stage_down.1.w = bf16[2,1024,896]{2,1,0:T(8,128)(2,1)S(1)} custom-call(s32[2,4]{1,0:T(2,128)} %bitcast.10, bf16[1,2,1024,896]{3,2,1,0:T(8,128)(2,1)} %w_down.1), custom_call_target="tpu_custom_call" | custom-call | bytes 7340032 | tf_op jit(solution)/shard_map/stage_down/pallas_call | solution.py:350
  47.0 0.7 %down.2 = (bf16[48,896]{1,0:T(8,128)(2,1)S(1)}, bf16[48,896]{1,0:T(8,128)(2,1)S(1)}, bf16[48,896]{1,0:T(8,128)(2,1)S(1)}, bf16[48,896]{1,0:T(8,128)(2,1)S(1)}) custom-call(bf16[2,1024,896]{2,1,0:T(8,128)(2,1)S(1)} %stage_down.1.w, bf16[192,256]{1,0:T(8,128)(2,1)S(1)} %hidden.2.refs_0_, bf16[192,256]{1,0:T(8,128)(2,1)S(1)} %collective-permute-done.6.refs_1_, ...), custom_call_target="tpu_custom_call" | custom-call | flops 352321536 | bytes 3670016 | tf_op jit(solution)/shard_map/down/pallas_call | solution.py:397
  48.1 1.5 %collective-permute-done.21.refs_3_ = bf16[192,256]{1,0:T(8,128)(2,1)S(1)} collective-permute-done((bf16[192,256]{1,0:T(8,128)(2,1)S(1)}, bf16[192,256]{1,0:T(8,128)(2,1)S(1)}, u32[]{:S(2)}, u32[]{:S(2)}) %collective-permute-start.21) | collective-permute-done | bytes 98336 | tf_op jit(solution)/shard_map/ppermute | solution.py:396
  49.6 0.7 %down.3 = (bf16[48,896]{1,0:T(8,128)(2,1)S(1)}, bf16[48,896]{1,0:T(8,128)(2,1)S(1)}, bf16[48,896]{1,0:T(8,128)(2,1)S(1)}, bf16[48,896]{1,0:T(8,128)(2,1)S(1)}) custom-call(bf16[2,1024,896]{2,1,0:T(8,128)(2,1)S(1)} %stage_down.1.w, bf16[192,256]{1,0:T(8,128)(2,1)S(1)} %hidden.3.refs_0_, bf16[192,256]{1,0:T(8,128)(2,1)S(1)} %collective-permute-done.19.refs_1_, ...), custom_call_target="tpu_custom_call" | custom-call | flops 352321536 | bytes 3670016 | tf_op jit(solution)/shard_map/down/pallas_call | solution.py:397
  50.4 0.5 collective-permute-start.22
  50.9 1.7 %collective-permute-start.9 = (bf16[48,896]{1,0:T(8,128)(2,1)S(1)}, bf16[48,896]{1,0:T(8,128)(2,1)S(1)}, u32[]{:S(2)}, u32[]{:S(2)}) collective-permute-start(bf16[48,896]{1,0:T(8,128)(2,1)S(1)} %get-tuple-element.48), channel_id=1, source_target_pairs={{0,4},{1,5},{2,6},{3,7},{4,0},{5,1},{6,2},{7,3},{8,12},{9,13},{10,... | collective-permute-start | bytes 258056 | tf_op jit(solution)/shard_map/ppermute | solution.py:281
  52.7 0.6 collective-permute-done.10.refs_3_
  53.3 2.3 %collective-permute-start.24 = (bf16[48,896]{1,0:T(8,128)(2,1)S(1)}, bf16[48,896]{1,0:T(8,128)(2,1)S(1)}, u32[]{:S(2)}, u32[]{:S(2)}) collective-permute-start(bf16[48,896]{1,0:T(8,128)(2,1)S(1)} %get-tuple-element.63), channel_id=1, source_target_pairs={{0,6},{1,7},{2,4},{3,5},{4,2},{5,3},{6,0},{7,1},{8,14},{9,15},{10,... | collective-permute-start | bytes 258056 | tf_op jit(solution)/shard_map/ppermute | solution.py:281
  55.6 1.3 %collective-permute-start.25 = (bf16[48,896]{1,0:T(8,128)(2,1)S(1)}, bf16[48,896]{1,0:T(8,128)(2,1)S(1)}, u32[]{:S(2)}, u32[]{:S(2)}) collective-permute-start(bf16[48,896]{1,0:T(8,128)(2,1)S(1)} %get-tuple-element.64), channel_id=1, source_target_pairs={{0,7},{1,6},{2,5},{3,4},{4,3},{5,2},{6,1},{7,0},{8,15},{9,14},{10,... | collective-permute-start | bytes 258056 | tf_op jit(solution)/shard_map/ppermute | solution.py:281
  56.9 1.7 %weigh.1 = (bf16[128,192]{1,0:T(8,128)(2,1)S(1)}, bf16[128,192]{1,0:T(8,128)(2,1)S(1)}, bf16[128,192]{1,0:T(8,128)(2,1)S(1)}, bf16[128,192]{1,0:T(8,128)(2,1)S(1)}) custom-call(s32[2,4]{1,0:T(2,128)} %bitcast.11, s32[12]{0:T(128)} %cap_in.3, s32[8,128]{1,0:T(8,128)} %bitcast.5, s32[8,128]{1,0:T(8,128)} %bitcast.7, f32[8,128]{1,0:T(8,128)} %bitcast.12), custom_call_target="tpu_custom_call" | custom-call | tf_op jit(solution)/shard_map/weigh/pallas_call | solution.py:326
  59.0 2.7 %collective-permute-done.24.refs_5_ = bf16[48,896]{1,0:T(8,128)(2,1)S(1)} collective-permute-done((bf16[48,896]{1,0:T(8,128)(2,1)S(1)}, bf16[48,896]{1,0:T(8,128)(2,1)S(1)}, u32[]{:S(2)}, u32[]{:S(2)}) %collective-permute-start.24) | collective-permute-done | bytes 86048 | tf_op jit(solution)/shard_map/ppermute | solution.py:281
  61.7 0.5 collective-permute-done.25.refs_6_
  62.2 1.0 %combine.3 = bf16[128,896]{1,0:T(8,128)(2,1)} custom-call(f32[128,896]{1,0:T(8,128)S(1)} %combine.2.refs_0_, bf16[128,192]{1,0:T(8,128)(2,1)S(1)} %get-tuple-element.52.refs_1_, bf16[128,192]{1,0:T(8,128)(2,1)S(1)} %get-tuple-element.53.refs_2_, bf16[48,896]{1,0:T(8,128)(2,1)S(1)} %collective-permute-done.22.refs_3_, ...), custom_call_target="tpu_custom_call" | custom-call | tf_op jit(solution)/shard_map/combine/pallas_call | solution.py:413
  (38 shorter events, 5.8 us)
Async XLA Ops:
  2.1 10.7 %collective-permute-start = (bf16[48,896]{1,0:T(8,128)(2,1)S(1)}, bf16[48,896]{1,0:T(8,128)(2,1)S(1)}, u32[]{:S(2)}, u32[]{:S(2)}) collective-permute-start(bf16[48,896]{1,0:T(8,128)(2,1)S(1)} %get-tuple-element.37), channel_id=1, source_target_pairs={{0,4},{1,5},{2,6},{3,7},{4,0},{5,1},{6,2},{7,3},{8,12},{9,13},{10,... | collective-permute-start | bytes 258056 | tf_op jit(solution)/shard_map/ppermute | solution.py:281
  6.2 10.0 %collective-permute-start.1 = (bf16[48,896]{1,0:T(8,128)(2,1)S(1)}, bf16[48,896]{1,0:T(8,128)(2,1)S(1)}, u32[]{:S(2)}, u32[]{:S(2)}) collective-permute-start(bf16[48,896]{1,0:T(8,128)(2,1)S(1)} %get-tuple-element.38), channel_id=1, source_target_pairs={{0,5},{1,4},{2,7},{3,6},{4,1},{5,0},{6,3},{7,2},{8,13},{9,12},{10,... | collective-permute-start | bytes 258056 | tf_op jit(solution)/shard_map/ppermute | solution.py:281
  6.2 11.3 %collective-permute-start.2 = (bf16[48,896]{1,0:T(8,128)(2,1)S(1)}, bf16[48,896]{1,0:T(8,128)(2,1)S(1)}, u32[]{:S(2)}, u32[]{:S(2)}) collective-permute-start(bf16[48,896]{1,0:T(8,128)(2,1)S(1)} %get-tuple-element.39), channel_id=1, source_target_pairs={{0,1},{1,0},{2,3},{3,2},{4,5},{5,4},{6,7},{7,6},{8,9},{9,8},{10,11... | collective-permute-start | bytes 258056 | tf_op jit(solution)/shard_map/ppermute | solution.py:281
  6.4 14.0 %collective-permute-start.12 = (bf16[48,896]{1,0:T(8,128)(2,1)S(1)}, bf16[48,896]{1,0:T(8,128)(2,1)S(1)}, u32[]{:S(2)}, u32[]{:S(2)}) collective-permute-start(bf16[48,896]{1,0:T(8,128)(2,1)S(1)} %get-tuple-element.54), channel_id=1, source_target_pairs={{0,2},{1,3},{2,0},{3,1},{4,6},{5,7},{6,4},{7,5},{8,10},{9,11},{10,... | collective-permute-start | bytes 258056 | tf_op jit(solution)/shard_map/ppermute | solution.py:281
  8.3 13.7 %collective-permute-start.13 = (bf16[48,896]{1,0:T(8,128)(2,1)S(1)}, bf16[48,896]{1,0:T(8,128)(2,1)S(1)}, u32[]{:S(2)}, u32[]{:S(2)}) collective-permute-start(bf16[48,896]{1,0:T(8,128)(2,1)S(1)} %get-tuple-element.55), channel_id=1, source_target_pairs={{0,3},{1,2},{2,1},{3,0},{4,7},{5,6},{6,5},{7,4},{8,11},{9,10},{10,... | collective-permute-start | bytes 258056 | tf_op jit(solution)/shard_map/ppermute | solution.py:281
  12.8 9.6 %collective-permute-start.14 = (bf16[48,896]{1,0:T(8,128)(2,1)S(1)}, bf16[48,896]{1,0:T(8,128)(2,1)S(1)}, u32[]{:S(2)}, u32[]{:S(2)}) collective-permute-start(bf16[48,896]{1,0:T(8,128)(2,1)S(1)} %get-tuple-element.56), channel_id=1, source_target_pairs={{0,6},{1,7},{2,4},{3,5},{4,2},{5,3},{6,0},{7,1},{8,14},{9,15},{10,... | collective-permute-start | bytes 258056 | tf_op jit(solution)/shard_map/ppermute | solution.py:281
  16.2 6.5 %collective-permute-start.15 = (bf16[48,896]{1,0:T(8,128)(2,1)S(1)}, bf16[48,896]{1,0:T(8,128)(2,1)S(1)}, u32[]{:S(2)}, u32[]{:S(2)}) collective-permute-start(bf16[48,896]{1,0:T(8,128)(2,1)S(1)} %get-tuple-element.57), channel_id=1, source_target_pairs={{0,7},{1,6},{2,5},{3,4},{4,3},{5,2},{6,1},{7,0},{8,15},{9,14},{10,... | collective-permute-start | bytes 258056 | tf_op jit(solution)/shard_map/ppermute | solution.py:281
  18.4 8.7 %collective-permute-start.4 = (bf16[192,512]{1,0:T(8,128)(2,1)S(1)}, bf16[192,512]{1,0:T(8,128)(2,1)S(1)}, u32[]{:S(2)}, u32[]{:S(2)}) collective-permute-start(bf16[192,512]{1,0:T(8,128)(2,1)S(1)} %up.11), channel_id=1, source_target_pairs={{0,16},{8,24},{16,0},{24,8},{1,17},{9,25},{17,1},{25,9},{2,18},{10... | collective-permute-start | bytes 589832 | tf_op jit(solution)/shard_map/ppermute | solution.py:385
  20.4 8.2 %collective-permute-start.3 = (bf16[192,512]{1,0:T(8,128)(2,1)S(1)}, bf16[192,512]{1,0:T(8,128)(2,1)S(1)}, u32[]{:S(2)}, u32[]{:S(2)}) collective-permute-start(bf16[192,512]{1,0:T(8,128)(2,1)S(1)} %up.10), channel_id=1, source_target_pairs={{0,8},{8,0},{16,24},{24,16},{1,9},{9,1},{17,25},{25,17},{2,10},{10... | collective-permute-start | bytes 589832 | tf_op jit(solution)/shard_map/ppermute | solution.py:385
  22.0 10.5 %collective-permute-start.5 = (bf16[192,512]{1,0:T(8,128)(2,1)S(1)}, bf16[192,512]{1,0:T(8,128)(2,1)S(1)}, u32[]{:S(2)}, u32[]{:S(2)}) collective-permute-start(bf16[192,512]{1,0:T(8,128)(2,1)S(1)} %get-tuple-element.47), channel_id=1, source_target_pairs={{0,24},{8,16},{16,8},{24,0},{1,25},{9,17},{17,9},{25,1},{2,26},{10... | collective-permute-start | bytes 589832 | tf_op jit(solution)/shard_map/ppermute | solution.py:385
  23.5 12.1 %collective-permute-start.17 = (bf16[192,512]{1,0:T(8,128)(2,1)S(1)}, bf16[192,512]{1,0:T(8,128)(2,1)S(1)}, u32[]{:S(2)}, u32[]{:S(2)}) collective-permute-start(bf16[192,512]{1,0:T(8,128)(2,1)S(1)} %up.15), channel_id=1, source_target_pairs={{0,16},{8,24},{16,0},{24,8},{1,17},{9,25},{17,1},{25,9},{2,18},{10... | collective-permute-start | bytes 589832 | tf_op jit(solution)/shard_map/ppermute | solution.py:385
  25.5 12.1 %collective-permute-start.16 = (bf16[192,512]{1,0:T(8,128)(2,1)S(1)}, bf16[192,512]{1,0:T(8,128)(2,1)S(1)}, u32[]{:S(2)}, u32[]{:S(2)}) collective-permute-start(bf16[192,512]{1,0:T(8,128)(2,1)S(1)} %up.14), channel_id=1, source_target_pairs={{0,8},{8,0},{16,24},{24,16},{1,9},{9,1},{17,25},{25,17},{2,10},{10... | collective-permute-start | bytes 589832 | tf_op jit(solution)/shard_map/ppermute | solution.py:385
  27.1 13.8 %collective-permute-start.18 = (bf16[192,512]{1,0:T(8,128)(2,1)S(1)}, bf16[192,512]{1,0:T(8,128)(2,1)S(1)}, u32[]{:S(2)}, u32[]{:S(2)}) collective-permute-start(bf16[192,512]{1,0:T(8,128)(2,1)S(1)} %get-tuple-element.60), channel_id=1, source_target_pairs={{0,24},{8,16},{16,8},{24,0},{1,25},{9,17},{17,9},{25,1},{2,26},{10... | collective-permute-start | bytes 589832 | tf_op jit(solution)/shard_map/ppermute | solution.py:385
  32.6 11.6 %collective-permute-start.6 = (bf16[192,256]{1,0:T(8,128)(2,1)S(1)}, bf16[192,256]{1,0:T(8,128)(2,1)S(1)}, u32[]{:S(2)}, u32[]{:S(2)}) collective-permute-start(bf16[192,256]{1,0:T(8,128)(2,1)S(1)} %hidden.2.refs_0_), channel_id=1, source_target_pairs={{0,8},{8,0},{16,24},{24,16},{1,9},{9,1},{17,25},{25,17},{2,10},{10... | collective-permute-start | bytes 294920 | tf_op jit(solution)/shard_map/ppermute | solution.py:396
  34.1 12.8 %collective-permute-start.7 = (bf16[192,256]{1,0:T(8,128)(2,1)S(1)}, bf16[192,256]{1,0:T(8,128)(2,1)S(1)}, u32[]{:S(2)}, u32[]{:S(2)}) collective-permute-start(bf16[192,256]{1,0:T(8,128)(2,1)S(1)} %hidden.2.refs_0_), channel_id=1, source_target_pairs={{0,16},{8,24},{16,0},{24,8},{1,17},{9,25},{17,1},{25,9},{2,18},{10... | collective-permute-start | bytes 294920 | tf_op jit(solution)/shard_map/ppermute | solution.py:396
  35.7 11.3 %collective-permute-start.8 = (bf16[192,256]{1,0:T(8,128)(2,1)S(1)}, bf16[192,256]{1,0:T(8,128)(2,1)S(1)}, u32[]{:S(2)}, u32[]{:S(2)}) collective-permute-start(bf16[192,256]{1,0:T(8,128)(2,1)S(1)} %hidden.2.refs_0_), channel_id=1, source_target_pairs={{0,24},{8,16},{16,8},{24,0},{1,25},{9,17},{17,9},{25,1},{2,26},{10... | collective-permute-start | bytes 294920 | tf_op jit(solution)/shard_map/ppermute | solution.py:396
  41.0 6.8 %collective-permute-start.19 = (bf16[192,256]{1,0:T(8,128)(2,1)S(1)}, bf16[192,256]{1,0:T(8,128)(2,1)S(1)}, u32[]{:S(2)}, u32[]{:S(2)}) collective-permute-start(bf16[192,256]{1,0:T(8,128)(2,1)S(1)} %hidden.3.refs_0_), channel_id=1, source_target_pairs={{0,8},{8,0},{16,24},{24,16},{1,9},{9,1},{17,25},{25,17},{2,10},{10... | collective-permute-start | bytes 294920 | tf_op jit(solution)/shard_map/ppermute | solution.py:396
  42.6 5.5 %collective-permute-start.20 = (bf16[192,256]{1,0:T(8,128)(2,1)S(1)}, bf16[192,256]{1,0:T(8,128)(2,1)S(1)}, u32[]{:S(2)}, u32[]{:S(2)}) collective-permute-start(bf16[192,256]{1,0:T(8,128)(2,1)S(1)} %hidden.3.refs_0_), channel_id=1, source_target_pairs={{0,16},{8,24},{16,0},{24,8},{1,17},{9,25},{17,1},{25,9},{2,18},{10... | collective-permute-start | bytes 294920 | tf_op jit(solution)/shard_map/ppermute | solution.py:396
  44.1 5.5 %collective-permute-start.21 = (bf16[192,256]{1,0:T(8,128)(2,1)S(1)}, bf16[192,256]{1,0:T(8,128)(2,1)S(1)}, u32[]{:S(2)}, u32[]{:S(2)}) collective-permute-start(bf16[192,256]{1,0:T(8,128)(2,1)S(1)} %hidden.3.refs_0_), channel_id=1, source_target_pairs={{0,24},{8,16},{16,8},{24,0},{1,25},{9,17},{17,9},{25,1},{2,26},{10... | collective-permute-start | bytes 294920 | tf_op jit(solution)/shard_map/ppermute | solution.py:396
  47.7 5.6 %collective-permute-start.10 = (bf16[48,896]{1,0:T(8,128)(2,1)S(1)}, bf16[48,896]{1,0:T(8,128)(2,1)S(1)}, u32[]{:S(2)}, u32[]{:S(2)}) collective-permute-start(bf16[48,896]{1,0:T(8,128)(2,1)S(1)} %get-tuple-element.49), channel_id=1, source_target_pairs={{0,5},{1,4},{2,7},{3,6},{4,1},{5,0},{6,3},{7,2},{8,13},{9,12},{10,... | collective-permute-start | bytes 258056 | tf_op jit(solution)/shard_map/ppermute | solution.py:281
  47.8 7.8 %collective-permute-start.11 = (bf16[48,896]{1,0:T(8,128)(2,1)S(1)}, bf16[48,896]{1,0:T(8,128)(2,1)S(1)}, u32[]{:S(2)}, u32[]{:S(2)}) collective-permute-start(bf16[48,896]{1,0:T(8,128)(2,1)S(1)} %get-tuple-element.50), channel_id=1, source_target_pairs={{0,1},{1,0},{2,3},{3,2},{4,5},{5,4},{6,7},{7,6},{8,9},{9,8},{10,11... | collective-permute-start | bytes 258056 | tf_op jit(solution)/shard_map/ppermute | solution.py:281
  50.4 8.6 %collective-permute-start.22 = (bf16[48,896]{1,0:T(8,128)(2,1)S(1)}, bf16[48,896]{1,0:T(8,128)(2,1)S(1)}, u32[]{:S(2)}, u32[]{:S(2)}) collective-permute-start(bf16[48,896]{1,0:T(8,128)(2,1)S(1)} %get-tuple-element.61), channel_id=1, source_target_pairs={{0,2},{1,3},{2,0},{3,1},{4,6},{5,7},{6,4},{7,5},{8,10},{9,11},{10,... | collective-permute-start | bytes 258056 | tf_op jit(solution)/shard_map/ppermute | solution.py:281
  50.9 7.7 %collective-permute-start.9 = (bf16[48,896]{1,0:T(8,128)(2,1)S(1)}, bf16[48,896]{1,0:T(8,128)(2,1)S(1)}, u32[]{:S(2)}, u32[]{:S(2)}) collective-permute-start(bf16[48,896]{1,0:T(8,128)(2,1)S(1)} %get-tuple-element.48), channel_id=1, source_target_pairs={{0,4},{1,5},{2,6},{3,7},{4,0},{5,1},{6,2},{7,3},{8,12},{9,13},{10,... | collective-permute-start | bytes 258056 | tf_op jit(solution)/shard_map/ppermute | solution.py:281
  52.7 6.3 %collective-permute-start.23 = (bf16[48,896]{1,0:T(8,128)(2,1)S(1)}, bf16[48,896]{1,0:T(8,128)(2,1)S(1)}, u32[]{:S(2)}, u32[]{:S(2)}) collective-permute-start(bf16[48,896]{1,0:T(8,128)(2,1)S(1)} %get-tuple-element.62), channel_id=1, source_target_pairs={{0,3},{1,2},{2,1},{3,0},{4,7},{5,6},{6,5},{7,4},{8,11},{9,10},{10,... | collective-permute-start | bytes 258056 | tf_op jit(solution)/shard_map/ppermute | solution.py:281
  53.3 8.4 %collective-permute-start.24 = (bf16[48,896]{1,0:T(8,128)(2,1)S(1)}, bf16[48,896]{1,0:T(8,128)(2,1)S(1)}, u32[]{:S(2)}, u32[]{:S(2)}) collective-permute-start(bf16[48,896]{1,0:T(8,128)(2,1)S(1)} %get-tuple-element.63), channel_id=1, source_target_pairs={{0,6},{1,7},{2,4},{3,5},{4,2},{5,3},{6,0},{7,1},{8,14},{9,15},{10,... | collective-permute-start | bytes 258056 | tf_op jit(solution)/shard_map/ppermute | solution.py:281
  55.6 6.6 %collective-permute-start.25 = (bf16[48,896]{1,0:T(8,128)(2,1)S(1)}, bf16[48,896]{1,0:T(8,128)(2,1)S(1)}, u32[]{:S(2)}, u32[]{:S(2)}) collective-permute-start(bf16[48,896]{1,0:T(8,128)(2,1)S(1)} %get-tuple-element.64), channel_id=1, source_target_pairs={{0,7},{1,6},{2,5},{3,4},{4,3},{5,2},{6,1},{7,0},{8,15},{9,14},{10,... | collective-permute-start | bytes 258056 | tf_op jit(solution)/shard_map/ppermute | solution.py:281

commit v2 on v1

--- a/solution.py
+++ b/solution.py
@@ -44,24 +44,22 @@
 def slots_of(sizes, place, cap, ids_ref, choice_ref):
     experts, hot = sizes[:2]
     top, count = ids_ref.shape
-    key = (ids_ref[...] + experts * choice_ref[...]).astype(F32).T
-    lane = lax.broadcasted_iota(I32, (count, 2 * experts), 1).astype(F32)
-    hits = [key[:, k : k + 1] == lane for k in range(top)]
-    member = jnp.zeros((count, 2 * experts), F32)
-    for hit in hits:
-        member = jnp.where(hit, 1.0, member)
-    earlier = lax.broadcasted_iota(I32, (count, count), 1) < lax.broadcasted_iota(
-        I32, (count, count), 0
+    key = ids_ref[...] + experts * choice_ref[...]
+    row = lax.broadcasted_iota(I32, (2 * experts, count), 0)
+    hits = [key[k : k + 1] == row for k in range(top)]
+    member = functools.reduce(jnp.logical_or, hits)
+    later = lax.broadcasted_iota(I32, (count, count), 0) < lax.broadcasted_iota(
+        I32, (count, count), 1
     )
-    rank = dot(jnp.where(earlier, 1.0, 0.0).astype(BF16), member.astype(BF16))
-    lane_row = lax.broadcasted_iota(I32, (1, 2 * experts), 1)
-    limit = jnp.zeros((1, 2 * experts), I32)
+    rank = dot(jnp.where(member, 1.0, 0.0).astype(BF16), jnp.where(later, 1.0, 0.0).astype(BF16))
+    row_one = lax.broadcasted_iota(I32, (2 * experts, 1), 0)
+    limit = jnp.zeros((2 * experts, 1), I32)
     for e in range(experts):
-        limit = jnp.where(lane_row == e, cap[e], limit)
+        limit = jnp.where(row_one == e, cap[e], limit)
     for j in range(hot):
-        limit = jnp.where(lane_row == place[0, j] + experts, cap[experts + j], limit)
-    kept = (member > 0.5) & (rank < limit.astype(F32))
-    return jnp.where(kept, rank, -1.0).astype(BF16), hits
+        limit = jnp.where(row_one == place[0, j] + experts, cap[experts + j], limit)
+    kept = member & (rank < limit.astype(F32))
+    return jnp.where(kept, rank, -1.0), hits
 
 
 def columns_of(sizes, place, chunk):
@@ -91,7 +89,7 @@
     place_rank = jnp.where(wanted >= 0, place_rank, -2.0)
     spread = jnp.where(
         lax.broadcasted_iota(I32, (2 * experts, columns), 0) == wanted, 1.0, 0.0
-    ).astype(BF16)
+    )
     return spread, place_rank
 
 
@@ -119,18 +117,17 @@
     )
     for copy in copies[:4]:
         copy.wait()
+    spread, place_rank = columns_of(sizes, place, sum(chunks, ()))
+    replicas = spread.shape[0]
+    turned = jnp.concatenate([spread, jnp.broadcast_to(place_rank, (8, place_rank.shape[1]))]).T
     rank, _ = slots_of(sizes, place, cap, ids_ref, choice_ref)
+    slot = dot(turned[:, :replicas].astype(BF16), rank.astype(BF16))
+    picks = jnp.where(slot == turned[:, replicas : replicas + 1], 1.0, 0.0).astype(BF16)
+    copies[4].wait()
+    rows = dot(picks, tok_ref[...]).astype(BF16)
     per = pieces[0].shape[0]
-    done = 0
-    for chunk in chunks:
-        spread, place_rank = columns_of(sizes, place, chunk)
-        picks = jnp.where(dot(rank, spread) == place_rank, 1.0, 0.0).T.astype(BF16)
-        if not done:
-            copies[4].wait()
-        rows = dot(picks, tok_ref[...]).astype(BF16)
-        for i in range(len(chunk)):
-            pieces[done + i][...] = rows[i * per : (i + 1) * per]
-        done += len(chunk)
+    for i, piece in enumerate(pieces):
+        piece[...] = rows[i * per : (i + 1) * per]
 
 
 def weigh_kernel(sizes, chunks, place_in, cap_in, ids_in, choice_in, gate_in, *refs):
@@ -149,14 +146,15 @@
     for copy in copies:
         copy.wait()
     rank, hits = slots_of(sizes, place, cap, ids_ref, choice_ref)
-    gate = gate_ref[...].T
     weight = jnp.zeros(rank.shape, F32)
     for k, hit in enumerate(hits):
-        weight = jnp.where(hit, gate[:, k : k + 1], weight)
+        weight = jnp.where(hit, gate_ref[k : k + 1], weight)
+    weight, rank = weight.T, rank.T.astype(BF16)
     weight_high = weight.astype(BF16)
     weight_low = (weight - weight_high.astype(F32)).astype(BF16)
     for c, chunk in enumerate(chunks):
         spread, place_rank = columns_of(sizes, place, chunk)
+        spread = spread.astype(BF16)
         chosen = dot(rank, spread) == place_rank
         for part, out in zip((weight_high, weight_low), mats[2 * c : 2 * c + 2]):
             out[...] = jnp.where(chosen, dot(part, spread), 0.0).astype(BF16)
@@ -192,7 +190,7 @@
 
     def moves(which, i):
         for k, out in enumerate(outs):
-            q = lax.axis_index("dp") ^ k
+            q = lax.axis_index("dp") ^ role(k, len(outs), lax.axis_index("expert"))
             columns = pl.ds(pl.multiple_of(q * block, block), block)
             for g, w in enumerate((w_gate, w_up)):
                 yield w.at[0, which, :, columns], out.at[i, :, pl.ds(g * block, block)]
@@ -205,7 +203,7 @@
 
     def moves(which, i):
         for k in range(parts):
-            q = lax.axis_index("dp") ^ k
+            q = lax.axis_index("dp") ^ role(k, parts, lax.axis_index("expert"))
             units = pl.ds(pl.multiple_of(q * block, block), block)
             yield w_down.at[0, which, units], out.at[i, pl.ds(k * block, block)]
 
@@ -269,6 +267,22 @@
 
 def flips(n, j):
     return [(i, i ^ j) for i in range(n)]
+
+
+def role(k, parts, expert):
+    if parts != 4 or k not in (1, 2):
+        return k
+    return k + (3 - 2 * k) * (expert % 2)
+
+
+def to_partner(x, k):
+    parts, experts = lax.axis_size("dp"), lax.axis_size("expert")
+    pairs = [
+        (p * experts + e, (p ^ role(k, parts, e)) * experts + e)
+        for p in range(parts)
+        for e in range(experts)
+    ]
+    return lax.ppermute(x, ("dp", "expert"), pairs)
 
 
 def exchange(pieces, chunks, axis):
@@ -382,7 +396,7 @@
             if not i:
                 xa, xb = made[1:]
             if k:
-                sums[k] = lax.ppermute(sums[k], "dp", flips(parts, k))
+                sums[k] = to_partner(sums[k], k)
         hidden = pl.pallas_call(
             hidden_kernel,
             out_shape=sds((rows, block), BF16),
@@ -393,7 +407,7 @@
         )(*[sums[k] for k in range(parts)])
         spread = {0: hidden}
         for k in order[:-1]:
-            spread[k] = lax.ppermute(hidden, "dp", flips(parts, k))
+            spread[k] = to_partner(hidden, k)
         results += pl.pallas_call(
             functools.partial(down_kernel, (parts, blocks, room_a, room_b)),
             out_shape=[sds((per, cols), BF16)] * blocks,

time: 64 us -> 63.8 us (level)
  starting transfers between devices: 32.9 us -> 37.9 us
  waiting for transfers between devices: 14 us -> 10.5 us
  Pallas kernels: 16 us -> 15.1 us
    ppermute x12, waiting for transfers between devices: 8.92 us -> 3.76 us  [to_partner(): return lax.ppermute(x, ('dp', 'expert'), pairs)]
    ppermute x12, starting transfers between devices: 16 us -> 20.5 us  [to_partner(): return lax.ppermute(x, ('dp', 'expert'), pairs)]
    ppermute x14, waiting for transfers between devices: 5.12 us -> 6.7 us  [exchange(): moved.append(lax.ppermute(piece, axis, flips(n, j)) if j else piece)]
  transfers between devices with their start and end apart: 26 -> 26, of which waited for: 9 -> 10; matrix products, arithmetic and copies ran while one was open for 0% -> 0% of each run, Pallas kernels for 20% -> 20%
where the time goes in v2:
time: 63.8 us; the launch traced here: 63.6 us
  starting transfers between devices  37.9 us (59%)
  Pallas kernels  15.1 us (24%)
  waiting for transfers between devices  10.5 us (16%)
    ppermute x12, starting transfers between devices, to_partner(): return lax.ppermute(x, ('dp', 'expert'), pairs)  20.5 us
    ppermute x14, starting transfers between devices, exchange(): moved.append(lax.ppermute(piece, axis, flips(n, j)) if j else piece)  17.4 us
    ppermute x14, waiting for transfers between devices, exchange(): moved.append(lax.ppermute(piece, axis, flips(n, j)) if j else piece)  6.7 us
    ppermute x12, waiting for transfers between devices, to_partner(): return lax.ppermute(x, ('dp', 'expert'), pairs)  3.76 us
    pallas_call x1, Pallas kernels, on_device(): pl.pallas_call(stage_kernel, out_shape=[sds((2, cols, 2 * block), BF16)]...  3.49 us
    pallas_call x8, Pallas kernels, on_device(): pl.pallas_call(up_next_kernel if i else functools.partial(up_first_kernel...  3.43 us
    pallas_call x1, Pallas kernels, on_device(): pl.pallas_call(functools.partial(stage_down_kernel, parts), out_shape=sds...  2.34 us
    pallas_call x1, Pallas kernels, on_device(): pl.pallas_call(functools.partial(route_kernel, sizes, chunks), out_shape=...  1.57 us
  transfers between devices with their start and end apart: 26, of which 10 were waited for; matrix products, arithmetic and copies ran while one was open for 0% of the time, Pallas kernels for 20%

profile of v2, /device:TPU:0, one launch (start us, length us, event | category | flops | bytes accessed | tf_op | source)
XLA Modules:
  0.0 63.6 jit_solution(3513420959534789592)
XLA Ops:
  0.0 1.6 %route.1 = (bf16[48,896]{1,0:T(8,128)(2,1)S(1)}, bf16[48,896]{1,0:T(8,128)(2,1)S(1)}, bf16[48,896]{1,0:T(8,128)(2,1)S(1)}, bf16[48,896]{1,0:T(8,128)(2,1)S(1)}, ...) custom-call(s32[2,4]{1,0:T(2,128)} %bitcast.8, ...), custom_call_target="tpu_custom_call" | custom-call | tf_op jit(solution)/shard_map/route/pallas_call | solution.py:329
  1.6 4.1 %collective-permute-start = (bf16[48,896]{1,0:T(8,128)(2,1)S(1)}, bf16[48,896]{1,0:T(8,128)(2,1)S(1)}, u32[]{:S(2)}, u32[]{:S(2)}) collective-permute-start(bf16[48,896]{1,0:T(8,128)(2,1)S(1)} %get-tuple-element.37), channel_id=1, source_target_pairs={{0,4},{1,5},{2,6},{3,7},{4,0},{5,1},{6,2},{7,3},{8,12},{9,13},{10,... | collective-permute-start | bytes 258056 | tf_op jit(solution)/shard_map/ppermute | solution.py:295
  5.9 1.8 %collective-permute-start.12 = (bf16[48,896]{1,0:T(8,128)(2,1)S(1)}, bf16[48,896]{1,0:T(8,128)(2,1)S(1)}, u32[]{:S(2)}, u32[]{:S(2)}) collective-permute-start(bf16[48,896]{1,0:T(8,128)(2,1)S(1)} %get-tuple-element.54), channel_id=1, source_target_pairs={{0,2},{1,3},{2,0},{3,1},{4,6},{5,7},{6,4},{7,5},{8,10},{9,11},{10,... | collective-permute-start | bytes 258056 | tf_op jit(solution)/shard_map/ppermute | solution.py:295
  7.7 3.5 %stage.1 = (bf16[2,896,512]{2,1,0:T(8,128)(2,1)S(1)}, bf16[2,896,512]{2,1,0:T(8,128)(2,1)S(1)}, bf16[2,896,512]{2,1,0:T(8,128)(2,1)S(1)}, bf16[2,896,512]{2,1,0:T(8,128)(2,1)S(1)}) custom-call(s32[2,4]{1,0:T(2,128)} %bitcast.9, bf16[1,2,896,1024]{3,2,1,0:T(8,128)(2,1)} %w_gate.1, bf16[1,2,896,1024]{3,2,1,0:T(8,128)(2,1)} %w_up.1), custom_call_target="tpu_custom_call" | custom-call | bytes 14680064 | tf_op jit(solution)/shard_map/stage/pallas_call | solution.py:354
  11.2 1.1 %collective-permute-done.refs_0_ = bf16[48,896]{1,0:T(8,128)(2,1)S(1)} collective-permute-done((bf16[48,896]{1,0:T(8,128)(2,1)S(1)}, bf16[48,896]{1,0:T(8,128)(2,1)S(1)}, u32[]{:S(2)}, u32[]{:S(2)}) %collective-permute-start) | collective-permute-done | bytes 86048 | tf_op jit(solution)/shard_map/ppermute | solution.py:295
  12.3 3.3 %collective-permute-start.14 = (bf16[48,896]{1,0:T(8,128)(2,1)S(1)}, bf16[48,896]{1,0:T(8,128)(2,1)S(1)}, u32[]{:S(2)}, u32[]{:S(2)}) collective-permute-start(bf16[48,896]{1,0:T(8,128)(2,1)S(1)} %get-tuple-element.56), channel_id=1, source_target_pairs={{0,6},{1,7},{2,4},{3,5},{4,2},{5,3},{6,0},{7,1},{8,14},{9,15},{10,... | collective-permute-start | bytes 258056 | tf_op jit(solution)/shard_map/ppermute | solution.py:295
  15.7 1.3 %collective-permute-start.15 = (bf16[48,896]{1,0:T(8,128)(2,1)S(1)}, bf16[48,896]{1,0:T(8,128)(2,1)S(1)}, u32[]{:S(2)}, u32[]{:S(2)}) collective-permute-start(bf16[48,896]{1,0:T(8,128)(2,1)S(1)} %get-tuple-element.57), channel_id=1, source_target_pairs={{0,7},{1,6},{2,5},{3,4},{4,3},{5,2},{6,1},{7,0},{8,15},{9,14},{10,... | collective-permute-start | bytes 258056 | tf_op jit(solution)/shard_map/ppermute | solution.py:295
  17.9 1.6 %collective-permute-start.4 = (bf16[192,512]{1,0:T(8,128)(2,1)S(1)}, bf16[192,512]{1,0:T(8,128)(2,1)S(1)}, u32[]{:S(2)}, u32[]{:S(2)}) collective-permute-start(bf16[192,512]{1,0:T(8,128)(2,1)S(1)} %up.11), channel_id=1, source_target_pairs={{0,16},{1,9},{2,18},{3,11},{4,20},{5,13},{6,22},{7,15},{8,24},{9,1... | collective-permute-start | bytes 589832 | tf_op jit(solution)/shard_map/ppermute | solution.py:285
  19.9 1.6 %collective-permute-start.3 = (bf16[192,512]{1,0:T(8,128)(2,1)S(1)}, bf16[192,512]{1,0:T(8,128)(2,1)S(1)}, u32[]{:S(2)}, u32[]{:S(2)}) collective-permute-start(bf16[192,512]{1,0:T(8,128)(2,1)S(1)} %up.10), channel_id=1, source_target_pairs={{0,8},{1,17},{2,10},{3,19},{4,12},{5,21},{6,14},{7,23},{8,0},{9,25... | collective-permute-start | bytes 589832 | tf_op jit(solution)/shard_map/ppermute | solution.py:285
  23.0 1.6 %collective-permute-start.17 = (bf16[192,512]{1,0:T(8,128)(2,1)S(1)}, bf16[192,512]{1,0:T(8,128)(2,1)S(1)}, u32[]{:S(2)}, u32[]{:S(2)}) collective-permute-start(bf16[192,512]{1,0:T(8,128)(2,1)S(1)} %up.15), channel_id=1, source_target_pairs={{0,16},{1,9},{2,18},{3,11},{4,20},{5,13},{6,22},{7,15},{8,24},{9,1... | collective-permute-start | bytes 589832 | tf_op jit(solution)/shard_map/ppermute | solution.py:285
  25.0 1.6 %collective-permute-start.16 = (bf16[192,512]{1,0:T(8,128)(2,1)S(1)}, bf16[192,512]{1,0:T(8,128)(2,1)S(1)}, u32[]{:S(2)}, u32[]{:S(2)}) collective-permute-start(bf16[192,512]{1,0:T(8,128)(2,1)S(1)} %up.14), channel_id=1, source_target_pairs={{0,8},{1,17},{2,10},{3,19},{4,12},{5,21},{6,14},{7,23},{8,0},{9,25... | collective-permute-start | bytes 589832 | tf_op jit(solution)/shard_map/ppermute | solution.py:285
  26.6 3.4 %collective-permute-start.18 = (bf16[192,512]{1,0:T(8,128)(2,1)S(1)}, bf16[192,512]{1,0:T(8,128)(2,1)S(1)}, u32[]{:S(2)}, u32[]{:S(2)}) collective-permute-start(bf16[192,512]{1,0:T(8,128)(2,1)S(1)} %get-tuple-element.60), channel_id=1, source_target_pairs={{0,24},{1,25},{2,26},{3,27},{4,28},{5,29},{6,30},{7,31},{8,16},{9,... | collective-permute-start | bytes 589832 | tf_op jit(solution)/shard_map/ppermute | solution.py:285
  30.4 1.3 %collective-permute-done.5.refs_2_ = bf16[192,512]{1,0:T(8,128)(2,1)S(1)} collective-permute-done((bf16[192,512]{1,0:T(8,128)(2,1)S(1)}, bf16[192,512]{1,0:T(8,128)(2,1)S(1)}, u32[]{:S(2)}, u32[]{:S(2)}) %collective-permute-start.5) | collective-permute-done | bytes 196640 | tf_op jit(solution)/shard_map/ppermute | solution.py:285
  31.8 1.8 %collective-permute-start.6 = (bf16[192,256]{1,0:T(8,128)(2,1)S(1)}, bf16[192,256]{1,0:T(8,128)(2,1)S(1)}, u32[]{:S(2)}, u32[]{:S(2)}) collective-permute-start(bf16[192,256]{1,0:T(8,128)(2,1)S(1)} %hidden.2.refs_0_), channel_id=1, source_target_pairs={{0,8},{1,17},{2,10},{3,19},{4,12},{5,21},{6,14},{7,23},{8,0},{9,25... | collective-permute-start | bytes 294920 | tf_op jit(solution)/shard_map/ppermute | solution.py:285
  33.6 1.6 %collective-permute-start.7 = (bf16[192,256]{1,0:T(8,128)(2,1)S(1)}, bf16[192,256]{1,0:T(8,128)(2,1)S(1)}, u32[]{:S(2)}, u32[]{:S(2)}) collective-permute-start(bf16[192,256]{1,0:T(8,128)(2,1)S(1)} %hidden.2.refs_0_), channel_id=1, source_target_pairs={{0,16},{1,9},{2,18},{3,11},{4,20},{5,13},{6,22},{7,15},{8,24},{9,1... | collective-permute-start | bytes 294920 | tf_op jit(solution)/shard_map/ppermute | solution.py:285
  35.2 3.2 %collective-permute-start.8 = (bf16[192,256]{1,0:T(8,128)(2,1)S(1)}, bf16[192,256]{1,0:T(8,128)(2,1)S(1)}, u32[]{:S(2)}, u32[]{:S(2)}) collective-permute-start(bf16[192,256]{1,0:T(8,128)(2,1)S(1)} %hidden.2.refs_0_), channel_id=1, source_target_pairs={{0,24},{1,25},{2,26},{3,27},{4,28},{5,29},{6,30},{7,31},{8,16},{9,... | collective-permute-start | bytes 294920 | tf_op jit(solution)/shard_map/ppermute | solution.py:285
  38.9 1.3 %collective-permute-done.18.refs_2_ = bf16[192,512]{1,0:T(8,128)(2,1)S(1)} collective-permute-done((bf16[192,512]{1,0:T(8,128)(2,1)S(1)}, bf16[192,512]{1,0:T(8,128)(2,1)S(1)}, u32[]{:S(2)}, u32[]{:S(2)}) %collective-permute-start.18) | collective-permute-done | bytes 196640 | tf_op jit(solution)/shard_map/ppermute | solution.py:285
  40.3 1.8 %collective-permute-start.19 = (bf16[192,256]{1,0:T(8,128)(2,1)S(1)}, bf16[192,256]{1,0:T(8,128)(2,1)S(1)}, u32[]{:S(2)}, u32[]{:S(2)}) collective-permute-start(bf16[192,256]{1,0:T(8,128)(2,1)S(1)} %hidden.3.refs_0_), channel_id=1, source_target_pairs={{0,8},{1,17},{2,10},{3,19},{4,12},{5,21},{6,14},{7,23},{8,0},{9,25... | collective-permute-start | bytes 294920 | tf_op jit(solution)/shard_map/ppermute | solution.py:285
  42.1 1.1 %collective-permute-start.20 = (bf16[192,256]{1,0:T(8,128)(2,1)S(1)}, bf16[192,256]{1,0:T(8,128)(2,1)S(1)}, u32[]{:S(2)}, u32[]{:S(2)}) collective-permute-start(bf16[192,256]{1,0:T(8,128)(2,1)S(1)} %hidden.3.refs_0_), channel_id=1, source_target_pairs={{0,16},{1,9},{2,18},{3,11},{4,20},{5,13},{6,22},{7,15},{8,24},{9,1... | collective-permute-start | bytes 294920 | tf_op jit(solution)/shard_map/ppermute | solution.py:285
  43.2 0.8 %collective-permute-start.21 = (bf16[192,256]{1,0:T(8,128)(2,1)S(1)}, bf16[192,256]{1,0:T(8,128)(2,1)S(1)}, u32[]{:S(2)}, u32[]{:S(2)}) collective-permute-start(bf16[192,256]{1,0:T(8,128)(2,1)S(1)} %hidden.3.refs_0_), channel_id=1, source_target_pairs={{0,24},{1,25},{2,26},{3,27},{4,28},{5,29},{6,30},{7,31},{8,16},{9,... | collective-permute-start | bytes 294920 | tf_op jit(solution)/shard_map/ppermute | solution.py:285
  44.0 2.3 %stage_down.1.w = bf16[2,1024,896]{2,1,0:T(8,128)(2,1)S(1)} custom-call(s32[2,4]{1,0:T(2,128)} %bitcast.10, bf16[1,2,1024,896]{3,2,1,0:T(8,128)(2,1)} %w_down.1), custom_call_target="tpu_custom_call" | custom-call | bytes 7340032 | tf_op jit(solution)/shard_map/stage_down/pallas_call | solution.py:364
  46.4 0.7 %down.2 = (bf16[48,896]{1,0:T(8,128)(2,1)S(1)}, bf16[48,896]{1,0:T(8,128)(2,1)S(1)}, bf16[48,896]{1,0:T(8,128)(2,1)S(1)}, bf16[48,896]{1,0:T(8,128)(2,1)S(1)}) custom-call(bf16[2,1024,896]{2,1,0:T(8,128)(2,1)S(1)} %stage_down.1.w, bf16[192,256]{1,0:T(8,128)(2,1)S(1)} %hidden.2.refs_0_, bf16[192,256]{1,0:T(8,128)(2,1)S(1)} %collective-permute-done.6.refs_1_, ...), custom_call_target="tpu_custom_call" | custom-call | flops 352321536 | bytes 3670016 | tf_op jit(solution)/shard_map/down/pallas_call | solution.py:411
  47.6 1.1 %collective-permute-done.21.refs_3_ = bf16[192,256]{1,0:T(8,128)(2,1)S(1)} collective-permute-done((bf16[192,256]{1,0:T(8,128)(2,1)S(1)}, bf16[192,256]{1,0:T(8,128)(2,1)S(1)}, u32[]{:S(2)}, u32[]{:S(2)}) %collective-permute-start.21) | collective-permute-done | bytes 98336 | tf_op jit(solution)/shard_map/ppermute | solution.py:285
  48.7 0.7 %down.3 = (bf16[48,896]{1,0:T(8,128)(2,1)S(1)}, bf16[48,896]{1,0:T(8,128)(2,1)S(1)}, bf16[48,896]{1,0:T(8,128)(2,1)S(1)}, bf16[48,896]{1,0:T(8,128)(2,1)S(1)}) custom-call(bf16[2,1024,896]{2,1,0:T(8,128)(2,1)S(1)} %stage_down.1.w, bf16[192,256]{1,0:T(8,128)(2,1)S(1)} %hidden.3.refs_0_, bf16[192,256]{1,0:T(8,128)(2,1)S(1)} %collective-permute-done.19.refs_1_, ...), custom_call_target="tpu_custom_call" | custom-call | flops 352321536 | bytes 3670016 | tf_op jit(solution)/shard_map/down/pallas_call | solution.py:411
  49.4 1.0 %collective-permute-start.22 = (bf16[48,896]{1,0:T(8,128)(2,1)S(1)}, bf16[48,896]{1,0:T(8,128)(2,1)S(1)}, u32[]{:S(2)}, u32[]{:S(2)}) collective-permute-start(bf16[48,896]{1,0:T(8,128)(2,1)S(1)} %get-tuple-element.61), channel_id=1, source_target_pairs={{0,2},{1,3},{2,0},{3,1},{4,6},{5,7},{6,4},{7,5},{8,10},{9,11},{10,... | collective-permute-start | bytes 258056 | tf_op jit(solution)/shard_map/ppermute | solution.py:295
  50.4 1.7 %collective-permute-start.9 = (bf16[48,896]{1,0:T(8,128)(2,1)S(1)}, bf16[48,896]{1,0:T(8,128)(2,1)S(1)}, u32[]{:S(2)}, u32[]{:S(2)}) collective-permute-start(bf16[48,896]{1,0:T(8,128)(2,1)S(1)} %get-tuple-element.48), channel_id=1, source_target_pairs={{0,4},{1,5},{2,6},{3,7},{4,0},{5,1},{6,2},{7,3},{8,12},{9,13},{10,... | collective-permute-start | bytes 258056 | tf_op jit(solution)/shard_map/ppermute | solution.py:295
  52.4 0.8 %collective-permute-done.10.refs_3_ = bf16[48,896]{1,0:T(8,128)(2,1)S(1)} collective-permute-done((bf16[48,896]{1,0:T(8,128)(2,1)S(1)}, bf16[48,896]{1,0:T(8,128)(2,1)S(1)}, u32[]{:S(2)}, u32[]{:S(2)}) %collective-permute-start.10) | collective-permute-done | bytes 86048 | tf_op jit(solution)/shard_map/ppermute | solution.py:295
  53.2 2.8 %collective-permute-start.24 = (bf16[48,896]{1,0:T(8,128)(2,1)S(1)}, bf16[48,896]{1,0:T(8,128)(2,1)S(1)}, u32[]{:S(2)}, u32[]{:S(2)}) collective-permute-start(bf16[48,896]{1,0:T(8,128)(2,1)S(1)} %get-tuple-element.63), channel_id=1, source_target_pairs={{0,6},{1,7},{2,4},{3,5},{4,2},{5,3},{6,0},{7,1},{8,14},{9,15},{10,... | collective-permute-start | bytes 258056 | tf_op jit(solution)/shard_map/ppermute | solution.py:295
  56.4 1.3 %weigh.1 = (bf16[128,192]{1,0:T(8,128)(2,1)S(1)}, bf16[128,192]{1,0:T(8,128)(2,1)S(1)}, bf16[128,192]{1,0:T(8,128)(2,1)S(1)}, bf16[128,192]{1,0:T(8,128)(2,1)S(1)}) custom-call(s32[2,4]{1,0:T(2,128)} %bitcast.11, s32[12]{0:T(128)} %cap_in.3, s32[8,128]{1,0:T(8,128)} %bitcast.5, s32[8,128]{1,0:T(8,128)} %bitcast.7, f32[8,128]{1,0:T(8,128)} %bitcast.12), custom_call_target="tpu_custom_call" | custom-call | tf_op jit(solution)/shard_map/weigh/pallas_call | solution.py:340
  58.6 2.2 %collective-permute-done.24.refs_5_ = bf16[48,896]{1,0:T(8,128)(2,1)S(1)} collective-permute-done((bf16[48,896]{1,0:T(8,128)(2,1)S(1)}, bf16[48,896]{1,0:T(8,128)(2,1)S(1)}, u32[]{:S(2)}, u32[]{:S(2)}) %collective-permute-start.24) | collective-permute-done | bytes 86048 | tf_op jit(solution)/shard_map/ppermute | solution.py:295
  60.8 1.8 %collective-permute-done.25.refs_6_ = bf16[48,896]{1,0:T(8,128)(2,1)S(1)} collective-permute-done((bf16[48,896]{1,0:T(8,128)(2,1)S(1)}, bf16[48,896]{1,0:T(8,128)(2,1)S(1)}, u32[]{:S(2)}, u32[]{:S(2)}) %collective-permute-start.25) | collective-permute-done | bytes 86048 | tf_op jit(solution)/shard_map/ppermute | solution.py:295
  62.6 1.0 %combine.3 = bf16[128,896]{1,0:T(8,128)(2,1)} custom-call(f32[128,896]{1,0:T(8,128)S(1)} %combine.2.refs_0_, bf16[128,192]{1,0:T(8,128)(2,1)S(1)} %get-tuple-element.52.refs_1_, bf16[128,192]{1,0:T(8,128)(2,1)S(1)} %get-tuple-element.53.refs_2_, bf16[48,896]{1,0:T(8,128)(2,1)S(1)} %collective-permute-done.22.refs_3_, ...), custom_call_target="tpu_custom_call" | custom-call | tf_op jit(solution)/shard_map/combine/pallas_call | solution.py:427
  (38 shorter events, 6.7 us)
Async XLA Ops:
  1.6 10.7 %collective-permute-start = (bf16[48,896]{1,0:T(8,128)(2,1)S(1)}, bf16[48,896]{1,0:T(8,128)(2,1)S(1)}, u32[]{:S(2)}, u32[]{:S(2)}) collective-permute-start(bf16[48,896]{1,0:T(8,128)(2,1)S(1)} %get-tuple-element.37), channel_id=1, source_target_pairs={{0,4},{1,5},{2,6},{3,7},{4,0},{5,1},{6,2},{7,3},{8,12},{9,13},{10,... | collective-permute-start | bytes 258056 | tf_op jit(solution)/shard_map/ppermute | solution.py:295
  5.7 10.0 %collective-permute-start.1 = (bf16[48,896]{1,0:T(8,128)(2,1)S(1)}, bf16[48,896]{1,0:T(8,128)(2,1)S(1)}, u32[]{:S(2)}, u32[]{:S(2)}) collective-permute-start(bf16[48,896]{1,0:T(8,128)(2,1)S(1)} %get-tuple-element.38), channel_id=1, source_target_pairs={{0,5},{1,4},{2,7},{3,6},{4,1},{5,0},{6,3},{7,2},{8,13},{9,12},{10,... | collective-permute-start | bytes 258056 | tf_op jit(solution)/shard_map/ppermute | solution.py:295
  5.7 11.3 %collective-permute-start.2 = (bf16[48,896]{1,0:T(8,128)(2,1)S(1)}, bf16[48,896]{1,0:T(8,128)(2,1)S(1)}, u32[]{:S(2)}, u32[]{:S(2)}) collective-permute-start(bf16[48,896]{1,0:T(8,128)(2,1)S(1)} %get-tuple-element.39), channel_id=1, source_target_pairs={{0,1},{1,0},{2,3},{3,2},{4,5},{5,4},{6,7},{7,6},{8,9},{9,8},{10,11... | collective-permute-start | bytes 258056 | tf_op jit(solution)/shard_map/ppermute | solution.py:295
  5.9 14.0 %collective-permute-start.12 = (bf16[48,896]{1,0:T(8,128)(2,1)S(1)}, bf16[48,896]{1,0:T(8,128)(2,1)S(1)}, u32[]{:S(2)}, u32[]{:S(2)}) collective-permute-start(bf16[48,896]{1,0:T(8,128)(2,1)S(1)} %get-tuple-element.54), channel_id=1, source_target_pairs={{0,2},{1,3},{2,0},{3,1},{4,6},{5,7},{6,4},{7,5},{8,10},{9,11},{10,... | collective-permute-start | bytes 258056 | tf_op jit(solution)/shard_map/ppermute | solution.py:295
  7.7 13.7 %collective-permute-start.13 = (bf16[48,896]{1,0:T(8,128)(2,1)S(1)}, bf16[48,896]{1,0:T(8,128)(2,1)S(1)}, u32[]{:S(2)}, u32[]{:S(2)}) collective-permute-start(bf16[48,896]{1,0:T(8,128)(2,1)S(1)} %get-tuple-element.55), channel_id=1, source_target_pairs={{0,3},{1,2},{2,1},{3,0},{4,7},{5,6},{6,5},{7,4},{8,11},{9,10},{10,... | collective-permute-start | bytes 258056 | tf_op jit(solution)/shard_map/ppermute | solution.py:295
  12.3 9.6 %collective-permute-start.14 = (bf16[48,896]{1,0:T(8,128)(2,1)S(1)}, bf16[48,896]{1,0:T(8,128)(2,1)S(1)}, u32[]{:S(2)}, u32[]{:S(2)}) collective-permute-start(bf16[48,896]{1,0:T(8,128)(2,1)S(1)} %get-tuple-element.56), channel_id=1, source_target_pairs={{0,6},{1,7},{2,4},{3,5},{4,2},{5,3},{6,0},{7,1},{8,14},{9,15},{10,... | collective-permute-start | bytes 258056 | tf_op jit(solution)/shard_map/ppermute | solution.py:295
  15.7 6.4 %collective-permute-start.15 = (bf16[48,896]{1,0:T(8,128)(2,1)S(1)}, bf16[48,896]{1,0:T(8,128)(2,1)S(1)}, u32[]{:S(2)}, u32[]{:S(2)}) collective-permute-start(bf16[48,896]{1,0:T(8,128)(2,1)S(1)} %get-tuple-element.57), channel_id=1, source_target_pairs={{0,7},{1,6},{2,5},{3,4},{4,3},{5,2},{6,1},{7,0},{8,15},{9,14},{10,... | collective-permute-start | bytes 258056 | tf_op jit(solution)/shard_map/ppermute | solution.py:295
  17.9 8.7 %collective-permute-start.4 = (bf16[192,512]{1,0:T(8,128)(2,1)S(1)}, bf16[192,512]{1,0:T(8,128)(2,1)S(1)}, u32[]{:S(2)}, u32[]{:S(2)}) collective-permute-start(bf16[192,512]{1,0:T(8,128)(2,1)S(1)} %up.11), channel_id=1, source_target_pairs={{0,16},{1,9},{2,18},{3,11},{4,20},{5,13},{6,22},{7,15},{8,24},{9,1... | collective-permute-start | bytes 589832 | tf_op jit(solution)/shard_map/ppermute | solution.py:285
  19.9 10.5 %collective-permute-start.3 = (bf16[192,512]{1,0:T(8,128)(2,1)S(1)}, bf16[192,512]{1,0:T(8,128)(2,1)S(1)}, u32[]{:S(2)}, u32[]{:S(2)}) collective-permute-start(bf16[192,512]{1,0:T(8,128)(2,1)S(1)} %up.10), channel_id=1, source_target_pairs={{0,8},{1,17},{2,10},{3,19},{4,12},{5,21},{6,14},{7,23},{8,0},{9,25... | collective-permute-start | bytes 589832 | tf_op jit(solution)/shard_map/ppermute | solution.py:285
  21.4 10.3 %collective-permute-start.5 = (bf16[192,512]{1,0:T(8,128)(2,1)S(1)}, bf16[192,512]{1,0:T(8,128)(2,1)S(1)}, u32[]{:S(2)}, u32[]{:S(2)}) collective-permute-start(bf16[192,512]{1,0:T(8,128)(2,1)S(1)} %get-tuple-element.47), channel_id=1, source_target_pairs={{0,24},{1,25},{2,26},{3,27},{4,28},{5,29},{6,30},{7,31},{8,16},{9,... | collective-permute-start | bytes 589832 | tf_op jit(solution)/shard_map/ppermute | solution.py:285
  23.0 12.2 %collective-permute-start.17 = (bf16[192,512]{1,0:T(8,128)(2,1)S(1)}, bf16[192,512]{1,0:T(8,128)(2,1)S(1)}, u32[]{:S(2)}, u32[]{:S(2)}) collective-permute-start(bf16[192,512]{1,0:T(8,128)(2,1)S(1)} %up.15), channel_id=1, source_target_pairs={{0,16},{1,9},{2,18},{3,11},{4,20},{5,13},{6,22},{7,15},{8,24},{9,1... | collective-permute-start | bytes 589832 | tf_op jit(solution)/shard_map/ppermute | solution.py:285
  25.0 13.9 %collective-permute-start.16 = (bf16[192,512]{1,0:T(8,128)(2,1)S(1)}, bf16[192,512]{1,0:T(8,128)(2,1)S(1)}, u32[]{:S(2)}, u32[]{:S(2)}) collective-permute-start(bf16[192,512]{1,0:T(8,128)(2,1)S(1)} %up.14), channel_id=1, source_target_pairs={{0,8},{1,17},{2,10},{3,19},{4,12},{5,21},{6,14},{7,23},{8,0},{9,25... | collective-permute-start | bytes 589832 | tf_op jit(solution)/shard_map/ppermute | solution.py:285
  26.6 13.6 %collective-permute-start.18 = (bf16[192,512]{1,0:T(8,128)(2,1)S(1)}, bf16[192,512]{1,0:T(8,128)(2,1)S(1)}, u32[]{:S(2)}, u32[]{:S(2)}) collective-permute-start(bf16[192,512]{1,0:T(8,128)(2,1)S(1)} %get-tuple-element.60), channel_id=1, source_target_pairs={{0,24},{1,25},{2,26},{3,27},{4,28},{5,29},{6,30},{7,31},{8,16},{9,... | collective-permute-start | bytes 589832 | tf_op jit(solution)/shard_map/ppermute | solution.py:285
  31.8 11.3 %collective-permute-start.6 = (bf16[192,256]{1,0:T(8,128)(2,1)S(1)}, bf16[192,256]{1,0:T(8,128)(2,1)S(1)}, u32[]{:S(2)}, u32[]{:S(2)}) collective-permute-start(bf16[192,256]{1,0:T(8,128)(2,1)S(1)} %hidden.2.refs_0_), channel_id=1, source_target_pairs={{0,8},{1,17},{2,10},{3,19},{4,12},{5,21},{6,14},{7,23},{8,0},{9,25... | collective-permute-start | bytes 294920 | tf_op jit(solution)/shard_map/ppermute | solution.py:285
  33.6 12.7 %collective-permute-start.7 = (bf16[192,256]{1,0:T(8,128)(2,1)S(1)}, bf16[192,256]{1,0:T(8,128)(2,1)S(1)}, u32[]{:S(2)}, u32[]{:S(2)}) collective-permute-start(bf16[192,256]{1,0:T(8,128)(2,1)S(1)} %hidden.2.refs_0_), channel_id=1, source_target_pairs={{0,16},{1,9},{2,18},{3,11},{4,20},{5,13},{6,22},{7,15},{8,24},{9,1... | collective-permute-start | bytes 294920 | tf_op jit(solution)/shard_map/ppermute | solution.py:285
  35.2 11.2 %collective-permute-start.8 = (bf16[192,256]{1,0:T(8,128)(2,1)S(1)}, bf16[192,256]{1,0:T(8,128)(2,1)S(1)}, u32[]{:S(2)}, u32[]{:S(2)}) collective-permute-start(bf16[192,256]{1,0:T(8,128)(2,1)S(1)} %hidden.2.refs_0_), channel_id=1, source_target_pairs={{0,24},{1,25},{2,26},{3,27},{4,28},{5,29},{6,30},{7,31},{8,16},{9,... | collective-permute-start | bytes 294920 | tf_op jit(solution)/shard_map/ppermute | solution.py:285
  40.3 7.2 %collective-permute-start.19 = (bf16[192,256]{1,0:T(8,128)(2,1)S(1)}, bf16[192,256]{1,0:T(8,128)(2,1)S(1)}, u32[]{:S(2)}, u32[]{:S(2)}) collective-permute-start(bf16[192,256]{1,0:T(8,128)(2,1)S(1)} %hidden.3.refs_0_), channel_id=1, source_target_pairs={{0,8},{1,17},{2,10},{3,19},{4,12},{5,21},{6,14},{7,23},{8,0},{9,25... | collective-permute-start | bytes 294920 | tf_op jit(solution)/shard_map/ppermute | solution.py:285
  42.1 5.6 %collective-permute-start.20 = (bf16[192,256]{1,0:T(8,128)(2,1)S(1)}, bf16[192,256]{1,0:T(8,128)(2,1)S(1)}, u32[]{:S(2)}, u32[]{:S(2)}) collective-permute-start(bf16[192,256]{1,0:T(8,128)(2,1)S(1)} %hidden.3.refs_0_), channel_id=1, source_target_pairs={{0,16},{1,9},{2,18},{3,11},{4,20},{5,13},{6,22},{7,15},{8,24},{9,1... | collective-permute-start | bytes 294920 | tf_op jit(solution)/shard_map/ppermute | solution.py:285
  43.2 5.5 %collective-permute-start.21 = (bf16[192,256]{1,0:T(8,128)(2,1)S(1)}, bf16[192,256]{1,0:T(8,128)(2,1)S(1)}, u32[]{:S(2)}, u32[]{:S(2)}) collective-permute-start(bf16[192,256]{1,0:T(8,128)(2,1)S(1)} %hidden.3.refs_0_), channel_id=1, source_target_pairs={{0,24},{1,25},{2,26},{3,27},{4,28},{5,29},{6,30},{7,31},{8,16},{9,... | collective-permute-start | bytes 294920 | tf_op jit(solution)/shard_map/ppermute | solution.py:285
  47.1 6.1 %collective-permute-start.10 = (bf16[48,896]{1,0:T(8,128)(2,1)S(1)}, bf16[48,896]{1,0:T(8,128)(2,1)S(1)}, u32[]{:S(2)}, u32[]{:S(2)}) collective-permute-start(bf16[48,896]{1,0:T(8,128)(2,1)S(1)} %get-tuple-element.49), channel_id=1, source_target_pairs={{0,5},{1,4},{2,7},{3,6},{4,1},{5,0},{6,3},{7,2},{8,13},{9,12},{10,... | collective-permute-start | bytes 258056 | tf_op jit(solution)/shard_map/ppermute | solution.py:295
  47.2 8.8 %collective-permute-start.11 = (bf16[48,896]{1,0:T(8,128)(2,1)S(1)}, bf16[48,896]{1,0:T(8,128)(2,1)S(1)}, u32[]{:S(2)}, u32[]{:S(2)}) collective-permute-start(bf16[48,896]{1,0:T(8,128)(2,1)S(1)} %get-tuple-element.50), channel_id=1, source_target_pairs={{0,1},{1,0},{2,3},{3,2},{4,5},{5,4},{6,7},{7,6},{8,9},{9,8},{10,11... | collective-permute-start | bytes 258056 | tf_op jit(solution)/shard_map/ppermute | solution.py:295
  49.4 8.6 %collective-permute-start.22 = (bf16[48,896]{1,0:T(8,128)(2,1)S(1)}, bf16[48,896]{1,0:T(8,128)(2,1)S(1)}, u32[]{:S(2)}, u32[]{:S(2)}) collective-permute-start(bf16[48,896]{1,0:T(8,128)(2,1)S(1)} %get-tuple-element.61), channel_id=1, source_target_pairs={{0,2},{1,3},{2,0},{3,1},{4,6},{5,7},{6,4},{7,5},{8,10},{9,11},{10,... | collective-permute-start | bytes 258056 | tf_op jit(solution)/shard_map/ppermute | solution.py:295
  50.4 7.4 %collective-permute-start.9 = (bf16[48,896]{1,0:T(8,128)(2,1)S(1)}, bf16[48,896]{1,0:T(8,128)(2,1)S(1)}, u32[]{:S(2)}, u32[]{:S(2)}) collective-permute-start(bf16[48,896]{1,0:T(8,128)(2,1)S(1)} %get-tuple-element.48), channel_id=1, source_target_pairs={{0,4},{1,5},{2,6},{3,7},{4,0},{5,1},{6,2},{7,3},{8,12},{9,13},{10,... | collective-permute-start | bytes 258056 | tf_op jit(solution)/shard_map/ppermute | solution.py:295
  52.0 6.5 %collective-permute-start.23 = (bf16[48,896]{1,0:T(8,128)(2,1)S(1)}, bf16[48,896]{1,0:T(8,128)(2,1)S(1)}, u32[]{:S(2)}, u32[]{:S(2)}) collective-permute-start(bf16[48,896]{1,0:T(8,128)(2,1)S(1)} %get-tuple-element.62), channel_id=1, source_target_pairs={{0,3},{1,2},{2,1},{3,0},{4,7},{5,6},{6,5},{7,4},{8,11},{9,10},{10,... | collective-permute-start | bytes 258056 | tf_op jit(solution)/shard_map/ppermute | solution.py:295
  53.2 7.6 %collective-permute-start.24 = (bf16[48,896]{1,0:T(8,128)(2,1)S(1)}, bf16[48,896]{1,0:T(8,128)(2,1)S(1)}, u32[]{:S(2)}, u32[]{:S(2)}) collective-permute-start(bf16[48,896]{1,0:T(8,128)(2,1)S(1)} %get-tuple-element.63), channel_id=1, source_target_pairs={{0,6},{1,7},{2,4},{3,5},{4,2},{5,3},{6,0},{7,1},{8,14},{9,15},{10,... | collective-permute-start | bytes 258056 | tf_op jit(solution)/shard_map/ppermute | solution.py:295
  55.9 6.7 %collective-permute-start.25 = (bf16[48,896]{1,0:T(8,128)(2,1)S(1)}, bf16[48,896]{1,0:T(8,128)(2,1)S(1)}, u32[]{:S(2)}, u32[]{:S(2)}) collective-permute-start(bf16[48,896]{1,0:T(8,128)(2,1)S(1)} %get-tuple-element.64), channel_id=1, source_target_pairs={{0,7},{1,6},{2,5},{3,4},{4,3},{5,2},{6,1},{7,0},{8,15},{9,14},{10,... | collective-permute-start | bytes 258056 | tf_op jit(solution)/shard_map/ppermute | solution.py:295

commit v3 on v2

--- a/solution.py
+++ b/solution.py
@@ -184,13 +184,13 @@
         copy.wait()
 
 
-def stage_kernel(place_in, w_gate, w_up, *refs):
+def stage_kernel(parts, ks, place_in, w_gate, w_up, *refs):
     outs, place, sems = refs[:-2], refs[-2], refs[-1]
     block = outs[0].shape[2] // 2
 
     def moves(which, i):
-        for k, out in enumerate(outs):
-            q = lax.axis_index("dp") ^ role(k, len(outs), lax.axis_index("expert"))
+        for k, out in zip(ks, outs):
+            q = lax.axis_index("dp") ^ role(k, parts, lax.axis_index("expert"))
             columns = pl.ds(pl.multiple_of(q * block, block), block)
             for g, w in enumerate((w_gate, w_up)):
                 yield w.at[0, which, :, columns], out.at[i, :, pl.ds(g * block, block)]
@@ -351,16 +351,18 @@
 
     block = ff // parts
     order = list(range(parts - 1, 0, -1)) + [0]
-    staged = pl.pallas_call(
-        stage_kernel,
-        out_shape=[sds((2, cols, 2 * block), BF16)] * parts,
-        in_specs=[hbm] * 3,
-        out_specs=vmem_specs(parts),
-        scratch_shapes=[pltpu.SMEM((2, hot), I32), pltpu.SemaphoreType.DMA((4 * parts + 1,))],
-        compiler_params=PARAMS,
-        cost_estimate=cost(0, 16 * cols * ff),
-        name="stage",
-    )(*map(in_hbm, [placement.T, w_gate, w_up]))
+    staged = {}
+    for ks in (order[:-1], [0]):
+        made = pl.pallas_call(
+            functools.partial(stage_kernel, parts, ks),
+            out_shape=[sds((2, cols, 2 * block), BF16)] * len(ks),
+            in_specs=[hbm] * 3,
+            out_specs=vmem_specs(len(ks)),
+            scratch_shapes=[pltpu.SMEM((2, hot), I32), pltpu.SemaphoreType.DMA((4 * len(ks) + 1,))],
+            compiler_params=PARAMS,
+            cost_estimate=cost(0, 16 * cols * block * len(ks)),
+        )(*map(in_hbm, [placement.T, w_gate, w_up]))
+        staged.update(zip(ks, made))
     staged_down = pl.pallas_call(
         functools.partial(stage_down_kernel, parts),
         out_shape=sds((2, ff, cols), BF16),

time: 63.8 us -> 63.8 us (level)
  Pallas kernels: 15.1 us -> 16.4 us
  starting transfers between devices: 37.9 us -> 37.1 us
  waiting for transfers between devices: 10.5 us -> 9.74 us
    pallas_call x1 -> x2, Pallas kernels: 3.49 us -> 4.87 us  [on_device(): pl.pallas_call(functools.partial(stage_kernel, parts, ks), out_shape=[sds...]
    ppermute x12, waiting for transfers between devices: 3.76 us -> 2.5 us  [to_partner(): return lax.ppermute(x, ('dp', 'expert'), pairs)]
    ppermute x12, starting transfers between devices: 20.5 us -> 19.8 us  [to_partner(): return lax.ppermute(x, ('dp', 'expert'), pairs)]
  transfers between devices with their start and end apart: 26 -> 26, of which waited for: 10 -> 9; matrix products, arithmetic and copies ran while one was open for 0% -> 0% of each run, Pallas kernels for 20% -> 22%
where the time goes in v3:
time: 63.8 us; the launch traced here: 63.5 us
  starting transfers between devices  37.1 us (58%)
  Pallas kernels  16.4 us (26%)
  waiting for transfers between devices  9.74 us (15%)
    ppermute x12, starting transfers between devices, to_partner(): return lax.ppermute(x, ('dp', 'expert'), pairs)  19.8 us
    ppermute x14, starting transfers between devices, exchange(): moved.append(lax.ppermute(piece, axis, flips(n, j)) if j else piece)  17.3 us
    ppermute x14, waiting for transfers between devices, exchange(): moved.append(lax.ppermute(piece, axis, flips(n, j)) if j else piece)  7.24 us
    pallas_call x2, Pallas kernels, on_device(): pl.pallas_call(functools.partial(stage_kernel, parts, ks), out_shape=[sds...  4.87 us
    pallas_call x8, Pallas kernels, on_device(): pl.pallas_call(up_next_kernel if i else functools.partial(up_first_kernel...  3.42 us
    ppermute x12, waiting for transfers between devices, to_partner(): return lax.ppermute(x, ('dp', 'expert'), pairs)  2.5 us
    pallas_call x1, Pallas kernels, on_device(): pl.pallas_call(functools.partial(stage_down_kernel, parts), out_shape=sds...  2.34 us
    pallas_call x1, Pallas kernels, on_device(): pl.pallas_call(functools.partial(route_kernel, sizes, chunks), out_shape=...  1.57 us
  transfers between devices with their start and end apart: 26, of which 9 were waited for; matrix products, arithmetic and copies ran while one was open for 0% of the time, Pallas kernels for 22%

profile of v3, /device:TPU:0, one launch (start us, length us, event | category | flops | bytes accessed | tf_op | source)
XLA Modules:
  0.0 63.5 jit_solution(2884470135213441542)
XLA Ops:
  0.0 1.6 %route.1 = (bf16[48,896]{1,0:T(8,128)(2,1)S(1)}, bf16[48,896]{1,0:T(8,128)(2,1)S(1)}, bf16[48,896]{1,0:T(8,128)(2,1)S(1)}, bf16[48,896]{1,0:T(8,128)(2,1)S(1)}, ...) custom-call(s32[2,4]{1,0:T(2,128)} %bitcast.4, ...), custom_call_target="tpu_custom_call" | custom-call | tf_op jit(solution)/shard_map/route/pallas_call | solution.py:329
  1.6 4.1 %collective-permute-start = (bf16[48,896]{1,0:T(8,128)(2,1)S(1)}, bf16[48,896]{1,0:T(8,128)(2,1)S(1)}, u32[]{:S(2)}, u32[]{:S(2)}) collective-permute-start(bf16[48,896]{1,0:T(8,128)(2,1)S(1)} %get-tuple-element.36), channel_id=1, source_target_pairs={{0,4},{1,5},{2,6},{3,7},{4,0},{5,1},{6,2},{7,3},{8,12},{9,13},{10,... | collective-permute-start | bytes 258056 | tf_op jit(solution)/shard_map/ppermute | solution.py:295
  5.9 1.8 %collective-permute-start.12 = (bf16[48,896]{1,0:T(8,128)(2,1)S(1)}, bf16[48,896]{1,0:T(8,128)(2,1)S(1)}, u32[]{:S(2)}, u32[]{:S(2)}) collective-permute-start(bf16[48,896]{1,0:T(8,128)(2,1)S(1)} %get-tuple-element.52), channel_id=1, source_target_pairs={{0,2},{1,3},{2,0},{3,1},{4,6},{5,7},{6,4},{7,5},{8,10},{9,11},{10,... | collective-permute-start | bytes 258056 | tf_op jit(solution)/shard_map/ppermute | solution.py:295
  7.7 2.9 %shard_map.91 = (bf16[2,896,512]{2,1,0:T(8,128)(2,1)S(1)}, bf16[2,896,512]{2,1,0:T(8,128)(2,1)S(1)}, bf16[2,896,512]{2,1,0:T(8,128)(2,1)S(1)}) custom-call(s32[2,4]{1,0:T(2,128)} %bitcast.5, bf16[1,2,896,1024]{3,2,1,0:T(8,128)(2,1)} %w_gate.3, bf16[1,2,896,1024]{3,2,1,0:T(8,128)(2,1)} %w_up.3), custom_call_target="tpu_custom_call" | custom-call | bytes 11010048 | tf_op jit(solution)/shard_map/pallas_call | solution.py:356
  10.6 1.7 %collective-permute-done.refs_0_ = bf16[48,896]{1,0:T(8,128)(2,1)S(1)} collective-permute-done((bf16[48,896]{1,0:T(8,128)(2,1)S(1)}, bf16[48,896]{1,0:T(8,128)(2,1)S(1)}, u32[]{:S(2)}, u32[]{:S(2)}) %collective-permute-start) | collective-permute-done | bytes 86048 | tf_op jit(solution)/shard_map/ppermute | solution.py:295
  12.3 3.3 %collective-permute-start.14 = (bf16[48,896]{1,0:T(8,128)(2,1)S(1)}, bf16[48,896]{1,0:T(8,128)(2,1)S(1)}, u32[]{:S(2)}, u32[]{:S(2)}) collective-permute-start(bf16[48,896]{1,0:T(8,128)(2,1)S(1)} %get-tuple-element.54), channel_id=1, source_target_pairs={{0,6},{1,7},{2,4},{3,5},{4,2},{5,3},{6,0},{7,1},{8,14},{9,15},{10,... | collective-permute-start | bytes 258056 | tf_op jit(solution)/shard_map/ppermute | solution.py:295
  15.7 1.3 %collective-permute-start.15 = (bf16[48,896]{1,0:T(8,128)(2,1)S(1)}, bf16[48,896]{1,0:T(8,128)(2,1)S(1)}, u32[]{:S(2)}, u32[]{:S(2)}) collective-permute-start(bf16[48,896]{1,0:T(8,128)(2,1)S(1)} %get-tuple-element.55), channel_id=1, source_target_pairs={{0,7},{1,6},{2,5},{3,4},{4,3},{5,2},{6,1},{7,0},{8,15},{9,14},{10,... | collective-permute-start | bytes 258056 | tf_op jit(solution)/shard_map/ppermute | solution.py:295
  17.9 1.6 %collective-permute-start.4 = (bf16[192,512]{1,0:T(8,128)(2,1)S(1)}, bf16[192,512]{1,0:T(8,128)(2,1)S(1)}, u32[]{:S(2)}, u32[]{:S(2)}) collective-permute-start(bf16[192,512]{1,0:T(8,128)(2,1)S(1)} %up.11), channel_id=1, source_target_pairs={{0,16},{1,9},{2,18},{3,11},{4,20},{5,13},{6,22},{7,15},{8,24},{9,1... | collective-permute-start | bytes 589832 | tf_op jit(solution)/shard_map/ppermute | solution.py:285
  19.9 1.6 %collective-permute-start.3 = (bf16[192,512]{1,0:T(8,128)(2,1)S(1)}, bf16[192,512]{1,0:T(8,128)(2,1)S(1)}, u32[]{:S(2)}, u32[]{:S(2)}) collective-permute-start(bf16[192,512]{1,0:T(8,128)(2,1)S(1)} %up.10), channel_id=1, source_target_pairs={{0,8},{1,17},{2,10},{3,19},{4,12},{5,21},{6,14},{7,23},{8,0},{9,25... | collective-permute-start | bytes 589832 | tf_op jit(solution)/shard_map/ppermute | solution.py:285
  23.0 1.6 %collective-permute-start.17 = (bf16[192,512]{1,0:T(8,128)(2,1)S(1)}, bf16[192,512]{1,0:T(8,128)(2,1)S(1)}, u32[]{:S(2)}, u32[]{:S(2)}) collective-permute-start(bf16[192,512]{1,0:T(8,128)(2,1)S(1)} %up.15), channel_id=1, source_target_pairs={{0,16},{1,9},{2,18},{3,11},{4,20},{5,13},{6,22},{7,15},{8,24},{9,1... | collective-permute-start | bytes 589832 | tf_op jit(solution)/shard_map/ppermute | solution.py:285
  25.0 1.6 %collective-permute-start.16 = (bf16[192,512]{1,0:T(8,128)(2,1)S(1)}, bf16[192,512]{1,0:T(8,128)(2,1)S(1)}, u32[]{:S(2)}, u32[]{:S(2)}) collective-permute-start(bf16[192,512]{1,0:T(8,128)(2,1)S(1)} %up.14), channel_id=1, source_target_pairs={{0,8},{1,17},{2,10},{3,19},{4,12},{5,21},{6,14},{7,23},{8,0},{9,25... | collective-permute-start | bytes 589832 | tf_op jit(solution)/shard_map/ppermute | solution.py:285
  26.6 3.4 %collective-permute-start.18 = (bf16[192,512]{1,0:T(8,128)(2,1)S(1)}, bf16[192,512]{1,0:T(8,128)(2,1)S(1)}, u32[]{:S(2)}, u32[]{:S(2)}) collective-permute-start(bf16[192,512]{1,0:T(8,128)(2,1)S(1)} %get-tuple-element.58), channel_id=1, source_target_pairs={{0,24},{1,25},{2,26},{3,27},{4,28},{5,29},{6,30},{7,31},{8,16},{9,... | collective-permute-start | bytes 589832 | tf_op jit(solution)/shard_map/ppermute | solution.py:285
  30.0 2.0 %shard_map.92.weights = bf16[2,896,512]{2,1,0:T(8,128)(2,1)S(1)} custom-call(s32[2,4]{1,0:T(2,128)} %bitcast.6, bf16[1,2,896,1024]{3,2,1,0:T(8,128)(2,1)} %w_gate.3, bf16[1,2,896,1024]{3,2,1,0:T(8,128)(2,1)} %w_up.3), custom_call_target="tpu_custom_call" | custom-call | bytes 3670016 | tf_op jit(solution)/shard_map/pallas_call | solution.py:356
  32.6 1.0 %collective-permute-start.6 = (bf16[192,256]{1,0:T(8,128)(2,1)S(1)}, bf16[192,256]{1,0:T(8,128)(2,1)S(1)}, u32[]{:S(2)}, u32[]{:S(2)}) collective-permute-start(bf16[192,256]{1,0:T(8,128)(2,1)S(1)} %hidden.2.refs_0_), channel_id=1, source_target_pairs={{0,8},{1,17},{2,10},{3,19},{4,12},{5,21},{6,14},{7,23},{8,0},{9,25... | collective-permute-start | bytes 294920 | tf_op jit(solution)/shard_map/ppermute | solution.py:285
  33.6 1.6 %collective-permute-start.7 = (bf16[192,256]{1,0:T(8,128)(2,1)S(1)}, bf16[192,256]{1,0:T(8,128)(2,1)S(1)}, u32[]{:S(2)}, u32[]{:S(2)}) collective-permute-start(bf16[192,256]{1,0:T(8,128)(2,1)S(1)} %hidden.2.refs_0_), channel_id=1, source_target_pairs={{0,16},{1,9},{2,18},{3,11},{4,20},{5,13},{6,22},{7,15},{8,24},{9,1... | collective-permute-start | bytes 294920 | tf_op jit(solution)/shard_map/ppermute | solution.py:285
  35.2 3.3 %collective-permute-start.8 = (bf16[192,256]{1,0:T(8,128)(2,1)S(1)}, bf16[192,256]{1,0:T(8,128)(2,1)S(1)}, u32[]{:S(2)}, u32[]{:S(2)}) collective-permute-start(bf16[192,256]{1,0:T(8,128)(2,1)S(1)} %hidden.2.refs_0_), channel_id=1, source_target_pairs={{0,24},{1,25},{2,26},{3,27},{4,28},{5,29},{6,30},{7,31},{8,16},{9,... | collective-permute-start | bytes 294920 | tf_op jit(solution)/shard_map/ppermute | solution.py:285
  38.9 1.3 %collective-permute-done.18.refs_2_ = bf16[192,512]{1,0:T(8,128)(2,1)S(1)} collective-permute-done((bf16[192,512]{1,0:T(8,128)(2,1)S(1)}, bf16[192,512]{1,0:T(8,128)(2,1)S(1)}, u32[]{:S(2)}, u32[]{:S(2)}) %collective-permute-start.18) | collective-permute-done | bytes 196640 | tf_op jit(solution)/shard_map/ppermute | solution.py:285
  40.3 1.8 %collective-permute-start.19 = (bf16[192,256]{1,0:T(8,128)(2,1)S(1)}, bf16[192,256]{1,0:T(8,128)(2,1)S(1)}, u32[]{:S(2)}, u32[]{:S(2)}) collective-permute-start(bf16[192,256]{1,0:T(8,128)(2,1)S(1)} %hidden.3.refs_0_), channel_id=1, source_target_pairs={{0,8},{1,17},{2,10},{3,19},{4,12},{5,21},{6,14},{7,23},{8,0},{9,25... | collective-permute-start | bytes 294920 | tf_op jit(solution)/shard_map/ppermute | solution.py:285
  42.1 1.1 %collective-permute-start.20 = (bf16[192,256]{1,0:T(8,128)(2,1)S(1)}, bf16[192,256]{1,0:T(8,128)(2,1)S(1)}, u32[]{:S(2)}, u32[]{:S(2)}) collective-permute-start(bf16[192,256]{1,0:T(8,128)(2,1)S(1)} %hidden.3.refs_0_), channel_id=1, source_target_pairs={{0,16},{1,9},{2,18},{3,11},{4,20},{5,13},{6,22},{7,15},{8,24},{9,1... | collective-permute-start | bytes 294920 | tf_op jit(solution)/shard_map/ppermute | solution.py:285
  43.2 0.8 %collective-permute-start.21 = (bf16[192,256]{1,0:T(8,128)(2,1)S(1)}, bf16[192,256]{1,0:T(8,128)(2,1)S(1)}, u32[]{:S(2)}, u32[]{:S(2)}) collective-permute-start(bf16[192,256]{1,0:T(8,128)(2,1)S(1)} %hidden.3.refs_0_), channel_id=1, source_target_pairs={{0,24},{1,25},{2,26},{3,27},{4,28},{5,29},{6,30},{7,31},{8,16},{9,... | collective-permute-start | bytes 294920 | tf_op jit(solution)/shard_map/ppermute | solution.py:285
  44.0 2.3 %stage_down.1.w = bf16[2,1024,896]{2,1,0:T(8,128)(2,1)S(1)} custom-call(s32[2,4]{1,0:T(2,128)} %bitcast.7, bf16[1,2,1024,896]{3,2,1,0:T(8,128)(2,1)} %w_down.1), custom_call_target="tpu_custom_call" | custom-call | bytes 7340032 | tf_op jit(solution)/shard_map/stage_down/pallas_call | solution.py:366
  46.4 0.7 %down.2 = (bf16[48,896]{1,0:T(8,128)(2,1)S(1)}, bf16[48,896]{1,0:T(8,128)(2,1)S(1)}, bf16[48,896]{1,0:T(8,128)(2,1)S(1)}, bf16[48,896]{1,0:T(8,128)(2,1)S(1)}) custom-call(bf16[2,1024,896]{2,1,0:T(8,128)(2,1)S(1)} %stage_down.1.w, bf16[192,256]{1,0:T(8,128)(2,1)S(1)} %hidden.2.refs_0_, bf16[192,256]{1,0:T(8,128)(2,1)S(1)} %collective-permute-done.6.refs_1_, ...), custom_call_target="tpu_custom_call" | custom-call | flops 352321536 | bytes 3670016 | tf_op jit(solution)/shard_map/down/pallas_call | solution.py:413
  47.6 1.1 %collective-permute-done.21.refs_3_ = bf16[192,256]{1,0:T(8,128)(2,1)S(1)} collective-permute-done((bf16[192,256]{1,0:T(8,128)(2,1)S(1)}, bf16[192,256]{1,0:T(8,128)(2,1)S(1)}, u32[]{:S(2)}, u32[]{:S(2)}) %collective-permute-start.21) | collective-permute-done | bytes 98336 | tf_op jit(solution)/shard_map/ppermute | solution.py:285
  48.7 0.7 %down.3 = (bf16[48,896]{1,0:T(8,128)(2,1)S(1)}, bf16[48,896]{1,0:T(8,128)(2,1)S(1)}, bf16[48,896]{1,0:T(8,128)(2,1)S(1)}, bf16[48,896]{1,0:T(8,128)(2,1)S(1)}) custom-call(bf16[2,1024,896]{2,1,0:T(8,128)(2,1)S(1)} %stage_down.1.w, bf16[192,256]{1,0:T(8,128)(2,1)S(1)} %hidden.3.refs_0_, bf16[192,256]{1,0:T(8,128)(2,1)S(1)} %collective-permute-done.19.refs_1_, ...), custom_call_target="tpu_custom_call" | custom-call | flops 352321536 | bytes 3670016 | tf_op jit(solution)/shard_map/down/pallas_call | solution.py:413
  49.4 1.0 %collective-permute-start.22 = (bf16[48,896]{1,0:T(8,128)(2,1)S(1)}, bf16[48,896]{1,0:T(8,128)(2,1)S(1)}, u32[]{:S(2)}, u32[]{:S(2)}) collective-permute-start(bf16[48,896]{1,0:T(8,128)(2,1)S(1)} %get-tuple-element.59), channel_id=1, source_target_pairs={{0,2},{1,3},{2,0},{3,1},{4,6},{5,7},{6,4},{7,5},{8,10},{9,11},{10,... | collective-permute-start | bytes 258056 | tf_op jit(solution)/shard_map/ppermute | solution.py:295
  50.4 1.7 %collective-permute-start.9 = (bf16[48,896]{1,0:T(8,128)(2,1)S(1)}, bf16[48,896]{1,0:T(8,128)(2,1)S(1)}, u32[]{:S(2)}, u32[]{:S(2)}) collective-permute-start(bf16[48,896]{1,0:T(8,128)(2,1)S(1)} %get-tuple-element.46), channel_id=1, source_target_pairs={{0,4},{1,5},{2,6},{3,7},{4,0},{5,1},{6,2},{7,3},{8,12},{9,13},{10,... | collective-permute-start | bytes 258056 | tf_op jit(solution)/shard_map/ppermute | solution.py:295
  52.3 0.8 %collective-permute-done.10.refs_3_ = bf16[48,896]{1,0:T(8,128)(2,1)S(1)} collective-permute-done((bf16[48,896]{1,0:T(8,128)(2,1)S(1)}, bf16[48,896]{1,0:T(8,128)(2,1)S(1)}, u32[]{:S(2)}, u32[]{:S(2)}) %collective-permute-start.10) | collective-permute-done | bytes 86048 | tf_op jit(solution)/shard_map/ppermute | solution.py:295
  53.2 2.8 %collective-permute-start.24 = (bf16[48,896]{1,0:T(8,128)(2,1)S(1)}, bf16[48,896]{1,0:T(8,128)(2,1)S(1)}, u32[]{:S(2)}, u32[]{:S(2)}) collective-permute-start(bf16[48,896]{1,0:T(8,128)(2,1)S(1)} %get-tuple-element.61), channel_id=1, source_target_pairs={{0,6},{1,7},{2,4},{3,5},{4,2},{5,3},{6,0},{7,1},{8,14},{9,15},{10,... | collective-permute-start | bytes 258056 | tf_op jit(solution)/shard_map/ppermute | solution.py:295
  56.4 1.3 %weigh.1 = (bf16[128,192]{1,0:T(8,128)(2,1)S(1)}, bf16[128,192]{1,0:T(8,128)(2,1)S(1)}, bf16[128,192]{1,0:T(8,128)(2,1)S(1)}, bf16[128,192]{1,0:T(8,128)(2,1)S(1)}) custom-call(s32[2,4]{1,0:T(2,128)} %bitcast.8, s32[12]{0:T(128)} %cap_in.3, s32[8,128]{1,0:T(8,128)} %bitcast.10, s32[8,128]{1,0:T(8,128)} %bitcast.12, f32[8,128]{1,0:T(8,128)} %bitcast.13), custom_call_target="tpu_custom_call" | custom-call | tf_op jit(solution)/shard_map/weigh/pallas_call | solution.py:340
  58.6 2.1 %collective-permute-done.24.refs_5_ = bf16[48,896]{1,0:T(8,128)(2,1)S(1)} collective-permute-done((bf16[48,896]{1,0:T(8,128)(2,1)S(1)}, bf16[48,896]{1,0:T(8,128)(2,1)S(1)}, u32[]{:S(2)}, u32[]{:S(2)}) %collective-permute-start.24) | collective-permute-done | bytes 86048 | tf_op jit(solution)/shard_map/ppermute | solution.py:295
  60.7 1.9 %collective-permute-done.25.refs_6_ = bf16[48,896]{1,0:T(8,128)(2,1)S(1)} collective-permute-done((bf16[48,896]{1,0:T(8,128)(2,1)S(1)}, bf16[48,896]{1,0:T(8,128)(2,1)S(1)}, u32[]{:S(2)}, u32[]{:S(2)}) %collective-permute-start.25) | collective-permute-done | bytes 86048 | tf_op jit(solution)/shard_map/ppermute | solution.py:295
  62.5 1.0 %combine.3 = bf16[128,896]{1,0:T(8,128)(2,1)} custom-call(f32[128,896]{1,0:T(8,128)S(1)} %combine.2.refs_0_, bf16[128,192]{1,0:T(8,128)(2,1)S(1)} %get-tuple-element.50.refs_1_, bf16[128,192]{1,0:T(8,128)(2,1)S(1)} %get-tuple-element.51.refs_2_, bf16[48,896]{1,0:T(8,128)(2,1)S(1)} %collective-permute-done.22.refs_3_, ...), custom_call_target="tpu_custom_call" | custom-call | tf_op jit(solution)/shard_map/combine/pallas_call | solution.py:429
  (39 shorter events, 6.7 us)
Async XLA Ops:
  1.6 10.7 %collective-permute-start = (bf16[48,896]{1,0:T(8,128)(2,1)S(1)}, bf16[48,896]{1,0:T(8,128)(2,1)S(1)}, u32[]{:S(2)}, u32[]{:S(2)}) collective-permute-start(bf16[48,896]{1,0:T(8,128)(2,1)S(1)} %get-tuple-element.36), channel_id=1, source_target_pairs={{0,4},{1,5},{2,6},{3,7},{4,0},{5,1},{6,2},{7,3},{8,12},{9,13},{10,... | collective-permute-start | bytes 258056 | tf_op jit(solution)/shard_map/ppermute | solution.py:295
  5.7 10.0 %collective-permute-start.1 = (bf16[48,896]{1,0:T(8,128)(2,1)S(1)}, bf16[48,896]{1,0:T(8,128)(2,1)S(1)}, u32[]{:S(2)}, u32[]{:S(2)}) collective-permute-start(bf16[48,896]{1,0:T(8,128)(2,1)S(1)} %get-tuple-element.37), channel_id=1, source_target_pairs={{0,5},{1,4},{2,7},{3,6},{4,1},{5,0},{6,3},{7,2},{8,13},{9,12},{10,... | collective-permute-start | bytes 258056 | tf_op jit(solution)/shard_map/ppermute | solution.py:295
  5.7 11.3 %collective-permute-start.2 = (bf16[48,896]{1,0:T(8,128)(2,1)S(1)}, bf16[48,896]{1,0:T(8,128)(2,1)S(1)}, u32[]{:S(2)}, u32[]{:S(2)}) collective-permute-start(bf16[48,896]{1,0:T(8,128)(2,1)S(1)} %get-tuple-element.38), channel_id=1, source_target_pairs={{0,1},{1,0},{2,3},{3,2},{4,5},{5,4},{6,7},{7,6},{8,9},{9,8},{10,11... | collective-permute-start | bytes 258056 | tf_op jit(solution)/shard_map/ppermute | solution.py:295
  5.9 14.0 %collective-permute-start.12 = (bf16[48,896]{1,0:T(8,128)(2,1)S(1)}, bf16[48,896]{1,0:T(8,128)(2,1)S(1)}, u32[]{:S(2)}, u32[]{:S(2)}) collective-permute-start(bf16[48,896]{1,0:T(8,128)(2,1)S(1)} %get-tuple-element.52), channel_id=1, source_target_pairs={{0,2},{1,3},{2,0},{3,1},{4,6},{5,7},{6,4},{7,5},{8,10},{9,11},{10,... | collective-permute-start | bytes 258056 | tf_op jit(solution)/shard_map/ppermute | solution.py:295
  7.7 13.7 %collective-permute-start.13 = (bf16[48,896]{1,0:T(8,128)(2,1)S(1)}, bf16[48,896]{1,0:T(8,128)(2,1)S(1)}, u32[]{:S(2)}, u32[]{:S(2)}) collective-permute-start(bf16[48,896]{1,0:T(8,128)(2,1)S(1)} %get-tuple-element.53), channel_id=1, source_target_pairs={{0,3},{1,2},{2,1},{3,0},{4,7},{5,6},{6,5},{7,4},{8,11},{9,10},{10,... | collective-permute-start | bytes 258056 | tf_op jit(solution)/shard_map/ppermute | solution.py:295
  12.3 9.6 %collective-permute-start.14 = (bf16[48,896]{1,0:T(8,128)(2,1)S(1)}, bf16[48,896]{1,0:T(8,128)(2,1)S(1)}, u32[]{:S(2)}, u32[]{:S(2)}) collective-permute-start(bf16[48,896]{1,0:T(8,128)(2,1)S(1)} %get-tuple-element.54), channel_id=1, source_target_pairs={{0,6},{1,7},{2,4},{3,5},{4,2},{5,3},{6,0},{7,1},{8,14},{9,15},{10,... | collective-permute-start | bytes 258056 | tf_op jit(solution)/shard_map/ppermute | solution.py:295
  15.7 6.5 %collective-permute-start.15 = (bf16[48,896]{1,0:T(8,128)(2,1)S(1)}, bf16[48,896]{1,0:T(8,128)(2,1)S(1)}, u32[]{:S(2)}, u32[]{:S(2)}) collective-permute-start(bf16[48,896]{1,0:T(8,128)(2,1)S(1)} %get-tuple-element.55), channel_id=1, source_target_pairs={{0,7},{1,6},{2,5},{3,4},{4,3},{5,2},{6,1},{7,0},{8,15},{9,14},{10,... | collective-permute-start | bytes 258056 | tf_op jit(solution)/shard_map/ppermute | solution.py:295
  17.9 8.7 %collective-permute-start.4 = (bf16[192,512]{1,0:T(8,128)(2,1)S(1)}, bf16[192,512]{1,0:T(8,128)(2,1)S(1)}, u32[]{:S(2)}, u32[]{:S(2)}) collective-permute-start(bf16[192,512]{1,0:T(8,128)(2,1)S(1)} %up.11), channel_id=1, source_target_pairs={{0,16},{1,9},{2,18},{3,11},{4,20},{5,13},{6,22},{7,15},{8,24},{9,1... | collective-permute-start | bytes 589832 | tf_op jit(solution)/shard_map/ppermute | solution.py:285
  19.9 12.5 %collective-permute-start.3 = (bf16[192,512]{1,0:T(8,128)(2,1)S(1)}, bf16[192,512]{1,0:T(8,128)(2,1)S(1)}, u32[]{:S(2)}, u32[]{:S(2)}) collective-permute-start(bf16[192,512]{1,0:T(8,128)(2,1)S(1)} %up.10), channel_id=1, source_target_pairs={{0,8},{1,17},{2,10},{3,19},{4,12},{5,21},{6,14},{7,23},{8,0},{9,25... | collective-permute-start | bytes 589832 | tf_op jit(solution)/shard_map/ppermute | solution.py:285
  21.4 11.0 %collective-permute-start.5 = (bf16[192,512]{1,0:T(8,128)(2,1)S(1)}, bf16[192,512]{1,0:T(8,128)(2,1)S(1)}, u32[]{:S(2)}, u32[]{:S(2)}) collective-permute-start(bf16[192,512]{1,0:T(8,128)(2,1)S(1)} %get-tuple-element.45), channel_id=1, source_target_pairs={{0,24},{1,25},{2,26},{3,27},{4,28},{5,29},{6,30},{7,31},{8,16},{9,... | collective-permute-start | bytes 589832 | tf_op jit(solution)/shard_map/ppermute | solution.py:285
  23.0 12.2 %collective-permute-start.17 = (bf16[192,512]{1,0:T(8,128)(2,1)S(1)}, bf16[192,512]{1,0:T(8,128)(2,1)S(1)}, u32[]{:S(2)}, u32[]{:S(2)}) collective-permute-start(bf16[192,512]{1,0:T(8,128)(2,1)S(1)} %up.15), channel_id=1, source_target_pairs={{0,16},{1,9},{2,18},{3,11},{4,20},{5,13},{6,22},{7,15},{8,24},{9,1... | collective-permute-start | bytes 589832 | tf_op jit(solution)/shard_map/ppermute | solution.py:285
  25.0 13.9 %collective-permute-start.16 = (bf16[192,512]{1,0:T(8,128)(2,1)S(1)}, bf16[192,512]{1,0:T(8,128)(2,1)S(1)}, u32[]{:S(2)}, u32[]{:S(2)}) collective-permute-start(bf16[192,512]{1,0:T(8,128)(2,1)S(1)} %up.14), channel_id=1, source_target_pairs={{0,8},{1,17},{2,10},{3,19},{4,12},{5,21},{6,14},{7,23},{8,0},{9,25... | collective-permute-start | bytes 589832 | tf_op jit(solution)/shard_map/ppermute | solution.py:285
  26.6 13.6 %collective-permute-start.18 = (bf16[192,512]{1,0:T(8,128)(2,1)S(1)}, bf16[192,512]{1,0:T(8,128)(2,1)S(1)}, u32[]{:S(2)}, u32[]{:S(2)}) collective-permute-start(bf16[192,512]{1,0:T(8,128)(2,1)S(1)} %get-tuple-element.58), channel_id=1, source_target_pairs={{0,24},{1,25},{2,26},{3,27},{4,28},{5,29},{6,30},{7,31},{8,16},{9,... | collective-permute-start | bytes 589832 | tf_op jit(solution)/shard_map/ppermute | solution.py:285
  32.6 10.6 %collective-permute-start.6 = (bf16[192,256]{1,0:T(8,128)(2,1)S(1)}, bf16[192,256]{1,0:T(8,128)(2,1)S(1)}, u32[]{:S(2)}, u32[]{:S(2)}) collective-permute-start(bf16[192,256]{1,0:T(8,128)(2,1)S(1)} %hidden.2.refs_0_), channel_id=1, source_target_pairs={{0,8},{1,17},{2,10},{3,19},{4,12},{5,21},{6,14},{7,23},{8,0},{9,25... | collective-permute-start | bytes 294920 | tf_op jit(solution)/shard_map/ppermute | solution.py:285
  33.6 12.7 %collective-permute-start.7 = (bf16[192,256]{1,0:T(8,128)(2,1)S(1)}, bf16[192,256]{1,0:T(8,128)(2,1)S(1)}, u32[]{:S(2)}, u32[]{:S(2)}) collective-permute-start(bf16[192,256]{1,0:T(8,128)(2,1)S(1)} %hidden.2.refs_0_), channel_id=1, source_target_pairs={{0,16},{1,9},{2,18},{3,11},{4,20},{5,13},{6,22},{7,15},{8,24},{9,1... | collective-permute-start | bytes 294920 | tf_op jit(solution)/shard_map/ppermute | solution.py:285
  35.2 11.2 %collective-permute-start.8 = (bf16[192,256]{1,0:T(8,128)(2,1)S(1)}, bf16[192,256]{1,0:T(8,128)(2,1)S(1)}, u32[]{:S(2)}, u32[]{:S(2)}) collective-permute-start(bf16[192,256]{1,0:T(8,128)(2,1)S(1)} %hidden.2.refs_0_), channel_id=1, source_target_pairs={{0,24},{1,25},{2,26},{3,27},{4,28},{5,29},{6,30},{7,31},{8,16},{9,... | collective-permute-start | bytes 294920 | tf_op jit(solution)/shard_map/ppermute | solution.py:285
  40.3 7.2 %collective-permute-start.19 = (bf16[192,256]{1,0:T(8,128)(2,1)S(1)}, bf16[192,256]{1,0:T(8,128)(2,1)S(1)}, u32[]{:S(2)}, u32[]{:S(2)}) collective-permute-start(bf16[192,256]{1,0:T(8,128)(2,1)S(1)} %hidden.3.refs_0_), channel_id=1, source_target_pairs={{0,8},{1,17},{2,10},{3,19},{4,12},{5,21},{6,14},{7,23},{8,0},{9,25... | collective-permute-start | bytes 294920 | tf_op jit(solution)/shard_map/ppermute | solution.py:285
  42.1 5.5 %collective-permute-start.20 = (bf16[192,256]{1,0:T(8,128)(2,1)S(1)}, bf16[192,256]{1,0:T(8,128)(2,1)S(1)}, u32[]{:S(2)}, u32[]{:S(2)}) collective-permute-start(bf16[192,256]{1,0:T(8,128)(2,1)S(1)} %hidden.3.refs_0_), channel_id=1, source_target_pairs={{0,16},{1,9},{2,18},{3,11},{4,20},{5,13},{6,22},{7,15},{8,24},{9,1... | collective-permute-start | bytes 294920 | tf_op jit(solution)/shard_map/ppermute | solution.py:285
  43.2 5.5 %collective-permute-start.21 = (bf16[192,256]{1,0:T(8,128)(2,1)S(1)}, bf16[192,256]{1,0:T(8,128)(2,1)S(1)}, u32[]{:S(2)}, u32[]{:S(2)}) collective-permute-start(bf16[192,256]{1,0:T(8,128)(2,1)S(1)} %hidden.3.refs_0_), channel_id=1, source_target_pairs={{0,24},{1,25},{2,26},{3,27},{4,28},{5,29},{6,30},{7,31},{8,16},{9,... | collective-permute-start | bytes 294920 | tf_op jit(solution)/shard_map/ppermute | solution.py:285
  47.1 6.1 %collective-permute-start.10 = (bf16[48,896]{1,0:T(8,128)(2,1)S(1)}, bf16[48,896]{1,0:T(8,128)(2,1)S(1)}, u32[]{:S(2)}, u32[]{:S(2)}) collective-permute-start(bf16[48,896]{1,0:T(8,128)(2,1)S(1)} %get-tuple-element.47), channel_id=1, source_target_pairs={{0,5},{1,4},{2,7},{3,6},{4,1},{5,0},{6,3},{7,2},{8,13},{9,12},{10,... | collective-permute-start | bytes 258056 | tf_op jit(solution)/shard_map/ppermute | solution.py:295
  47.2 8.7 %collective-permute-start.11 = (bf16[48,896]{1,0:T(8,128)(2,1)S(1)}, bf16[48,896]{1,0:T(8,128)(2,1)S(1)}, u32[]{:S(2)}, u32[]{:S(2)}) collective-permute-start(bf16[48,896]{1,0:T(8,128)(2,1)S(1)} %get-tuple-element.48), channel_id=1, source_target_pairs={{0,1},{1,0},{2,3},{3,2},{4,5},{5,4},{6,7},{7,6},{8,9},{9,8},{10,11... | collective-permute-start | bytes 258056 | tf_op jit(solution)/shard_map/ppermute | solution.py:295
  49.4 8.6 %collective-permute-start.22 = (bf16[48,896]{1,0:T(8,128)(2,1)S(1)}, bf16[48,896]{1,0:T(8,128)(2,1)S(1)}, u32[]{:S(2)}, u32[]{:S(2)}) collective-permute-start(bf16[48,896]{1,0:T(8,128)(2,1)S(1)} %get-tuple-element.59), channel_id=1, source_target_pairs={{0,2},{1,3},{2,0},{3,1},{4,6},{5,7},{6,4},{7,5},{8,10},{9,11},{10,... | collective-permute-start | bytes 258056 | tf_op jit(solution)/shard_map/ppermute | solution.py:295
  50.4 7.3 %collective-permute-start.9 = (bf16[48,896]{1,0:T(8,128)(2,1)S(1)}, bf16[48,896]{1,0:T(8,128)(2,1)S(1)}, u32[]{:S(2)}, u32[]{:S(2)}) collective-permute-start(bf16[48,896]{1,0:T(8,128)(2,1)S(1)} %get-tuple-element.46), channel_id=1, source_target_pairs={{0,4},{1,5},{2,6},{3,7},{4,0},{5,1},{6,2},{7,3},{8,12},{9,13},{10,... | collective-permute-start | bytes 258056 | tf_op jit(solution)/shard_map/ppermute | solution.py:295
  52.0 6.5 %collective-permute-start.23 = (bf16[48,896]{1,0:T(8,128)(2,1)S(1)}, bf16[48,896]{1,0:T(8,128)(2,1)S(1)}, u32[]{:S(2)}, u32[]{:S(2)}) collective-permute-start(bf16[48,896]{1,0:T(8,128)(2,1)S(1)} %get-tuple-element.60), channel_id=1, source_target_pairs={{0,3},{1,2},{2,1},{3,0},{4,7},{5,6},{6,5},{7,4},{8,11},{9,10},{10,... | collective-permute-start | bytes 258056 | tf_op jit(solution)/shard_map/ppermute | solution.py:295
  53.2 7.5 %collective-permute-start.24 = (bf16[48,896]{1,0:T(8,128)(2,1)S(1)}, bf16[48,896]{1,0:T(8,128)(2,1)S(1)}, u32[]{:S(2)}, u32[]{:S(2)}) collective-permute-start(bf16[48,896]{1,0:T(8,128)(2,1)S(1)} %get-tuple-element.61), channel_id=1, source_target_pairs={{0,6},{1,7},{2,4},{3,5},{4,2},{5,3},{6,0},{7,1},{8,14},{9,15},{10,... | collective-permute-start | bytes 258056 | tf_op jit(solution)/shard_map/ppermute | solution.py:295
  55.9 6.6 %collective-permute-start.25 = (bf16[48,896]{1,0:T(8,128)(2,1)S(1)}, bf16[48,896]{1,0:T(8,128)(2,1)S(1)}, u32[]{:S(2)}, u32[]{:S(2)}) collective-permute-start(bf16[48,896]{1,0:T(8,128)(2,1)S(1)} %get-tuple-element.62), channel_id=1, source_target_pairs={{0,7},{1,6},{2,5},{3,4},{4,3},{5,2},{6,1},{7,0},{8,15},{9,14},{10,... | collective-permute-start | bytes 258056 | tf_op jit(solution)/shard_map/ppermute | solution.py:295

commit v4 on v3

--- a/solution.py
+++ b/solution.py
@@ -287,7 +287,7 @@
 
 def exchange(pieces, chunks, axis):
     n = len(pieces)
-    if n > DIRECT_LIMIT:
+    if not direct(n):
         moved = lax.all_to_all(jnp.stack(pieces), axis, split_axis=0, concat_axis=0, tiled=True)
         return [moved[i] for i in range(n)]
     moved = []
@@ -296,10 +296,15 @@
     return moved
 
 
+def direct(experts):
+    return experts <= DIRECT_LIMIT and experts & (experts - 1) == 0
+
+
 def chunks_of(experts):
-    if experts == 8:
-        return ((4, 5, 1, 0), (2, 3, 6, 7))
-    return (tuple(range(experts)),)
+    if experts < 4 or not direct(experts):
+        return (tuple(range(experts)),)
+    near = [j for j in range(2, experts) if not j & 2]
+    return (tuple(near + [1, 0]), tuple(j for j in range(experts) if j & 2))
 
 
 def on_device(
@@ -318,7 +323,7 @@
     sds = jax.ShapeDtypeStruct
     hbm = pl.BlockSpec(memory_space=pltpu.HBM)
     top = expert_ids.shape[1]
-    sizes = (experts, hot, room, half, room_a, room_b, experts <= DIRECT_LIMIT)
+    sizes = (experts, hot, room, half, room_a, room_b, direct(experts))
     small = [placement.T, capacity, expert_ids.T, replica_choice.T]
     small_scratch = [
         pltpu.SMEM((2, hot), I32),

time: 63.8 us -> 63.8 us (level)
  no operation moved by 1% of the time
where the time goes in v4:
time: 63.8 us; the launch traced here: 63.5 us
  starting transfers between devices  37.1 us (58%)
  Pallas kernels  16.4 us (26%)
  waiting for transfers between devices  9.74 us (15%)
    ppermute x12, starting transfers between devices, to_partner(): return lax.ppermute(x, ('dp', 'expert'), pairs)  19.8 us
    ppermute x14, starting transfers between devices, exchange(): moved.append(lax.ppermute(piece, axis, flips(n, j)) if j else piece)  17.3 us
    ppermute x14, waiting for transfers between devices, exchange(): moved.append(lax.ppermute(piece, axis, flips(n, j)) if j else piece)  7.24 us
    pallas_call x2, Pallas kernels, on_device(): pl.pallas_call(functools.partial(stage_kernel, parts, ks), out_shape=[sds...  4.87 us
    pallas_call x8, Pallas kernels, on_device(): pl.pallas_call(up_next_kernel if i else functools.partial(up_first_kernel...  3.42 us
    ppermute x12, waiting for transfers between devices, to_partner(): return lax.ppermute(x, ('dp', 'expert'), pairs)  2.5 us
    pallas_call x1, Pallas kernels, on_device(): pl.pallas_call(functools.partial(stage_down_kernel, parts), out_shape=sds...  2.34 us
    pallas_call x1, Pallas kernels, on_device(): pl.pallas_call(functools.partial(route_kernel, sizes, chunks), out_shape=...  1.57 us
  transfers between devices with their start and end apart: 26, of which 9 were waited for; matrix products, arithmetic and copies ran while one was open for 0% of the time, Pallas kernels for 22%

profile of v4, /device:TPU:0, one launch (start us, length us, event | category | flops | bytes accessed | tf_op | source)
XLA Modules:
  0.0 63.5 jit_solution(2884470135213441542)
XLA Ops:
  0.0 1.6 %route.1 = (bf16[48,896]{1,0:T(8,128)(2,1)S(1)}, bf16[48,896]{1,0:T(8,128)(2,1)S(1)}, bf16[48,896]{1,0:T(8,128)(2,1)S(1)}, bf16[48,896]{1,0:T(8,128)(2,1)S(1)}, ...) custom-call(s32[2,4]{1,0:T(2,128)} %bitcast.4, ...), custom_call_target="tpu_custom_call" | custom-call | tf_op jit(solution)/shard_map/route/pallas_call | solution.py:334
  1.6 4.1 %collective-permute-start = (bf16[48,896]{1,0:T(8,128)(2,1)S(1)}, bf16[48,896]{1,0:T(8,128)(2,1)S(1)}, u32[]{:S(2)}, u32[]{:S(2)}) collective-permute-start(bf16[48,896]{1,0:T(8,128)(2,1)S(1)} %get-tuple-element.36), channel_id=1, source_target_pairs={{0,4},{1,5},{2,6},{3,7},{4,0},{5,1},{6,2},{7,3},{8,12},{9,13},{10,... | collective-permute-start | bytes 258056 | tf_op jit(solution)/shard_map/ppermute | solution.py:295
  5.9 1.8 %collective-permute-start.12 = (bf16[48,896]{1,0:T(8,128)(2,1)S(1)}, bf16[48,896]{1,0:T(8,128)(2,1)S(1)}, u32[]{:S(2)}, u32[]{:S(2)}) collective-permute-start(bf16[48,896]{1,0:T(8,128)(2,1)S(1)} %get-tuple-element.52), channel_id=1, source_target_pairs={{0,2},{1,3},{2,0},{3,1},{4,6},{5,7},{6,4},{7,5},{8,10},{9,11},{10,... | collective-permute-start | bytes 258056 | tf_op jit(solution)/shard_map/ppermute | solution.py:295
  7.7 2.9 %shard_map.91 = (bf16[2,896,512]{2,1,0:T(8,128)(2,1)S(1)}, bf16[2,896,512]{2,1,0:T(8,128)(2,1)S(1)}, bf16[2,896,512]{2,1,0:T(8,128)(2,1)S(1)}) custom-call(s32[2,4]{1,0:T(2,128)} %bitcast.5, bf16[1,2,896,1024]{3,2,1,0:T(8,128)(2,1)} %w_gate.3, bf16[1,2,896,1024]{3,2,1,0:T(8,128)(2,1)} %w_up.3), custom_call_target="tpu_custom_call" | custom-call | bytes 11010048 | tf_op jit(solution)/shard_map/pallas_call | solution.py:361
  10.6 1.7 %collective-permute-done.refs_0_ = bf16[48,896]{1,0:T(8,128)(2,1)S(1)} collective-permute-done((bf16[48,896]{1,0:T(8,128)(2,1)S(1)}, bf16[48,896]{1,0:T(8,128)(2,1)S(1)}, u32[]{:S(2)}, u32[]{:S(2)}) %collective-permute-start) | collective-permute-done | bytes 86048 | tf_op jit(solution)/shard_map/ppermute | solution.py:295
  12.3 3.3 %collective-permute-start.14 = (bf16[48,896]{1,0:T(8,128)(2,1)S(1)}, bf16[48,896]{1,0:T(8,128)(2,1)S(1)}, u32[]{:S(2)}, u32[]{:S(2)}) collective-permute-start(bf16[48,896]{1,0:T(8,128)(2,1)S(1)} %get-tuple-element.54), channel_id=1, source_target_pairs={{0,6},{1,7},{2,4},{3,5},{4,2},{5,3},{6,0},{7,1},{8,14},{9,15},{10,... | collective-permute-start | bytes 258056 | tf_op jit(solution)/shard_map/ppermute | solution.py:295
  15.7 1.3 %collective-permute-start.15 = (bf16[48,896]{1,0:T(8,128)(2,1)S(1)}, bf16[48,896]{1,0:T(8,128)(2,1)S(1)}, u32[]{:S(2)}, u32[]{:S(2)}) collective-permute-start(bf16[48,896]{1,0:T(8,128)(2,1)S(1)} %get-tuple-element.55), channel_id=1, source_target_pairs={{0,7},{1,6},{2,5},{3,4},{4,3},{5,2},{6,1},{7,0},{8,15},{9,14},{10,... | collective-permute-start | bytes 258056 | tf_op jit(solution)/shard_map/ppermute | solution.py:295
  17.9 1.6 %collective-permute-start.4 = (bf16[192,512]{1,0:T(8,128)(2,1)S(1)}, bf16[192,512]{1,0:T(8,128)(2,1)S(1)}, u32[]{:S(2)}, u32[]{:S(2)}) collective-permute-start(bf16[192,512]{1,0:T(8,128)(2,1)S(1)} %up.11), channel_id=1, source_target_pairs={{0,16},{1,9},{2,18},{3,11},{4,20},{5,13},{6,22},{7,15},{8,24},{9,1... | collective-permute-start | bytes 589832 | tf_op jit(solution)/shard_map/ppermute | solution.py:285
  19.9 1.6 %collective-permute-start.3 = (bf16[192,512]{1,0:T(8,128)(2,1)S(1)}, bf16[192,512]{1,0:T(8,128)(2,1)S(1)}, u32[]{:S(2)}, u32[]{:S(2)}) collective-permute-start(bf16[192,512]{1,0:T(8,128)(2,1)S(1)} %up.10), channel_id=1, source_target_pairs={{0,8},{1,17},{2,10},{3,19},{4,12},{5,21},{6,14},{7,23},{8,0},{9,25... | collective-permute-start | bytes 589832 | tf_op jit(solution)/shard_map/ppermute | solution.py:285
  23.0 1.6 %collective-permute-start.17 = (bf16[192,512]{1,0:T(8,128)(2,1)S(1)}, bf16[192,512]{1,0:T(8,128)(2,1)S(1)}, u32[]{:S(2)}, u32[]{:S(2)}) collective-permute-start(bf16[192,512]{1,0:T(8,128)(2,1)S(1)} %up.15), channel_id=1, source_target_pairs={{0,16},{1,9},{2,18},{3,11},{4,20},{5,13},{6,22},{7,15},{8,24},{9,1... | collective-permute-start | bytes 589832 | tf_op jit(solution)/shard_map/ppermute | solution.py:285
  25.0 1.6 %collective-permute-start.16 = (bf16[192,512]{1,0:T(8,128)(2,1)S(1)}, bf16[192,512]{1,0:T(8,128)(2,1)S(1)}, u32[]{:S(2)}, u32[]{:S(2)}) collective-permute-start(bf16[192,512]{1,0:T(8,128)(2,1)S(1)} %up.14), channel_id=1, source_target_pairs={{0,8},{1,17},{2,10},{3,19},{4,12},{5,21},{6,14},{7,23},{8,0},{9,25... | collective-permute-start | bytes 589832 | tf_op jit(solution)/shard_map/ppermute | solution.py:285
  26.6 3.4 %collective-permute-start.18 = (bf16[192,512]{1,0:T(8,128)(2,1)S(1)}, bf16[192,512]{1,0:T(8,128)(2,1)S(1)}, u32[]{:S(2)}, u32[]{:S(2)}) collective-permute-start(bf16[192,512]{1,0:T(8,128)(2,1)S(1)} %get-tuple-element.58), channel_id=1, source_target_pairs={{0,24},{1,25},{2,26},{3,27},{4,28},{5,29},{6,30},{7,31},{8,16},{9,... | collective-permute-start | bytes 589832 | tf_op jit(solution)/shard_map/ppermute | solution.py:285
  30.0 2.0 %shard_map.92.weights = bf16[2,896,512]{2,1,0:T(8,128)(2,1)S(1)} custom-call(s32[2,4]{1,0:T(2,128)} %bitcast.6, bf16[1,2,896,1024]{3,2,1,0:T(8,128)(2,1)} %w_gate.3, bf16[1,2,896,1024]{3,2,1,0:T(8,128)(2,1)} %w_up.3), custom_call_target="tpu_custom_call" | custom-call | bytes 3670016 | tf_op jit(solution)/shard_map/pallas_call | solution.py:361
  32.6 1.0 %collective-permute-start.6 = (bf16[192,256]{1,0:T(8,128)(2,1)S(1)}, bf16[192,256]{1,0:T(8,128)(2,1)S(1)}, u32[]{:S(2)}, u32[]{:S(2)}) collective-permute-start(bf16[192,256]{1,0:T(8,128)(2,1)S(1)} %hidden.2.refs_0_), channel_id=1, source_target_pairs={{0,8},{1,17},{2,10},{3,19},{4,12},{5,21},{6,14},{7,23},{8,0},{9,25... | collective-permute-start | bytes 294920 | tf_op jit(solution)/shard_map/ppermute | solution.py:285
  33.6 1.6 %collective-permute-start.7 = (bf16[192,256]{1,0:T(8,128)(2,1)S(1)}, bf16[192,256]{1,0:T(8,128)(2,1)S(1)}, u32[]{:S(2)}, u32[]{:S(2)}) collective-permute-start(bf16[192,256]{1,0:T(8,128)(2,1)S(1)} %hidden.2.refs_0_), channel_id=1, source_target_pairs={{0,16},{1,9},{2,18},{3,11},{4,20},{5,13},{6,22},{7,15},{8,24},{9,1... | collective-permute-start | bytes 294920 | tf_op jit(solution)/shard_map/ppermute | solution.py:285
  35.2 3.3 %collective-permute-start.8 = (bf16[192,256]{1,0:T(8,128)(2,1)S(1)}, bf16[192,256]{1,0:T(8,128)(2,1)S(1)}, u32[]{:S(2)}, u32[]{:S(2)}) collective-permute-start(bf16[192,256]{1,0:T(8,128)(2,1)S(1)} %hidden.2.refs_0_), channel_id=1, source_target_pairs={{0,24},{1,25},{2,26},{3,27},{4,28},{5,29},{6,30},{7,31},{8,16},{9,... | collective-permute-start | bytes 294920 | tf_op jit(solution)/shard_map/ppermute | solution.py:285
  38.9 1.3 %collective-permute-done.18.refs_2_ = bf16[192,512]{1,0:T(8,128)(2,1)S(1)} collective-permute-done((bf16[192,512]{1,0:T(8,128)(2,1)S(1)}, bf16[192,512]{1,0:T(8,128)(2,1)S(1)}, u32[]{:S(2)}, u32[]{:S(2)}) %collective-permute-start.18) | collective-permute-done | bytes 196640 | tf_op jit(solution)/shard_map/ppermute | solution.py:285
  40.3 1.8 %collective-permute-start.19 = (bf16[192,256]{1,0:T(8,128)(2,1)S(1)}, bf16[192,256]{1,0:T(8,128)(2,1)S(1)}, u32[]{:S(2)}, u32[]{:S(2)}) collective-permute-start(bf16[192,256]{1,0:T(8,128)(2,1)S(1)} %hidden.3.refs_0_), channel_id=1, source_target_pairs={{0,8},{1,17},{2,10},{3,19},{4,12},{5,21},{6,14},{7,23},{8,0},{9,25... | collective-permute-start | bytes 294920 | tf_op jit(solution)/shard_map/ppermute | solution.py:285
  42.1 1.1 %collective-permute-start.20 = (bf16[192,256]{1,0:T(8,128)(2,1)S(1)}, bf16[192,256]{1,0:T(8,128)(2,1)S(1)}, u32[]{:S(2)}, u32[]{:S(2)}) collective-permute-start(bf16[192,256]{1,0:T(8,128)(2,1)S(1)} %hidden.3.refs_0_), channel_id=1, source_target_pairs={{0,16},{1,9},{2,18},{3,11},{4,20},{5,13},{6,22},{7,15},{8,24},{9,1... | collective-permute-start | bytes 294920 | tf_op jit(solution)/shard_map/ppermute | solution.py:285
  43.2 0.8 %collective-permute-start.21 = (bf16[192,256]{1,0:T(8,128)(2,1)S(1)}, bf16[192,256]{1,0:T(8,128)(2,1)S(1)}, u32[]{:S(2)}, u32[]{:S(2)}) collective-permute-start(bf16[192,256]{1,0:T(8,128)(2,1)S(1)} %hidden.3.refs_0_), channel_id=1, source_target_pairs={{0,24},{1,25},{2,26},{3,27},{4,28},{5,29},{6,30},{7,31},{8,16},{9,... | collective-permute-start | bytes 294920 | tf_op jit(solution)/shard_map/ppermute | solution.py:285
  44.0 2.3 %stage_down.1.w = bf16[2,1024,896]{2,1,0:T(8,128)(2,1)S(1)} custom-call(s32[2,4]{1,0:T(2,128)} %bitcast.7, bf16[1,2,1024,896]{3,2,1,0:T(8,128)(2,1)} %w_down.1), custom_call_target="tpu_custom_call" | custom-call | bytes 7340032 | tf_op jit(solution)/shard_map/stage_down/pallas_call | solution.py:371
  46.4 0.7 %down.2 = (bf16[48,896]{1,0:T(8,128)(2,1)S(1)}, bf16[48,896]{1,0:T(8,128)(2,1)S(1)}, bf16[48,896]{1,0:T(8,128)(2,1)S(1)}, bf16[48,896]{1,0:T(8,128)(2,1)S(1)}) custom-call(bf16[2,1024,896]{2,1,0:T(8,128)(2,1)S(1)} %stage_down.1.w, bf16[192,256]{1,0:T(8,128)(2,1)S(1)} %hidden.2.refs_0_, bf16[192,256]{1,0:T(8,128)(2,1)S(1)} %collective-permute-done.6.refs_1_, ...), custom_call_target="tpu_custom_call" | custom-call | flops 352321536 | bytes 3670016 | tf_op jit(solution)/shard_map/down/pallas_call | solution.py:418
  47.6 1.1 %collective-permute-done.21.refs_3_ = bf16[192,256]{1,0:T(8,128)(2,1)S(1)} collective-permute-done((bf16[192,256]{1,0:T(8,128)(2,1)S(1)}, bf16[192,256]{1,0:T(8,128)(2,1)S(1)}, u32[]{:S(2)}, u32[]{:S(2)}) %collective-permute-start.21) | collective-permute-done | bytes 98336 | tf_op jit(solution)/shard_map/ppermute | solution.py:285
  48.7 0.7 %down.3 = (bf16[48,896]{1,0:T(8,128)(2,1)S(1)}, bf16[48,896]{1,0:T(8,128)(2,1)S(1)}, bf16[48,896]{1,0:T(8,128)(2,1)S(1)}, bf16[48,896]{1,0:T(8,128)(2,1)S(1)}) custom-call(bf16[2,1024,896]{2,1,0:T(8,128)(2,1)S(1)} %stage_down.1.w, bf16[192,256]{1,0:T(8,128)(2,1)S(1)} %hidden.3.refs_0_, bf16[192,256]{1,0:T(8,128)(2,1)S(1)} %collective-permute-done.19.refs_1_, ...), custom_call_target="tpu_custom_call" | custom-call | flops 352321536 | bytes 3670016 | tf_op jit(solution)/shard_map/down/pallas_call | solution.py:418
  49.4 1.0 %collective-permute-start.22 = (bf16[48,896]{1,0:T(8,128)(2,1)S(1)}, bf16[48,896]{1,0:T(8,128)(2,1)S(1)}, u32[]{:S(2)}, u32[]{:S(2)}) collective-permute-start(bf16[48,896]{1,0:T(8,128)(2,1)S(1)} %get-tuple-element.59), channel_id=1, source_target_pairs={{0,2},{1,3},{2,0},{3,1},{4,6},{5,7},{6,4},{7,5},{8,10},{9,11},{10,... | collective-permute-start | bytes 258056 | tf_op jit(solution)/shard_map/ppermute | solution.py:295
  50.4 1.7 %collective-permute-start.9 = (bf16[48,896]{1,0:T(8,128)(2,1)S(1)}, bf16[48,896]{1,0:T(8,128)(2,1)S(1)}, u32[]{:S(2)}, u32[]{:S(2)}) collective-permute-start(bf16[48,896]{1,0:T(8,128)(2,1)S(1)} %get-tuple-element.46), channel_id=1, source_target_pairs={{0,4},{1,5},{2,6},{3,7},{4,0},{5,1},{6,2},{7,3},{8,12},{9,13},{10,... | collective-permute-start | bytes 258056 | tf_op jit(solution)/shard_map/ppermute | solution.py:295
  52.3 0.8 %collective-permute-done.10.refs_3_ = bf16[48,896]{1,0:T(8,128)(2,1)S(1)} collective-permute-done((bf16[48,896]{1,0:T(8,128)(2,1)S(1)}, bf16[48,896]{1,0:T(8,128)(2,1)S(1)}, u32[]{:S(2)}, u32[]{:S(2)}) %collective-permute-start.10) | collective-permute-done | bytes 86048 | tf_op jit(solution)/shard_map/ppermute | solution.py:295
  53.2 2.8 %collective-permute-start.24 = (bf16[48,896]{1,0:T(8,128)(2,1)S(1)}, bf16[48,896]{1,0:T(8,128)(2,1)S(1)}, u32[]{:S(2)}, u32[]{:S(2)}) collective-permute-start(bf16[48,896]{1,0:T(8,128)(2,1)S(1)} %get-tuple-element.61), channel_id=1, source_target_pairs={{0,6},{1,7},{2,4},{3,5},{4,2},{5,3},{6,0},{7,1},{8,14},{9,15},{10,... | collective-permute-start | bytes 258056 | tf_op jit(solution)/shard_map/ppermute | solution.py:295
  56.4 1.3 %weigh.1 = (bf16[128,192]{1,0:T(8,128)(2,1)S(1)}, bf16[128,192]{1,0:T(8,128)(2,1)S(1)}, bf16[128,192]{1,0:T(8,128)(2,1)S(1)}, bf16[128,192]{1,0:T(8,128)(2,1)S(1)}) custom-call(s32[2,4]{1,0:T(2,128)} %bitcast.8, s32[12]{0:T(128)} %cap_in.3, s32[8,128]{1,0:T(8,128)} %bitcast.10, s32[8,128]{1,0:T(8,128)} %bitcast.12, f32[8,128]{1,0:T(8,128)} %bitcast.13), custom_call_target="tpu_custom_call" | custom-call | tf_op jit(solution)/shard_map/weigh/pallas_call | solution.py:345
  58.6 2.1 %collective-permute-done.24.refs_5_ = bf16[48,896]{1,0:T(8,128)(2,1)S(1)} collective-permute-done((bf16[48,896]{1,0:T(8,128)(2,1)S(1)}, bf16[48,896]{1,0:T(8,128)(2,1)S(1)}, u32[]{:S(2)}, u32[]{:S(2)}) %collective-permute-start.24) | collective-permute-done | bytes 86048 | tf_op jit(solution)/shard_map/ppermute | solution.py:295
  60.7 1.9 %collective-permute-done.25.refs_6_ = bf16[48,896]{1,0:T(8,128)(2,1)S(1)} collective-permute-done((bf16[48,896]{1,0:T(8,128)(2,1)S(1)}, bf16[48,896]{1,0:T(8,128)(2,1)S(1)}, u32[]{:S(2)}, u32[]{:S(2)}) %collective-permute-start.25) | collective-permute-done | bytes 86048 | tf_op jit(solution)/shard_map/ppermute | solution.py:295
  62.5 1.0 %combine.3 = bf16[128,896]{1,0:T(8,128)(2,1)} custom-call(f32[128,896]{1,0:T(8,128)S(1)} %combine.2.refs_0_, bf16[128,192]{1,0:T(8,128)(2,1)S(1)} %get-tuple-element.50.refs_1_, bf16[128,192]{1,0:T(8,128)(2,1)S(1)} %get-tuple-element.51.refs_2_, bf16[48,896]{1,0:T(8,128)(2,1)S(1)} %collective-permute-done.22.refs_3_, ...), custom_call_target="tpu_custom_call" | custom-call | tf_op jit(solution)/shard_map/combine/pallas_call | solution.py:434
  (39 shorter events, 6.7 us)
Async XLA Ops:
  1.6 10.7 %collective-permute-start = (bf16[48,896]{1,0:T(8,128)(2,1)S(1)}, bf16[48,896]{1,0:T(8,128)(2,1)S(1)}, u32[]{:S(2)}, u32[]{:S(2)}) collective-permute-start(bf16[48,896]{1,0:T(8,128)(2,1)S(1)} %get-tuple-element.36), channel_id=1, source_target_pairs={{0,4},{1,5},{2,6},{3,7},{4,0},{5,1},{6,2},{7,3},{8,12},{9,13},{10,... | collective-permute-start | bytes 258056 | tf_op jit(solution)/shard_map/ppermute | solution.py:295
  5.7 10.0 %collective-permute-start.1 = (bf16[48,896]{1,0:T(8,128)(2,1)S(1)}, bf16[48,896]{1,0:T(8,128)(2,1)S(1)}, u32[]{:S(2)}, u32[]{:S(2)}) collective-permute-start(bf16[48,896]{1,0:T(8,128)(2,1)S(1)} %get-tuple-element.37), channel_id=1, source_target_pairs={{0,5},{1,4},{2,7},{3,6},{4,1},{5,0},{6,3},{7,2},{8,13},{9,12},{10,... | collective-permute-start | bytes 258056 | tf_op jit(solution)/shard_map/ppermute | solution.py:295
  5.7 11.3 %collective-permute-start.2 = (bf16[48,896]{1,0:T(8,128)(2,1)S(1)}, bf16[48,896]{1,0:T(8,128)(2,1)S(1)}, u32[]{:S(2)}, u32[]{:S(2)}) collective-permute-start(bf16[48,896]{1,0:T(8,128)(2,1)S(1)} %get-tuple-element.38), channel_id=1, source_target_pairs={{0,1},{1,0},{2,3},{3,2},{4,5},{5,4},{6,7},{7,6},{8,9},{9,8},{10,11... | collective-permute-start | bytes 258056 | tf_op jit(solution)/shard_map/ppermute | solution.py:295
  5.9 14.0 %collective-permute-start.12 = (bf16[48,896]{1,0:T(8,128)(2,1)S(1)}, bf16[48,896]{1,0:T(8,128)(2,1)S(1)}, u32[]{:S(2)}, u32[]{:S(2)}) collective-permute-start(bf16[48,896]{1,0:T(8,128)(2,1)S(1)} %get-tuple-element.52), channel_id=1, source_target_pairs={{0,2},{1,3},{2,0},{3,1},{4,6},{5,7},{6,4},{7,5},{8,10},{9,11},{10,... | collective-permute-start | bytes 258056 | tf_op jit(solution)/shard_map/ppermute | solution.py:295
  7.7 13.7 %collective-permute-start.13 = (bf16[48,896]{1,0:T(8,128)(2,1)S(1)}, bf16[48,896]{1,0:T(8,128)(2,1)S(1)}, u32[]{:S(2)}, u32[]{:S(2)}) collective-permute-start(bf16[48,896]{1,0:T(8,128)(2,1)S(1)} %get-tuple-element.53), channel_id=1, source_target_pairs={{0,3},{1,2},{2,1},{3,0},{4,7},{5,6},{6,5},{7,4},{8,11},{9,10},{10,... | collective-permute-start | bytes 258056 | tf_op jit(solution)/shard_map/ppermute | solution.py:295
  12.3 9.6 %collective-permute-start.14 = (bf16[48,896]{1,0:T(8,128)(2,1)S(1)}, bf16[48,896]{1,0:T(8,128)(2,1)S(1)}, u32[]{:S(2)}, u32[]{:S(2)}) collective-permute-start(bf16[48,896]{1,0:T(8,128)(2,1)S(1)} %get-tuple-element.54), channel_id=1, source_target_pairs={{0,6},{1,7},{2,4},{3,5},{4,2},{5,3},{6,0},{7,1},{8,14},{9,15},{10,... | collective-permute-start | bytes 258056 | tf_op jit(solution)/shard_map/ppermute | solution.py:295
  15.7 6.5 %collective-permute-start.15 = (bf16[48,896]{1,0:T(8,128)(2,1)S(1)}, bf16[48,896]{1,0:T(8,128)(2,1)S(1)}, u32[]{:S(2)}, u32[]{:S(2)}) collective-permute-start(bf16[48,896]{1,0:T(8,128)(2,1)S(1)} %get-tuple-element.55), channel_id=1, source_target_pairs={{0,7},{1,6},{2,5},{3,4},{4,3},{5,2},{6,1},{7,0},{8,15},{9,14},{10,... | collective-permute-start | bytes 258056 | tf_op jit(solution)/shard_map/ppermute | solution.py:295
  17.9 8.7 %collective-permute-start.4 = (bf16[192,512]{1,0:T(8,128)(2,1)S(1)}, bf16[192,512]{1,0:T(8,128)(2,1)S(1)}, u32[]{:S(2)}, u32[]{:S(2)}) collective-permute-start(bf16[192,512]{1,0:T(8,128)(2,1)S(1)} %up.11), channel_id=1, source_target_pairs={{0,16},{1,9},{2,18},{3,11},{4,20},{5,13},{6,22},{7,15},{8,24},{9,1... | collective-permute-start | bytes 589832 | tf_op jit(solution)/shard_map/ppermute | solution.py:285
  19.9 12.5 %collective-permute-start.3 = (bf16[192,512]{1,0:T(8,128)(2,1)S(1)}, bf16[192,512]{1,0:T(8,128)(2,1)S(1)}, u32[]{:S(2)}, u32[]{:S(2)}) collective-permute-start(bf16[192,512]{1,0:T(8,128)(2,1)S(1)} %up.10), channel_id=1, source_target_pairs={{0,8},{1,17},{2,10},{3,19},{4,12},{5,21},{6,14},{7,23},{8,0},{9,25... | collective-permute-start | bytes 589832 | tf_op jit(solution)/shard_map/ppermute | solution.py:285
  21.4 11.0 %collective-permute-start.5 = (bf16[192,512]{1,0:T(8,128)(2,1)S(1)}, bf16[192,512]{1,0:T(8,128)(2,1)S(1)}, u32[]{:S(2)}, u32[]{:S(2)}) collective-permute-start(bf16[192,512]{1,0:T(8,128)(2,1)S(1)} %get-tuple-element.45), channel_id=1, source_target_pairs={{0,24},{1,25},{2,26},{3,27},{4,28},{5,29},{6,30},{7,31},{8,16},{9,... | collective-permute-start | bytes 589832 | tf_op jit(solution)/shard_map/ppermute | solution.py:285
  23.0 12.2 %collective-permute-start.17 = (bf16[192,512]{1,0:T(8,128)(2,1)S(1)}, bf16[192,512]{1,0:T(8,128)(2,1)S(1)}, u32[]{:S(2)}, u32[]{:S(2)}) collective-permute-start(bf16[192,512]{1,0:T(8,128)(2,1)S(1)} %up.15), channel_id=1, source_target_pairs={{0,16},{1,9},{2,18},{3,11},{4,20},{5,13},{6,22},{7,15},{8,24},{9,1... | collective-permute-start | bytes 589832 | tf_op jit(solution)/shard_map/ppermute | solution.py:285
  25.0 13.9 %collective-permute-start.16 = (bf16[192,512]{1,0:T(8,128)(2,1)S(1)}, bf16[192,512]{1,0:T(8,128)(2,1)S(1)}, u32[]{:S(2)}, u32[]{:S(2)}) collective-permute-start(bf16[192,512]{1,0:T(8,128)(2,1)S(1)} %up.14), channel_id=1, source_target_pairs={{0,8},{1,17},{2,10},{3,19},{4,12},{5,21},{6,14},{7,23},{8,0},{9,25... | collective-permute-start | bytes 589832 | tf_op jit(solution)/shard_map/ppermute | solution.py:285
  26.6 13.6 %collective-permute-start.18 = (bf16[192,512]{1,0:T(8,128)(2,1)S(1)}, bf16[192,512]{1,0:T(8,128)(2,1)S(1)}, u32[]{:S(2)}, u32[]{:S(2)}) collective-permute-start(bf16[192,512]{1,0:T(8,128)(2,1)S(1)} %get-tuple-element.58), channel_id=1, source_target_pairs={{0,24},{1,25},{2,26},{3,27},{4,28},{5,29},{6,30},{7,31},{8,16},{9,... | collective-permute-start | bytes 589832 | tf_op jit(solution)/shard_map/ppermute | solution.py:285
  32.6 10.6 %collective-permute-start.6 = (bf16[192,256]{1,0:T(8,128)(2,1)S(1)}, bf16[192,256]{1,0:T(8,128)(2,1)S(1)}, u32[]{:S(2)}, u32[]{:S(2)}) collective-permute-start(bf16[192,256]{1,0:T(8,128)(2,1)S(1)} %hidden.2.refs_0_), channel_id=1, source_target_pairs={{0,8},{1,17},{2,10},{3,19},{4,12},{5,21},{6,14},{7,23},{8,0},{9,25... | collective-permute-start | bytes 294920 | tf_op jit(solution)/shard_map/ppermute | solution.py:285
  33.6 12.7 %collective-permute-start.7 = (bf16[192,256]{1,0:T(8,128)(2,1)S(1)}, bf16[192,256]{1,0:T(8,128)(2,1)S(1)}, u32[]{:S(2)}, u32[]{:S(2)}) collective-permute-start(bf16[192,256]{1,0:T(8,128)(2,1)S(1)} %hidden.2.refs_0_), channel_id=1, source_target_pairs={{0,16},{1,9},{2,18},{3,11},{4,20},{5,13},{6,22},{7,15},{8,24},{9,1... | collective-permute-start | bytes 294920 | tf_op jit(solution)/shard_map/ppermute | solution.py:285
  35.2 11.2 %collective-permute-start.8 = (bf16[192,256]{1,0:T(8,128)(2,1)S(1)}, bf16[192,256]{1,0:T(8,128)(2,1)S(1)}, u32[]{:S(2)}, u32[]{:S(2)}) collective-permute-start(bf16[192,256]{1,0:T(8,128)(2,1)S(1)} %hidden.2.refs_0_), channel_id=1, source_target_pairs={{0,24},{1,25},{2,26},{3,27},{4,28},{5,29},{6,30},{7,31},{8,16},{9,... | collective-permute-start | bytes 294920 | tf_op jit(solution)/shard_map/ppermute | solution.py:285
  40.3 7.2 %collective-permute-start.19 = (bf16[192,256]{1,0:T(8,128)(2,1)S(1)}, bf16[192,256]{1,0:T(8,128)(2,1)S(1)}, u32[]{:S(2)}, u32[]{:S(2)}) collective-permute-start(bf16[192,256]{1,0:T(8,128)(2,1)S(1)} %hidden.3.refs_0_), channel_id=1, source_target_pairs={{0,8},{1,17},{2,10},{3,19},{4,12},{5,21},{6,14},{7,23},{8,0},{9,25... | collective-permute-start | bytes 294920 | tf_op jit(solution)/shard_map/ppermute | solution.py:285
  42.1 5.5 %collective-permute-start.20 = (bf16[192,256]{1,0:T(8,128)(2,1)S(1)}, bf16[192,256]{1,0:T(8,128)(2,1)S(1)}, u32[]{:S(2)}, u32[]{:S(2)}) collective-permute-start(bf16[192,256]{1,0:T(8,128)(2,1)S(1)} %hidden.3.refs_0_), channel_id=1, source_target_pairs={{0,16},{1,9},{2,18},{3,11},{4,20},{5,13},{6,22},{7,15},{8,24},{9,1... | collective-permute-start | bytes 294920 | tf_op jit(solution)/shard_map/ppermute | solution.py:285
  43.2 5.5 %collective-permute-start.21 = (bf16[192,256]{1,0:T(8,128)(2,1)S(1)}, bf16[192,256]{1,0:T(8,128)(2,1)S(1)}, u32[]{:S(2)}, u32[]{:S(2)}) collective-permute-start(bf16[192,256]{1,0:T(8,128)(2,1)S(1)} %hidden.3.refs_0_), channel_id=1, source_target_pairs={{0,24},{1,25},{2,26},{3,27},{4,28},{5,29},{6,30},{7,31},{8,16},{9,... | collective-permute-start | bytes 294920 | tf_op jit(solution)/shard_map/ppermute | solution.py:285
  47.1 6.1 %collective-permute-start.10 = (bf16[48,896]{1,0:T(8,128)(2,1)S(1)}, bf16[48,896]{1,0:T(8,128)(2,1)S(1)}, u32[]{:S(2)}, u32[]{:S(2)}) collective-permute-start(bf16[48,896]{1,0:T(8,128)(2,1)S(1)} %get-tuple-element.47), channel_id=1, source_target_pairs={{0,5},{1,4},{2,7},{3,6},{4,1},{5,0},{6,3},{7,2},{8,13},{9,12},{10,... | collective-permute-start | bytes 258056 | tf_op jit(solution)/shard_map/ppermute | solution.py:295
  47.2 8.7 %collective-permute-start.11 = (bf16[48,896]{1,0:T(8,128)(2,1)S(1)}, bf16[48,896]{1,0:T(8,128)(2,1)S(1)}, u32[]{:S(2)}, u32[]{:S(2)}) collective-permute-start(bf16[48,896]{1,0:T(8,128)(2,1)S(1)} %get-tuple-element.48), channel_id=1, source_target_pairs={{0,1},{1,0},{2,3},{3,2},{4,5},{5,4},{6,7},{7,6},{8,9},{9,8},{10,11... | collective-permute-start | bytes 258056 | tf_op jit(solution)/shard_map/ppermute | solution.py:295
  49.4 8.6 %collective-permute-start.22 = (bf16[48,896]{1,0:T(8,128)(2,1)S(1)}, bf16[48,896]{1,0:T(8,128)(2,1)S(1)}, u32[]{:S(2)}, u32[]{:S(2)}) collective-permute-start(bf16[48,896]{1,0:T(8,128)(2,1)S(1)} %get-tuple-element.59), channel_id=1, source_target_pairs={{0,2},{1,3},{2,0},{3,1},{4,6},{5,7},{6,4},{7,5},{8,10},{9,11},{10,... | collective-permute-start | bytes 258056 | tf_op jit(solution)/shard_map/ppermute | solution.py:295
  50.4 7.3 %collective-permute-start.9 = (bf16[48,896]{1,0:T(8,128)(2,1)S(1)}, bf16[48,896]{1,0:T(8,128)(2,1)S(1)}, u32[]{:S(2)}, u32[]{:S(2)}) collective-permute-start(bf16[48,896]{1,0:T(8,128)(2,1)S(1)} %get-tuple-element.46), channel_id=1, source_target_pairs={{0,4},{1,5},{2,6},{3,7},{4,0},{5,1},{6,2},{7,3},{8,12},{9,13},{10,... | collective-permute-start | bytes 258056 | tf_op jit(solution)/shard_map/ppermute | solution.py:295
  52.0 6.5 %collective-permute-start.23 = (bf16[48,896]{1,0:T(8,128)(2,1)S(1)}, bf16[48,896]{1,0:T(8,128)(2,1)S(1)}, u32[]{:S(2)}, u32[]{:S(2)}) collective-permute-start(bf16[48,896]{1,0:T(8,128)(2,1)S(1)} %get-tuple-element.60), channel_id=1, source_target_pairs={{0,3},{1,2},{2,1},{3,0},{4,7},{5,6},{6,5},{7,4},{8,11},{9,10},{10,... | collective-permute-start | bytes 258056 | tf_op jit(solution)/shard_map/ppermute | solution.py:295
  53.2 7.5 %collective-permute-start.24 = (bf16[48,896]{1,0:T(8,128)(2,1)S(1)}, bf16[48,896]{1,0:T(8,128)(2,1)S(1)}, u32[]{:S(2)}, u32[]{:S(2)}) collective-permute-start(bf16[48,896]{1,0:T(8,128)(2,1)S(1)} %get-tuple-element.61), channel_id=1, source_target_pairs={{0,6},{1,7},{2,4},{3,5},{4,2},{5,3},{6,0},{7,1},{8,14},{9,15},{10,... | collective-permute-start | bytes 258056 | tf_op jit(solution)/shard_map/ppermute | solution.py:295
  55.9 6.6 %collective-permute-start.25 = (bf16[48,896]{1,0:T(8,128)(2,1)S(1)}, bf16[48,896]{1,0:T(8,128)(2,1)S(1)}, u32[]{:S(2)}, u32[]{:S(2)}) collective-permute-start(bf16[48,896]{1,0:T(8,128)(2,1)S(1)} %get-tuple-element.62), channel_id=1, source_target_pairs={{0,7},{1,6},{2,5},{3,4},{4,3},{5,2},{6,1},{7,0},{8,15},{9,14},{10,... | collective-permute-start | bytes 258056 | tf_op jit(solution)/shard_map/ppermute | solution.py:295
